TPU v7x, 32 devices: a whole 2x2x4 slice. The times are simulated.
32 devices in a mesh: groups: 2 (over y), chol: 4 (over z), walk: 2 (over x), orb: 2 (over core).
Axes of the slice: x: 2, y: 2, z: 4, core: 2. Of those that a mesh axis runs over, the one named last changes fastest.
Arguments:
- walkers: float32 [32, 2, 36864], P(('groups', 'walk'), None, ('chol', 'orb')), parts along dimension 0, may hold values from -6 to 6
- correlation_inverse: float32 [32, 2, 96, 96], P(('groups', 'walk')), parts along dimension 0, may hold values from -0.625 to 0.625
- half_vectors: bfloat16 [4096, 36864], P(('groups', 'walk'), ('chol', 'orb')), parts along dimension 0, may hold values from -0.01953125 to 0.01953125
- field_vectors: bfloat16 [4096, 384, 384], P(('groups', 'walk'), ('chol', 'orb')), parts along dimension 0, may hold values from -0.0048828125 to 0.0048828125
- samples: float32 [32, 2048], P('groups', 'walk'), parts along dimension 0, may hold values from -6 to 6
- source: int32 [32], P(('groups', 'walk')), parts along dimension 0, may hold values from 0 to 15
Outputs:
- walkers_next: float32 [32, 2, 36864], P(('groups', 'walk'), None, ('chol', 'orb')), parts along dimension 0
There are 2 independent parts, one for each index of `groups`. A program takes and returns all parts, laid end to end along the dimension named above; each array names one. Nothing has to cross between parts.
All inputs are finite; a program needn't handle non-finite values.
Results may differ from a plain program's by a relative error of at most 0.02.
Values may be sent and summed in bfloat16 or wider, within the bound.
No kernel may reach another device: no remote copies, remote signals or barrier semaphores. Data moves between devices by JAX's collectives and lax.ppermute only.
A program may use at most 128 MiB of HBM per device.

v0:
```python
import jax
import jax.numpy as jnp
from jax import lax
from jax.sharding import PartitionSpec as P

TERMS = 4
NS_STEPS = 2


def for_sending(shard):
    return jax.tree.map(lambda a: a.astype(jnp.bfloat16) if a.dtype == jnp.float32 else a, shard)


def complex_product(left_real, left_imag, right_real, right_imag, formula):
    first = jnp.einsum(formula, left_real, right_real, precision=lax.Precision.HIGHEST)
    second = jnp.einsum(formula, left_imag, right_imag, precision=lax.Precision.HIGHEST)
    third = jnp.einsum(formula, left_real, right_imag, precision=lax.Precision.HIGHEST)
    fourth = jnp.einsum(formula, left_imag, right_real, precision=lax.Precision.HIGHEST)
    return (first - second, third + fourth)


def normalizer(gram_real, gram_imag):
    electrons = gram_real.shape[-1]
    identity = jnp.eye(electrons, dtype=jnp.float32)
    scale_factor = jnp.trace(gram_real, axis1=1, axis2=2) / electrons
    iter_real = gram_real / scale_factor[:, None, None]
    iter_imag = gram_imag / scale_factor[:, None, None]
    root_real = jnp.broadcast_to(identity, gram_real.shape)
    root_imag = jnp.zeros_like(gram_real)
    for sweep_index in range(NS_STEPS):
        prod_real, prod_imag = complex_product(
            root_real, root_imag, iter_real, iter_imag, "wij,wjk->wik"
        )
        step_real = 1.5 * identity - 0.5 * prod_real
        step_imag = -0.5 * prod_imag
        iter_real, iter_imag = complex_product(
            iter_real, iter_imag, step_real, step_imag, "wij,wjk->wik"
        )
        root_real, root_imag = complex_product(
            step_real, step_imag, root_real, root_imag, "wij,wjk->wik"
        )
    inverse_root = lax.rsqrt(scale_factor)[:, None, None]
    return (root_real * inverse_root, root_imag * inverse_root)


def field_apply(field_block, values):
    next_real = jnp.einsum(
        "wab,wbn->wan", field_block[:, 0], values[:, 0], preferred_element_type=jnp.float32
    )
    next_real = next_real - jnp.einsum(
        "wab,wbn->wan", field_block[:, 1], values[:, 1], preferred_element_type=jnp.float32
    )
    next_imag = jnp.einsum(
        "wab,wbn->wan", field_block[:, 0], values[:, 1], preferred_element_type=jnp.float32
    )
    next_imag = next_imag + jnp.einsum(
        "wab,wbn->wan", field_block[:, 1], values[:, 0], preferred_element_type=jnp.float32
    )
    return jnp.stack([next_real, next_imag], 1)


def body(walkers, correlation_inverse, half_vectors, field_vectors, samples, source):
    local_walkers = walkers.shape[0]
    row_block = field_vectors.shape[1]
    orbitals = field_vectors.shape[2]
    electrons = correlation_inverse.shape[2]
    grid = walkers.reshape(local_walkers, 2, row_block, electrons)
    theta_real, theta_imag = complex_product(
        grid[:, 0], grid[:, 1], correlation_inverse[:, 0], correlation_inverse[:, 1], "wmk,wkn->wmn"
    )
    theta = (
        jnp.stack([theta_real, theta_imag], 1)
        .reshape(local_walkers, 2, row_block * electrons)
        .astype(jnp.bfloat16)
    )
    all_theta = lax.all_gather(theta, "walk", axis=0, tiled=True)
    bias_part = jnp.einsum(
        "wcj,gj->wcg", all_theta, half_vectors, preferred_element_type=jnp.float32
    )
    bias = lax.psum(bias_part, ("chol", "orb"))
    coefficient = jnp.stack([bias[:, 1], samples - bias[:, 0]], 1).astype(jnp.bfloat16)
    field_part = jnp.einsum(
        "wcg,gab->wcab", coefficient, field_vectors, preferred_element_type=jnp.float32
    )
    field = lax.psum_scatter(field_part, "walk", scatter_dimension=0, tiled=True).astype(
        jnp.bfloat16
    )
    devices_rows = lax.axis_size(("chol", "orb"))
    sharers = devices_rows // local_walkers
    col_width = electrons // sharers
    parted = grid.reshape(local_walkers, 2, row_block, sharers, col_width)
    parted = parted.transpose(0, 3, 1, 2, 4).reshape(devices_rows, 2, row_block, col_width)
    columns = lax.all_to_all(
        parted.astype(jnp.bfloat16), ("chol", "orb"), split_axis=0, concat_axis=2, tiled=True
    ).astype(parted.dtype)
    spread = jnp.broadcast_to(field[:, None], (local_walkers, sharers, 2, row_block, orbitals))
    spread = spread.reshape(devices_rows, 2, row_block, orbitals)
    whole_field = lax.all_to_all(spread, ("chol", "orb"), split_axis=0, concat_axis=2, tiled=True)
    current = columns
    col_summed = columns
    for order_index in range(1, TERMS + 1):
        current = field_apply(whole_field, current.astype(jnp.bfloat16)) / order_index
        col_summed = col_summed + current
    returned = lax.all_to_all(
        col_summed.astype(jnp.bfloat16), ("chol", "orb"), split_axis=2, concat_axis=0, tiled=True
    ).astype(col_summed.dtype)
    returned = returned.reshape(local_walkers, sharers, 2, row_block, col_width)
    summed = returned.transpose(0, 2, 3, 1, 4).reshape(local_walkers, 2, row_block, electrons)
    whole = lax.all_gather(summed.astype(jnp.bfloat16), ("chol", "orb"), axis=2, tiled=True).astype(
        summed.dtype
    )
    gram_real, gram_imag = complex_product(
        whole[:, 0], -whole[:, 1], whole[:, 0], whole[:, 1], "wmi,wmj->wij"
    )
    gram_real = gram_real / orbitals
    gram_imag = gram_imag / orbitals
    root_real, root_imag = normalizer(gram_real, gram_imag)
    norm_real, norm_imag = complex_product(
        summed[:, 0], summed[:, 1], root_real, root_imag, "wmk,wkn->wmn"
    )
    normalized = jnp.stack([norm_real, norm_imag], 1).reshape(
        local_walkers, 2, row_block * electrons
    )
    moved = lax.all_gather(for_sending(normalized), "walk", axis=0, tiled=True).astype(
        normalized.dtype
    )
    return jnp.take(moved, source, axis=0)


def solution(mesh):
    placed = (
        P(("groups", "walk"), None, ("chol", "orb")),
        P(("groups", "walk"), None, None, None),
        P(("groups", "walk"), ("chol", "orb")),
        P(("groups", "walk"), ("chol", "orb"), None),
        P("groups", "walk"),
        P(("groups", "walk")),
    )
    return jax.shard_map(
        body,
        mesh=mesh,
        in_specs=placed,
        out_specs=P(("groups", "walk"), None, ("chol", "orb")),
        check_vma=False,
    )
```

profile of v0, /device:TPU:0, one launch (start us, length us, event | category | flops | bytes accessed | tf_op | source)
XLA Modules:
  0.0 241.8 jit_solution(14504771620466679729)
XLA Ops:
  6.5 1.1 copy.45
  7.8 0.5 fusion.37
  8.3 0.5 fusion.41
  8.7 0.5 fusion.29
  9.4 0.5 fusion.28
  10.0 7.5 %all_gather.9 = bf16[16,2,4608]{2,0,1:T(8,128)(2,1)S(1)} all-gather(bf16[8,2,4608]{2,0,1:T(8,128)(2,1)S(1)} %pad_maximum_fusion.1), channel_id=1, replica_groups=mesh['groups'=2,'chol'=4,'walk'=2,'orb'=2] {'walk'}, dimensions={0}, use_global_device_ids=true | all-gather | bytes 442368 | tf_op jit(solution)/shard_map/all_gather | solution.py:76
  17.5 7.2 %fusion.3 = f32[16,2,1024]{2,0,1:T(8,128)} fusion(bf16[16,2,4608]{2,0,1:T(8,128)(2,1)S(1)} %all_gather.9, bf16[1024,4608]{1,0:T(8,128)(2,1)} %param.8), kind=kOutput, calls=%fused_computation.4 | convolution fusion | flops 301989888 | bytes 9863168 | tf_op jit(solution)/shard_map/wcj,gj->wcg/dot_general | solution.py:77
  25.0 56.4 %all-reduce.2.cloned.1.call-done = f32[16,2,1024]{2,0,1:T(8,128)} async-done(((f32[16,2,1024]{2,0,1:T(8,128)}), f32[16,2,1024]{2,0,1:T(8,128)}) %all-reduce.2.cloned.1.call-update) | async-done | bytes 131088 | tf_op jit(solution)/shard_map/psum | solution.py:80
  81.4 0.8 slice.232
  82.2 0.8 fusion.78
  83.1 29.4 %fusion = f32[16,2,48,384]{3,0,2,1:T(8,128)} fusion(bf16[1024,48,384]{2,1,0:T(8,128)(2,1)} %param.9, bf16[16,1,1024]{2,0,1:T(8,128)(2,1)S(1)} %fusion.78, bf16[16,1,1024]{2,0,1:T(8,128)(2,1)S(1)} %slice.232), kind=kOutput, calls=%fused_computation.1 | convolution fusion | flops 1208090624 | bytes 40173568 | tf_op jit(solution)/shard_map/wcg,gab->wcab/dot_general | solution.py:82
  112.5 0.7 copy.46
  113.2 3.4 %all-to-all-start = ((bf16[8,2,48,96]{3,2,1,0:T(8,128)(2,1)}), bf16[8,2,48,96]{3,2,1,0:T(8,128)(2,1)S(1)}, u32[]{:S(2)}, u32[]{:S(2)}) async-start(bf16[8,2,48,96]{3,2,1,0:T(8,128)(2,1)} %copy.46), calls=%async_computation | async-start | bytes 393216 | tf_op jit(solution)/shard_map/all_to_all | solution.py:93
  116.6 29.9 %reduce-scatter.2.cloned.1.call-done = f32[8,2,48,384]{3,0,2,1:T(8,128)} async-done(((f32[16,2,48,384]{3,0,2,1:T(8,128)}), f32[8,2,48,384]{3,0,2,1:T(8,128)}) %reduce-scatter.2.cloned.1.call-update) | async-done | bytes 1179664 | tf_op jit(solution)/shard_map/reduce_scatter | solution.py:85
  146.5 1.3 convert_element_type.82
  147.8 0.9 copy.52
  148.7 4.6 %all-to-all-start.1 = ((bf16[8,2,48,384]{3,2,1,0:T(8,128)(2,1)}), bf16[8,2,48,384]{3,2,1,0:T(8,128)(2,1)S(1)}, u32[]{:S(2)}, u32[]{:S(2)}) async-start(bf16[8,2,48,384]{3,2,1,0:T(8,128)(2,1)} %copy.52), calls=%async_computation.2 | async-start | bytes 1179648 | tf_op jit(solution)/shard_map/all_to_all | solution.py:98
  153.8 16.3 %all-to-all-done.1 = bf16[8,2,48,384]{3,2,1,0:T(8,128)(2,1)S(1)} async-done(((bf16[8,2,48,384]{3,2,1,0:T(8,128)(2,1)}), bf16[8,2,48,384]{3,2,1,0:T(8,128)(2,1)S(1)}, u32[]{:S(2)}, u32[]{:S(2)}) %all-to-all-start.1) | async-done | bytes 589856 | tf_op jit(solution)/shard_map/all_to_all | solution.py:98
  174.4 10.7 %all_to_all.54 = bf16[1,2,384,96]{3,1,0,2:T(2,128)(2,1)S(1)} all-to-all(bf16[1,2,384,96]{3,1,0,2:T(2,128)(2,1)S(1)} %copy.54), channel_id=1, replica_groups=mesh['groups'=2,'chol'=4,'walk'=2,'orb'=2] {'chol','orb'}, dimensions={2} | all-to-all | bytes 294912 | tf_op jit(solution)/shard_map/all_to_all | solution.py:104
  185.2 0.7 copy.56
  186.0 23.3 %all-gather.3.cloned.1.call-done = bf16[8,1,2,384,96]{4,0,2,1,3:T(8,128)(2,1)} async-done(((bf16[8,1,2,48,96]{4,0,2,1,3:T(8,128)(2,1)}), bf16[8,1,2,384,96]{4,0,2,1,3:T(8,128)(2,1)}) %all-gather.3.cloned.1.call-update) | async-done | bytes 1179664 | tf_op jit(solution)/shard_map/all_gather | solution.py:109
  209.3 2.1 copy.57
  211.4 0.8 fusion.18
  212.2 0.8 fusion.16
  213.1 0.4 select_reduce_fusion
  213.9 0.5 fusion.62
  214.5 0.5 fusion.58
  214.9 0.5 fusion.15
  215.4 0.5 fusion.60
  215.9 0.6 fusion.88
  216.5 0.5 fusion.52
  217.0 0.5 fusion.13
  217.5 0.6 fusion.87
  218.1 0.5 convolution_subtract_fusion.4
  218.6 0.5 convolution_subtract_fusion.3
  219.1 0.5 convolution_add_fusion.4
  219.6 0.5 convolution_add_fusion.3
  220.2 0.5 fusion.89
  220.7 0.5 fusion.91
  221.2 0.5 fusion.12
  221.8 0.5 fusion.92
  222.3 0.5 fusion.90
  222.9 0.5 fusion.10
  223.4 0.5 fusion.8
  223.9 0.8 fusion.9
  226.7 6.6 %all_gather.11 = bf16[16,2,4608]{2,1,0:T(2,128)(2,1)S(1)} all-gather(bf16[8,2,4608]{2,1,0:T(2,128)(2,1)S(1)} %pad_maximum_fusion.2), channel_id=1, replica_groups=mesh['groups'=2,'chol'=4,'walk'=2,'orb'=2] {'walk'}, dimensions={0}, use_global_device_ids=true | all-gather | bytes 442368 | tf_op jit(solution)/shard_map/all_gather | solution.py:124
  233.5 0.9 gather_fusion
  234.4 0.9 broadcast_select_fusion
  (59 shorter events, 8.0 us)
Async XLA Ops:
  6.5 1.3 copy-start
  6.5 74.9 %all-reduce.2.cloned.1.call-start = ((), (), s32[]{:S(2)}) async-start(), calls=%async_computation.4 | async-start | bytes 262144 | tf_op jit(solution)/shard_map/psum | solution.py:80
  17.5 64.7 %copy-start.1 = (f32[16,1024]{1,0:T(8,128)S(1)}, f32[16,1024]{1,0:T(8,128)}, u32[]{:S(2)}) copy-start(f32[16,1024]{1,0:T(8,128)} %param.10) | copy-start | bytes 196612
  24.7 121.7 %reduce-scatter.2.cloned.1.call-start = ((), (), s32[]{:S(2)}) async-start(), calls=%async_computation.5 | async-start | bytes 3538944 | tf_op jit(solution)/shard_map/reduce_scatter | solution.py:85
  113.2 35.5 %all-to-all-start = ((bf16[8,2,48,96]{3,2,1,0:T(8,128)(2,1)}), bf16[8,2,48,96]{3,2,1,0:T(8,128)(2,1)S(1)}, u32[]{:S(2)}, u32[]{:S(2)}) async-start(bf16[8,2,48,96]{3,2,1,0:T(8,128)(2,1)} %copy.46), calls=%async_computation | async-start | bytes 393216 | tf_op jit(solution)/shard_map/all_to_all | solution.py:93
  148.7 21.4 %all-to-all-start.1 = ((bf16[8,2,48,384]{3,2,1,0:T(8,128)(2,1)}), bf16[8,2,48,384]{3,2,1,0:T(8,128)(2,1)S(1)}, u32[]{:S(2)}, u32[]{:S(2)}) async-start(bf16[8,2,48,384]{3,2,1,0:T(8,128)(2,1)} %copy.52), calls=%async_computation.2 | async-start | bytes 1179648 | tf_op jit(solution)/shard_map/all_to_all | solution.py:98
  153.3 56.0 %all-gather.3.cloned.1.call-start = ((), (), s32[]{:S(2)}) async-start(), calls=%async_computation.6 | async-start | bytes 1769472 | tf_op jit(solution)/shard_map/all_gather | solution.py:109
  174.2 11.7 %copy-start.2 = (s32[8]{0:T(128)S(1)}, s32[8]{0:T(128)}, u32[]{:S(2)}) copy-start(s32[8]{0:T(128)} %param.11) | copy-start | bytes 100
Sparse Core Ops, SparseCore 0:
  24.8 56.5 all-reduce.1
  112.6 33.8 reduce-scatter.1
  186.0 23.2 all-gather.2
where the time goes:
time: 242 us
  waiting for transfers between devices  126 us (52%)
  matrix products  56.8 us (23%)
  blocking collectives  24.8 us (10%)
  between operations  13.6 us (6%)
  starting transfers between devices  8.5 us (4%)
  local copies, waits for them, and re-layouts  8.36 us (3%)
  other arithmetic  3.9 us (2%)
    psum x1, waiting for transfers between devices, body(): bias = lax.psum(bias_part, ('chol', 'orb'))  56.4 us
    reduce_scatter x1, waiting for transfers between devices, body(): lax.psum_scatter(field_part, 'walk', scatter_dimension=0, tiled=True)  29.9 us
    dot_general x1, matrix products, body(): jnp.einsum('wcg,gab->wcab', coefficient, field_vectors, preferred_element...  29.4 us
    all_gather x1, waiting for transfers between devices, body(): lax.all_gather(summed.astype(jnp.bfloat16), ('chol', 'orb'), axis=2, tile...  23.3 us
    all_to_all x1, waiting for transfers between devices, body(): lax.all_to_all(spread, ('chol', 'orb'), split_axis=0, concat_axis=2, tile...  16.3 us
    all_to_all x1, blocking collectives, body(): lax.all_to_all(col_summed.astype(jnp.bfloat16), ('chol', 'orb'), split_ax...  10.7 us
    all_gather x1, blocking collectives, body(): all_theta = lax.all_gather(theta, 'walk', axis=0, tiled=True)  7.47 us
    dot_general x1, matrix products, body(): jnp.einsum('wcj,gj->wcg', all_theta, half_vectors, preferred_element_type...  7.2 us
  transfers between devices with their start and end apart: 5, of which 4 were waited for; matrix products, arithmetic and copies ran while one was open for 1% of the time, Pallas kernels for 0%

commit v1 on v0

v1 whole, which is shorter than its diff:
```python
import jax
import jax.numpy as jnp
from jax import lax
from jax.sharding import PartitionSpec as P

TERMS = 4
NS_STEPS = 2
ROWS = ("chol", "orb")
HALF = jnp.bfloat16


def complex_product(left_real, left_imag, right_real, right_imag, formula):
    first = jnp.einsum(formula, left_real, right_real, precision=lax.Precision.HIGHEST)
    second = jnp.einsum(formula, left_imag, right_imag, precision=lax.Precision.HIGHEST)
    third = jnp.einsum(formula, left_real, right_imag, precision=lax.Precision.HIGHEST)
    fourth = jnp.einsum(formula, left_imag, right_real, precision=lax.Precision.HIGHEST)
    return (first - second, third + fourth)


def normalizer(gram_real, gram_imag):
    electrons = gram_real.shape[-1]
    identity = jnp.eye(electrons, dtype=jnp.float32)
    scale_factor = jnp.trace(gram_real, axis1=1, axis2=2) / electrons
    iter_real = gram_real / scale_factor[:, None, None]
    iter_imag = gram_imag / scale_factor[:, None, None]
    root_real = jnp.broadcast_to(identity, gram_real.shape)
    root_imag = jnp.zeros_like(gram_real)
    for sweep_index in range(NS_STEPS):
        if sweep_index == 0:
            prod_real, prod_imag = iter_real, iter_imag
        else:
            prod_real, prod_imag = complex_product(
                root_real, root_imag, iter_real, iter_imag, "wij,wjk->wik"
            )
        step_real = 1.5 * identity - 0.5 * prod_real
        step_imag = -0.5 * prod_imag
        if sweep_index + 1 < NS_STEPS:
            iter_real, iter_imag = complex_product(
                iter_real, iter_imag, step_real, step_imag, "wij,wjk->wik"
            )
        if sweep_index == 0:
            root_real, root_imag = step_real, step_imag
        else:
            root_real, root_imag = complex_product(
                step_real, step_imag, root_real, root_imag, "wij,wjk->wik"
            )
    inverse_root = lax.rsqrt(scale_factor)[:, None, None]
    return (root_real * inverse_root, root_imag * inverse_root)


def field_apply(field_block, values):
    next_real = jnp.einsum(
        "wab,wbn->wan", field_block[:, 0], values[:, 0], preferred_element_type=jnp.float32
    )
    next_real = next_real - jnp.einsum(
        "wab,wbn->wan", field_block[:, 1], values[:, 1], preferred_element_type=jnp.float32
    )
    next_imag = jnp.einsum(
        "wab,wbn->wan", field_block[:, 0], values[:, 1], preferred_element_type=jnp.float32
    )
    next_imag = next_imag + jnp.einsum(
        "wab,wbn->wan", field_block[:, 1], values[:, 0], preferred_element_type=jnp.float32
    )
    return jnp.stack([next_real, next_imag], 1)


def shift(value, axis, step):
    size = lax.axis_size(axis)
    return lax.ppermute(value, axis, [(i, (i + step) % size) for i in range(size)])


def gather_relative(value, axis):
    size = lax.axis_size(axis)
    return jnp.concatenate([value] + [shift(value, axis, -s) for s in range(1, size)], 0)


def scatter_sum(value, axis, dim):
    size = lax.axis_size(axis)
    here = lax.axis_index(axis)
    width = value.shape[dim] // size
    total = lax.dynamic_slice_in_dim(value, here * width, width, dim)
    for s in range(1, size):
        block = lax.dynamic_slice_in_dim(value, ((here + s) % size) * width, width, dim)
        total = total + shift(block, axis, s)
    return total


def gather_ordered(value, axis, dim):
    size = lax.axis_size(axis)
    here = lax.axis_index(axis)
    width = value.shape[dim]
    shape = list(value.shape)
    shape[dim] = width * size
    whole = jnp.zeros(shape, value.dtype)
    for s in range(size):
        block = value if s == 0 else shift(value, axis, s)
        whole = lax.dynamic_update_slice_in_dim(whole, block, ((here - s) % size) * width, dim)
    return whole


def exchange_sum(value, axis):
    size = lax.axis_size(axis)
    if size & (size - 1):
        return sum([shift(value, axis, s) for s in range(1, size)], value)
    step = 1
    while step < size:
        value = value + lax.ppermute(value, axis, [(i, i ^ step) for i in range(size)])
        step *= 2
    return value


def body(walkers, correlation_inverse, half_vectors, field_vectors, samples, source):
    local_walkers = walkers.shape[0]
    row_block = field_vectors.shape[1]
    orbitals = field_vectors.shape[2]
    electrons = correlation_inverse.shape[2]
    planes = lax.axis_size("walk")
    population = local_walkers * planes
    plane = lax.axis_index("walk")
    devices_rows = lax.axis_size(ROWS)
    sharers = devices_rows // local_walkers
    col_width = electrons // sharers

    wanted = gather_relative(source, "walk")
    wanted = (wanted - plane * local_walkers) % population
    grid = walkers.reshape(local_walkers, 2, row_block, electrons)
    all_grid = gather_relative(grid.astype(HALF), "walk")
    picked = jnp.take(all_grid, wanted[:local_walkers], axis=0)
    theta_real, theta_imag = complex_product(
        grid[:, 0], grid[:, 1], correlation_inverse[:, 0], correlation_inverse[:, 1], "wmk,wkn->wmn"
    )
    theta = (
        jnp.stack([theta_real, theta_imag], 1)
        .reshape(local_walkers, 2, row_block * electrons)
        .astype(HALF)
    )
    all_theta = gather_relative(theta, "walk")
    bias = jnp.einsum("wcj,gj->wcg", all_theta, half_vectors, preferred_element_type=jnp.float32)
    bias = exchange_sum(scatter_sum(bias, "orb", 2), "chol")
    width = bias.shape[2]
    drawn = lax.dynamic_slice_in_dim(samples, lax.axis_index("orb") * width, width, 1)
    drawn = jnp.roll(drawn, -plane * local_walkers, axis=0)
    coefficient = jnp.stack([bias[:, 1], drawn - bias[:, 0]], 1).astype(HALF)
    coefficient = jnp.take(coefficient, wanted, axis=0)
    coefficient = gather_ordered(coefficient, "orb", 2)

    def to_owners(value):
        value = jnp.broadcast_to(value[:, None], (local_walkers, sharers) + value.shape[1:])
        value = value.reshape((devices_rows,) + value.shape[2:])
        return lax.all_to_all(value, ROWS, split_axis=0, concat_axis=0, tiled=True)

    columns = to_owners(picked).transpose(1, 0, 2, 3)
    columns = columns.reshape(1, 2, orbitals, electrons).astype(jnp.float32)

    parts = max(1, row_block // 16) if row_block % 16 == 0 else 1
    rows = row_block // parts
    pieces = []
    for part in range(parts):
        vectors = lax.slice_in_dim(field_vectors, part * rows, (part + 1) * rows, axis=1)
        field = jnp.einsum(
            "wcg,gab->wcab", coefficient, vectors, preferred_element_type=jnp.float32
        )
        total = field[:local_walkers]
        for s in range(1, planes):
            sent = field[s * local_walkers : (s + 1) * local_walkers].astype(HALF)
            total = total + shift(sent, "walk", s)
        pieces.append(to_owners(total.astype(HALF)))
    whole_field = jnp.stack(pieces, 1)
    whole_field = whole_field.transpose(2, 0, 1, 3, 4).reshape(1, 2, orbitals, orbitals)

    current = columns
    summed = columns
    for order_index in range(1, TERMS + 1):
        current = field_apply(whole_field, current.astype(HALF)) / order_index
        summed = summed + current
    gram_real, gram_imag = complex_product(
        summed[:, 0], -summed[:, 1], summed[:, 0], summed[:, 1], "wmi,wmj->wij"
    )
    root_real, root_imag = normalizer(gram_real / orbitals, gram_imag / orbitals)
    norm_real, norm_imag = complex_product(
        summed[:, 0], summed[:, 1], root_real, root_imag, "wmk,wkn->wmn"
    )
    normalized = jnp.concatenate([norm_real, norm_imag], 0).astype(HALF)
    share = lax.axis_index(ROWS) % sharers
    normalized = lax.dynamic_slice_in_dim(normalized, share * col_width, col_width, 2)
    normalized = normalized.reshape(2, devices_rows, row_block, col_width).transpose(1, 0, 2, 3)
    returned = lax.all_to_all(normalized, ROWS, split_axis=0, concat_axis=0, tiled=True)
    returned = returned.reshape(local_walkers, sharers, 2, row_block, col_width)
    returned = returned.transpose(0, 2, 3, 1, 4)
    return returned.reshape(local_walkers, 2, row_block * electrons).astype(jnp.float32)


def solution(mesh):
    placed = (
        P(("groups", "walk"), None, ("chol", "orb")),
        P(("groups", "walk"), None, None, None),
        P(("groups", "walk"), ("chol", "orb")),
        P(("groups", "walk"), ("chol", "orb"), None),
        P("groups", "walk"),
        P(("groups", "walk")),
    )
    return jax.shard_map(
        body,
        mesh=mesh,
        in_specs=placed,
        out_specs=P(("groups", "walk"), None, ("chol", "orb")),
        check_vma=False,
    )
```

time: 242 us -> 140 us (0.58)
  waiting for transfers between devices: 126 us -> 19.7 us
  local copies, waits for them, and re-layouts: 8.36 us -> 31.9 us
  starting transfers between devices: 8.5 us -> 29.6 us
  blocking collectives: 24.8 us -> 10.7 us
  between operations: 13.6 us -> 1.15 us
  matrix products: 56.8 us -> 44.7 us
    psum x1 -> x0, waiting for transfers between devices: 56.4 us -> none  [body(): bias = lax.psum(bias_part, ('chol', 'orb'))]
    reduce_scatter x1 -> x0, waiting for transfers between devices: 29.9 us -> none  [body(): lax.psum_scatter(field_part, 'walk', scatter_dimension=0, tiled=True)]
    slice x1 -> x5, local copies, waits for them, and re-layouts: 0.84 us -> 25.4 us  [the longest x1 25.3 us: body(): lax.slice_in_dim(field_vectors, part * rows, (part + 1) * rows, axis=1)]
    all_gather x1 -> x0, waiting for transfers between devices: 23.3 us -> none  [body(): lax.all_gather(summed.astype(jnp.bfloat16), ('chol', 'orb'), axis=2, tile...]
    all_gather x2 -> x0, blocking collectives: 14.1 us -> none  [the longest x1 7.47 us: body(): all_theta = lax.all_gather(theta, 'walk', axis=0, tiled=True)]
    ppermute x0 -> x10, starting transfers between devices: none -> 12.7 us  [the longest x8 8.4 us: shift(): lax.ppermute(value, axis, [(i, (i + step) % size) for i in range(size)])]
    all_to_all x2 -> x4, starting transfers between devices: 8.02 us -> 16.9 us  [to_owners(): return lax.all_to_all(value, ROWS, split_axis=0, concat_axis=0, tiled=True)]
    dot_general x1 -> x3, matrix products: 29.4 us -> 23 us  [body(): jnp.einsum('wcg,gab->wcab', coefficient, vectors, preferred_element_type=...]
  transfers between devices with their start and end apart: 5 -> 14, of which waited for: 4 -> 6; matrix products, arithmetic and copies ran while one was open for 1% -> 47% of each run, Pallas kernels for 0% -> 0%
where the time goes in v1:
time: 140 us; the launch traced here: 139 us
  matrix products  44.7 us (32%)
  local copies, waits for them, and re-layouts  31.9 us (23%)
  starting transfers between devices  29.6 us (21%)
  waiting for transfers between devices  19.7 us (14%)
  blocking collectives  10.7 us (8%)
  other arithmetic  1.64 us (1%)
    slice x1, local copies, waits for them, and re-layouts, body(): lax.slice_in_dim(field_vectors, part * rows, (part + 1) * rows, axis=1)  25.3 us
    dot_general x3, matrix products, body(): jnp.einsum('wcg,gab->wcab', coefficient, vectors, preferred_element_type=...  23 us
    all_to_all x4, starting transfers between devices, to_owners(): return lax.all_to_all(value, ROWS, split_axis=0, concat_axis=0, tiled=True)  16.9 us
    all_to_all x4, waiting for transfers between devices, to_owners(): return lax.all_to_all(value, ROWS, split_axis=0, concat_axis=0, tiled=True)  14.6 us
    all_to_all x1, blocking collectives, body(): lax.all_to_all(normalized, ROWS, split_axis=0, concat_axis=0, tiled=True)  10.7 us
    ppermute x8, starting transfers between devices, shift(): lax.ppermute(value, axis, [(i, (i + step) % size) for i in range(size)])  8.4 us
    dot_general x1, matrix products, body(): jnp.einsum('wcj,gj->wcg', all_theta, half_vectors, preferred_element_type...  6.5 us
    ppermute x2, starting transfers between devices, exchange_sum(): lax.ppermute(value, axis, [(i, i ^ step) for i in range(size)])  4.3 us
  transfers between devices with their start and end apart: 14, of which 6 were waited for; matrix products, arithmetic and copies ran while one was open for 47% of the time, Pallas kernels for 0%

profile of v1, /device:TPU:0, one launch (start us, length us, event | category | flops | bytes accessed | tf_op | source)
XLA Modules:
  0.0 139.4 jit_solution(5051828887542980376)
XLA Ops:
  0.0 1.1 copy.29
  1.2 3.0 %collective-permute-start.1 = (bf16[8,2,48,96]{3,2,0,1:T(8,128)(2,1)S(1)}, bf16[8,2,48,96]{3,2,0,1:T(8,128)(2,1)S(1)}, u32[]{:S(2)}, u32[]{:S(2)}) collective-permute-start(bf16[8,2,48,96]{3,2,0,1:T(8,128)(2,1)S(1)} %convert_element_type.80), channel_id=1, source_target_pairs={{0,2},{2,0},{1,3},{3,1},{4,6},{6,4},{5,7},{7,5},{8,10},{10,8},{9,1... | collective-permute-start | bytes 442376 | tf_op jit(solution)/shard_map/ppermute | solution.py:69
  4.4 1.5 %fusion.32 = f32[8,48,96]{2,1,0:T(8,128)S(1)} fusion(f32[8,2,96,96]{3,2,1,0:T(8,128)} %param.7, f32[8,2,48,96]{3,2,0,1:T(8,128)S(1)} %reshape.615), kind=kOutput, calls=%fused_computation.65 | convolution fusion | flops 42467328 | bytes 737280 | tf_op jit(solution)/shard_map/wmk,wkn->wmn/dot_general | solution.py:13
  5.8 1.5 %fusion.28 = f32[8,48,96]{2,1,0:T(8,128)S(1)} fusion(f32[8,2,96,96]{3,2,1,0:T(8,128)} %param.7, f32[8,2,48,96]{3,2,0,1:T(8,128)S(1)} %reshape.615), kind=kOutput, calls=%fused_computation.61 | convolution fusion | flops 42467328 | bytes 737280 | tf_op jit(solution)/shard_map/wmk,wkn->wmn/dot_general | solution.py:15
  7.3 1.5 %fusion.13 = bf16[8,48,96]{2,1,0:T(8,128)(2,1)S(1)} fusion(f32[8,48,96]{2,1,0:T(8,128)S(1)} %fusion.32, f32[8,2,96,96]{3,2,1,0:T(8,128)} %param.7, f32[8,2,48,96]{3,2,0,1:T(8,128)S(1)} %reshape.615), kind=kOutput, calls=%fused_computation.30 | convolution fusion | flops 42541056 | bytes 860160 | tf_op jit(solution)/shard_map/wmk,wkn->wmn/dot_general | solution.py:14
  8.9 1.5 %fusion.14 = bf16[8,48,96]{2,1,0:T(8,128)(2,1)S(1)} fusion(f32[8,48,96]{2,1,0:T(8,128)S(1)} %fusion.28, f32[8,2,96,96]{3,2,1,0:T(8,128)} %param.7, f32[8,2,48,96]{3,2,0,1:T(8,128)S(1)} %reshape.615), kind=kOutput, calls=%fused_computation.31 | convolution fusion | flops 42541056 | bytes 860160 | tf_op jit(solution)/shard_map/wmk,wkn->wmn/dot_general | solution.py:16
  10.6 2.0 %collective-permute-start.2 = (bf16[8,2,4608]{2,0,1:T(8,128)(2,1)S(1)}, bf16[8,2,4608]{2,0,1:T(8,128)(2,1)S(1)}, u32[]{:S(2)}, u32[]{:S(2)}) collective-permute-start(bf16[8,2,4608]{2,0,1:T(8,128)(2,1)S(1)} %constant_dynamic-update-slice_fusion), channel_id=1, source_target_pairs={{0,2},{2,0},{1,3},{3,1},{4,6},{6,4},{5,7},{7,5},{8,10},{10,8},{9,1... | collective-permute-start | bytes 442376 | tf_op jit(solution)/shard_map/ppermute | solution.py:69
  12.6 25.3 %fusion.123 = (bf16[1024,16,384]{2,1,0:T(8,128)(2,1)}, bf16[1024,16,384]{2,1,0:T(8,128)(2,1)}, bf16[1024,16,384]{2,1,0:T(8,128)(2,1)}) fusion(bf16[1024,48,384]{2,1,0:T(8,128)(2,1)} %param.9), kind=kLoop, calls=%fused_computation.210 | loop fusion | bytes 75497472 | tf_op jit(solution)/shard_map/slice | solution.py:159
  38.2 6.5 %fusion.3 = f32[16,2,1024]{2,0,1:T(8,128)S(1)} fusion(bf16[1024,4608]{1,0:T(8,128)(2,1)} %param.8, bf16[8,2,4608]{2,0,1:T(8,128)(2,1)S(1)} %collective-permute-done.2, bf16[8,2,4608]{2,0,1:T(8,128)(2,1)S(1)} %constant_dynamic-update-slice_fusion), kind=kOutput, calls=%fused_computation.8 | convolution fusion | flops 302579712 | bytes 9863168 | tf_op jit(solution)/shard_map/wcj,gj->wcg/dot_general | solution.py:138
  44.8 1.2 collective-permute-done.3
  46.0 1.6 %collective-permute-start.4 = (f32[16,2,512]{2,0,1:T(8,128)S(1)}, f32[16,2,512]{2,0,1:T(8,128)S(1)}, u32[]{:S(2)}, u32[]{:S(2)}) collective-permute-start(f32[16,2,512]{2,0,1:T(8,128)S(1)} %dynamic-slice_add_fusion), channel_id=1, source_target_pairs={{0,4},{4,0},{8,12},{12,8},{1,5},{5,1},{9,13},{13,9},{2,6},{6,2},{1... | collective-permute-start | bytes 196616 | tf_op jit(solution)/shard_map/ppermute | solution.py:107
  47.8 0.6 gather_fusion
  48.4 2.0 %collective-permute-done.4 = f32[16,2,512]{2,0,1:T(8,128)S(1)} collective-permute-done((f32[16,2,512]{2,0,1:T(8,128)S(1)}, f32[16,2,512]{2,0,1:T(8,128)S(1)}, u32[]{:S(2)}, u32[]{:S(2)}) %collective-permute-start.4) | collective-permute-done | bytes 65568 | tf_op jit(solution)/shard_map/ppermute | solution.py:107
  50.4 2.7 %collective-permute-start.5 = (f32[16,2,512]{2,0,1:T(8,128)S(1)}, f32[16,2,512]{2,0,1:T(8,128)S(1)}, u32[]{:S(2)}, u32[]{:S(2)}) collective-permute-start(f32[16,2,512]{2,0,1:T(8,128)S(1)} %add.186), channel_id=1, source_target_pairs={{0,8},{4,12},{8,0},{12,4},{1,9},{5,13},{9,1},{13,5},{2,10},{6,14},... | collective-permute-start | bytes 196616 | tf_op jit(solution)/shard_map/ppermute | solution.py:107
  53.0 0.8 broadcast_select_fusion
  53.8 3.4 %all-to-all-start = ((bf16[8,2,48,96]{3,2,1,0:T(8,128)(2,1)}), bf16[8,2,48,96]{3,2,1,0:T(8,128)(2,1)S(1)}, u32[]{:S(2)}, u32[]{:S(2)}) async-start(bf16[8,2,48,96]{3,2,1,0:T(8,128)(2,1)} %broadcast_select_fusion), calls=%async_computation | async-start | bytes 393216 | tf_op jit(solution)/shard_map/all_to_all | solution.py:150
  57.3 0.6 gather_fusion.1
  58.1 0.5 collective-permute-start.6
  58.5 0.8 collective-permute-done.6
  59.4 7.7 %fusion = f32[16,2,16,384]{3,0,2,1:T(8,128)S(1)} fusion(bf16[1024,16,384]{2,1,0:T(8,128)(2,1)} %get-tuple-element.11, bf16[16,2,1024]{2,0,1:T(8,128)(2,1)S(1)} %copy_dynamic-update-slice_fusion), kind=kOutput, calls=%fused_computation.3 | convolution fusion | flops 402653184 | bytes 13434880 | tf_op jit(solution)/shard_map/wcg,gab->wcab/dot_general | solution.py:160
  67.1 0.6 collective-permute-start.9
  67.7 7.6 %fusion.1 = f32[16,2,16,384]{3,0,2,1:T(8,128)S(1)} fusion(bf16[1024,16,384]{2,1,0:T(8,128)(2,1)} %get-tuple-element.10, bf16[16,2,1024]{2,0,1:T(8,128)(2,1)S(1)} %copy_dynamic-update-slice_fusion), kind=kOutput, calls=%fused_computation.5 | convolution fusion | flops 402653184 | bytes 13434880 | tf_op jit(solution)/shard_map/wcg,gab->wcab/dot_general | solution.py:160
  75.4 1.6 %collective-permute-start.8 = (bf16[8,2,16,384]{3,0,2,1:T(8,128)(2,1)S(1)}, bf16[8,2,16,384]{3,0,2,1:T(8,128)(2,1)S(1)}, u32[]{:S(2)}, u32[]{:S(2)}) collective-permute-start(bf16[8,2,16,384]{3,0,2,1:T(8,128)(2,1)S(1)} %slice.280), channel_id=1, source_target_pairs={{0,2},{2,0},{1,3},{3,1},{4,6},{6,4},{5,7},{7,5},{8,10},{10,8},{9,1... | collective-permute-start | bytes 589832 | tf_op jit(solution)/shard_map/ppermute | solution.py:69
  77.0 0.7 copy.44
  77.7 5.0 %all-to-all-start.3 = ((bf16[8,2,16,384]{3,2,1,0:T(8,128)(2,1)}), bf16[8,2,16,384]{3,2,1,0:T(8,128)(2,1)S(1)}, u32[]{:S(2)}, u32[]{:S(2)}) async-start(bf16[8,2,16,384]{3,2,1,0:T(8,128)(2,1)} %copy.44), calls=%async_computation.3 | async-start | bytes 393216 | tf_op jit(solution)/shard_map/all_to_all | solution.py:150
  82.7 7.7 %fusion.2 = f32[16,2,16,384]{3,0,2,1:T(8,128)S(1)} fusion(bf16[1024,16,384]{2,1,0:T(8,128)(2,1)} %get-tuple-element.9, bf16[16,2,1024]{2,0,1:T(8,128)(2,1)S(1)} %copy_dynamic-update-slice_fusion), kind=kOutput, calls=%fused_computation.7 | convolution fusion | flops 402653184 | bytes 13434880 | tf_op jit(solution)/shard_map/wcg,gab->wcab/dot_general | solution.py:160
  90.4 0.6 collective-permute-start.7
  91.0 0.7 copy.41
  91.7 5.1 %all-to-all-start.2 = ((bf16[8,2,16,384]{3,2,1,0:T(8,128)(2,1)}), bf16[8,2,16,384]{3,2,1,0:T(8,128)(2,1)S(1)}, u32[]{:S(2)}, u32[]{:S(2)}) async-start(bf16[8,2,16,384]{3,2,1,0:T(8,128)(2,1)} %copy.41), calls=%async_computation.2 | async-start | bytes 393216 | tf_op jit(solution)/shard_map/all_to_all | solution.py:150
  96.8 0.9 collective-permute-done.7
  97.8 0.7 copy.38
  98.5 6.6 %all-to-all-done.2 = bf16[8,2,16,384]{3,2,1,0:T(8,128)(2,1)S(1)} async-done(((bf16[8,2,16,384]{3,2,1,0:T(8,128)(2,1)}), bf16[8,2,16,384]{3,2,1,0:T(8,128)(2,1)S(1)}, u32[]{:S(2)}, u32[]{:S(2)}) %all-to-all-start.2) | async-done | bytes 196640 | tf_op jit(solution)/shard_map/all_to_all | solution.py:150
  105.1 3.4 %all-to-all-start.1 = ((bf16[8,2,16,384]{3,2,1,0:T(8,128)(2,1)}), bf16[8,2,16,384]{3,2,1,0:T(8,128)(2,1)S(1)}, u32[]{:S(2)}, u32[]{:S(2)}) async-start(bf16[8,2,16,384]{3,2,1,0:T(8,128)(2,1)} %copy.38), calls=%async_computation.1 | async-start | bytes 393216 | tf_op jit(solution)/shard_map/all_to_all | solution.py:150
  108.8 8.0 %all-to-all-done.1 = bf16[8,2,16,384]{3,2,1,0:T(8,128)(2,1)S(1)} async-done(((bf16[8,2,16,384]{3,2,1,0:T(8,128)(2,1)}), bf16[8,2,16,384]{3,2,1,0:T(8,128)(2,1)S(1)}, u32[]{:S(2)}, u32[]{:S(2)}) %all-to-all-start.1) | async-done | bytes 196640 | tf_op jit(solution)/shard_map/all_to_all | solution.py:150
  116.9 0.3 fusion.63
  117.1 0.3 fusion.62
  117.4 0.3 fusion.11
  117.7 0.3 fusion.12
  121.0 0.3 fusion.56
  121.3 0.3 fusion.47
  121.6 0.9 select_reduce_fusion
  123.4 0.3 fusion.24
  125.7 0.3 fusion.54
  126.2 0.3 fusion.55
  126.5 0.3 fusion.16
  127.0 0.3 fusion.15
  127.6 10.7 %all_to_all.25 = bf16[8,2,48,96]{3,2,1,0:T(8,128)(2,1)S(1)} all-to-all(bf16[8,2,48,96]{3,2,1,0:T(8,128)(2,1)S(1)} %copy.48), channel_id=1, replica_groups=mesh['groups'=2,'chol'=4,'walk'=2,'orb'=2] {'chol','orb'}, dimensions={0} | all-to-all | bytes 294912 | tf_op jit(solution)/shard_map/all_to_all | solution.py:187
  138.3 1.1 reshape.630
  (83 shorter events, 7.3 us)
Async XLA Ops:
  0.0 37.9 %copy-start = (f32[16,1024]{1,0:T(8,128)S(1)}, f32[16,1024]{1,0:T(8,128)}, u32[]{:S(2)}) copy-start(f32[16,1024]{1,0:T(8,128)} %param.10) | copy-start | bytes 196612
  1.2 46.4 %collective-permute-start.1 = (bf16[8,2,48,96]{3,2,0,1:T(8,128)(2,1)S(1)}, bf16[8,2,48,96]{3,2,0,1:T(8,128)(2,1)S(1)}, u32[]{:S(2)}, u32[]{:S(2)}) collective-permute-start(bf16[8,2,48,96]{3,2,0,1:T(8,128)(2,1)S(1)} %convert_element_type.80), channel_id=1, source_target_pairs={{0,2},{2,0},{1,3},{3,1},{4,6},{6,4},{5,7},{7,5},{8,10},{10,8},{9,1... | collective-permute-start | bytes 442376 | tf_op jit(solution)/shard_map/ppermute | solution.py:69
  4.3 33.7 %collective-permute-start = (s32[8]{0:T(128)}, s32[8]{0:T(128)S(1)}, u32[]{:S(2)}, u32[]{:S(2)}) collective-permute-start(s32[8]{0:T(128)} %param.11), channel_id=1, source_target_pairs={{0,2},{2,0},{1,3},{3,1},{4,6},{6,4},{5,7},{7,5},{8,10},{10,8},{9,1... | collective-permute-start | bytes 104 | tf_op jit(solution)/shard_map/ppermute | solution.py:69
  10.6 27.6 %collective-permute-start.2 = (bf16[8,2,4608]{2,0,1:T(8,128)(2,1)S(1)}, bf16[8,2,4608]{2,0,1:T(8,128)(2,1)S(1)}, u32[]{:S(2)}, u32[]{:S(2)}) collective-permute-start(bf16[8,2,4608]{2,0,1:T(8,128)(2,1)S(1)} %constant_dynamic-update-slice_fusion), channel_id=1, source_target_pairs={{0,2},{2,0},{1,3},{3,1},{4,6},{6,4},{5,7},{7,5},{8,10},{10,8},{9,1... | collective-permute-start | bytes 442376 | tf_op jit(solution)/shard_map/ppermute | solution.py:69
  12.6 25.4 %copy-start.1 = (s32[8]{0:T(128)S(1)}, s32[8]{0:T(128)}, u32[]{:S(2)}) copy-start(s32[8]{0:T(128)} %param.11) | copy-start | bytes 100
  44.7 1.3 collective-permute-start.3
  46.0 4.3 %collective-permute-start.4 = (f32[16,2,512]{2,0,1:T(8,128)S(1)}, f32[16,2,512]{2,0,1:T(8,128)S(1)}, u32[]{:S(2)}, u32[]{:S(2)}) collective-permute-start(f32[16,2,512]{2,0,1:T(8,128)S(1)} %dynamic-slice_add_fusion), channel_id=1, source_target_pairs={{0,4},{4,0},{8,12},{12,8},{1,5},{5,1},{9,13},{13,9},{2,6},{6,2},{1... | collective-permute-start | bytes 196616 | tf_op jit(solution)/shard_map/ppermute | solution.py:107
  50.4 6.8 %collective-permute-start.5 = (f32[16,2,512]{2,0,1:T(8,128)S(1)}, f32[16,2,512]{2,0,1:T(8,128)S(1)}, u32[]{:S(2)}, u32[]{:S(2)}) collective-permute-start(f32[16,2,512]{2,0,1:T(8,128)S(1)} %add.186), channel_id=1, source_target_pairs={{0,8},{4,12},{8,0},{12,4},{1,9},{5,13},{9,1},{13,5},{2,10},{6,14},... | collective-permute-start | bytes 196616 | tf_op jit(solution)/shard_map/ppermute | solution.py:107
  53.8 23.9 %all-to-all-start = ((bf16[8,2,48,96]{3,2,1,0:T(8,128)(2,1)}), bf16[8,2,48,96]{3,2,1,0:T(8,128)(2,1)S(1)}, u32[]{:S(2)}, u32[]{:S(2)}) async-start(bf16[8,2,48,96]{3,2,1,0:T(8,128)(2,1)} %broadcast_select_fusion), calls=%async_computation | async-start | bytes 393216 | tf_op jit(solution)/shard_map/all_to_all | solution.py:150
  58.1 1.3 collective-permute-start.6
  67.1 9.8 %collective-permute-start.9 = (bf16[8,2,16,384]{3,0,2,1:T(8,128)(2,1)S(1)}, bf16[8,2,16,384]{3,0,2,1:T(8,128)(2,1)S(1)}, u32[]{:S(2)}, u32[]{:S(2)}) collective-permute-start(bf16[8,2,16,384]{3,0,2,1:T(8,128)(2,1)S(1)} %slice.279), channel_id=1, source_target_pairs={{0,2},{2,0},{1,3},{3,1},{4,6},{6,4},{5,7},{7,5},{8,10},{10,8},{9,1... | collective-permute-start | bytes 589832 | tf_op jit(solution)/shard_map/ppermute | solution.py:69
  75.4 15.6 %collective-permute-start.8 = (bf16[8,2,16,384]{3,0,2,1:T(8,128)(2,1)S(1)}, bf16[8,2,16,384]{3,0,2,1:T(8,128)(2,1)S(1)}, u32[]{:S(2)}, u32[]{:S(2)}) collective-permute-start(bf16[8,2,16,384]{3,0,2,1:T(8,128)(2,1)S(1)} %slice.280), channel_id=1, source_target_pairs={{0,2},{2,0},{1,3},{3,1},{4,6},{6,4},{5,7},{7,5},{8,10},{10,8},{9,1... | collective-permute-start | bytes 589832 | tf_op jit(solution)/shard_map/ppermute | solution.py:69
  77.7 14.0 %all-to-all-start.3 = ((bf16[8,2,16,384]{3,2,1,0:T(8,128)(2,1)}), bf16[8,2,16,384]{3,2,1,0:T(8,128)(2,1)S(1)}, u32[]{:S(2)}, u32[]{:S(2)}) async-start(bf16[8,2,16,384]{3,2,1,0:T(8,128)(2,1)} %copy.44), calls=%async_computation.3 | async-start | bytes 393216 | tf_op jit(solution)/shard_map/all_to_all | solution.py:150
  90.4 7.4 %collective-permute-start.7 = (bf16[8,2,16,384]{3,0,2,1:T(8,128)(2,1)S(1)}, bf16[8,2,16,384]{3,0,2,1:T(8,128)(2,1)S(1)}, u32[]{:S(2)}, u32[]{:S(2)}) collective-permute-start(bf16[8,2,16,384]{3,0,2,1:T(8,128)(2,1)S(1)} %slice.281), channel_id=1, source_target_pairs={{0,2},{2,0},{1,3},{3,1},{4,6},{6,4},{5,7},{7,5},{8,10},{10,8},{9,1... | collective-permute-start | bytes 589832 | tf_op jit(solution)/shard_map/ppermute | solution.py:69
  91.7 13.4 %all-to-all-start.2 = ((bf16[8,2,16,384]{3,2,1,0:T(8,128)(2,1)}), bf16[8,2,16,384]{3,2,1,0:T(8,128)(2,1)S(1)}, u32[]{:S(2)}, u32[]{:S(2)}) async-start(bf16[8,2,16,384]{3,2,1,0:T(8,128)(2,1)} %copy.41), calls=%async_computation.2 | async-start | bytes 393216 | tf_op jit(solution)/shard_map/all_to_all | solution.py:150
  105.1 11.6 %all-to-all-start.1 = ((bf16[8,2,16,384]{3,2,1,0:T(8,128)(2,1)}), bf16[8,2,16,384]{3,2,1,0:T(8,128)(2,1)S(1)}, u32[]{:S(2)}, u32[]{:S(2)}) async-start(bf16[8,2,16,384]{3,2,1,0:T(8,128)(2,1)} %copy.38), calls=%async_computation.1 | async-start | bytes 393216 | tf_op jit(solution)/shard_map/all_to_all | solution.py:150

commit v2 on v1

v2 whole, which is shorter than its diff:
```python
import functools

import jax
import jax.numpy as jnp
from jax import lax
from jax.experimental import pallas as pl
from jax.experimental.pallas import tpu as pltpu
from jax.sharding import PartitionSpec as P

TERMS = 4
NS_STEPS = 2
ROWS = ("chol", "orb")
HALF = jnp.bfloat16
FULL = jnp.float32
LANES = 128
TILE = 8
VMEM = pltpu.VMEM


def split_half(value):
    high = value.astype(HALF)
    return high, (value - high.astype(FULL)).astype(HALF)


def dot(left, right, contract=((1,), (0,))):
    return lax.dot_general(left, right, (contract, ((), ())), preferred_element_type=FULL)


def fine_dot(left, right):
    left_high, left_low = split_half(left)
    right_high, right_low = split_half(right)
    height = left.shape[0]
    both = dot(jnp.concatenate([left_high, left_low], 0), right_high)
    return both[:height] + both[height:] + dot(left_high, right_low)


def theta_kernel(grid_ref, inverse_ref, theta_ref):
    rows = grid_ref.shape[2]
    for w in range(grid_ref.shape[0]):
        stacked = jnp.concatenate([grid_ref[w, 0], grid_ref[w, 1]], 0)
        by_real = fine_dot(stacked, inverse_ref[w, 0])
        by_imag = fine_dot(stacked, inverse_ref[w, 1])
        theta_ref[w, 0] = (by_real[:rows] - by_imag[rows:]).astype(HALF)
        theta_ref[w, 1] = (by_imag[:rows] + by_real[rows:]).astype(HALF)


def spread_kernel(repeated_ref, spread_ref):
    height, vectors = repeated_ref.shape
    wide = LANES * TILE
    row = lax.broadcasted_iota(jnp.int32, (LANES, wide), 0)
    column = lax.broadcasted_iota(jnp.int32, (LANES, wide), 1)
    copies = (column // TILE == row).astype(FULL).astype(HALF)
    a = lax.broadcasted_iota(jnp.int32, (height, wide), 0) % TILE
    b = lax.broadcasted_iota(jnp.int32, (height, wide), 1) % TILE
    keep = a == b
    for block in range(vectors // LANES):
        values = dot(repeated_ref[:, block * LANES : (block + 1) * LANES], copies)
        spread_ref[:, block * wide : (block + 1) * wide] = jnp.where(keep, values, 0.0).astype(HALF)


def spread_coefficient(coefficient):
    count, vectors = coefficient.shape
    repeated = jnp.repeat(coefficient, TILE, axis=0)
    return pl.pallas_call(
        spread_kernel,
        out_shape=jax.ShapeDtypeStruct((count * TILE, vectors * TILE), HALF),
        in_specs=[pl.BlockSpec(memory_space=VMEM)],
        out_specs=pl.BlockSpec(memory_space=VMEM),
        compiler_params=pltpu.CompilerParams(vmem_limit_bytes=24 << 20),
        name="spread",
    )(repeated)


def field_kernel(steps, mine, spread_ref, vectors_ref, own_ref, sent_ref, total_ref):
    step = pl.program_id(0)
    group, tiles, _, orbitals = vectors_ref.shape
    depth = group * TILE
    count = spread_ref.shape[0] // TILE
    left = spread_ref[:, pl.ds(pl.multiple_of(step * depth, LANES), depth)]
    right = jnp.concatenate(
        [vectors_ref[:, t].reshape(depth, orbitals) for t in range(tiles)], 1
    )
    product = dot(left, right)

    @pl.when(step == 0)
    def _():
        total_ref[...] = product

    @pl.when(step > 0)
    def _():
        total_ref[...] += product

    @pl.when(step == steps - 1)
    def _():
        for t in range(tiles):
            block = total_ref[:, t * orbitals : (t + 1) * orbitals]
            block = block.reshape(count, TILE, orbitals)
            own_ref[:, t * TILE : (t + 1) * TILE] = block[:mine]
            sent_ref[:, t * TILE : (t + 1) * TILE] = block[mine:].astype(HALF)


def field_rows(spread, tiled_vectors, part, tiles, mine):
    vectors, _, _, orbitals = tiled_vectors.shape
    count = spread.shape[0] // TILE
    group = min(vectors, 512)
    steps = vectors // group
    rows = tiles * TILE
    return pl.pallas_call(
        functools.partial(field_kernel, steps, mine),
        grid=(steps,),
        in_specs=[
            pl.BlockSpec(memory_space=VMEM),
            pl.BlockSpec((group, tiles, TILE, orbitals), lambda k: (k, part, 0, 0)),
        ],
        out_specs=[
            pl.BlockSpec((mine, rows, orbitals), lambda k: (0, 0, 0)),
            pl.BlockSpec((count - mine, rows, orbitals), lambda k: (0, 0, 0)),
        ],
        out_shape=[
            jax.ShapeDtypeStruct((mine, rows, orbitals), FULL),
            jax.ShapeDtypeStruct((count - mine, rows, orbitals), HALF),
        ],
        scratch_shapes=[VMEM((count * TILE, tiles * orbitals), FULL)],
        compiler_params=pltpu.CompilerParams(vmem_limit_bytes=32 << 20),
        cost_estimate=pl.CostEstimate(
            flops=2 * count * TILE * vectors * rows * orbitals,
            bytes_accessed=2 * vectors * rows * orbitals,
            transcendentals=0,
        ),
        name="field",
    )(spread, tiled_vectors)


def walker_kernel(count, orbitals, electrons, *refs):
    piece_refs = refs[:count]
    start_ref, out_ref, field_ref, start_wide_ref = refs[count:]
    blocks, _, rows, _ = start_ref.shape
    wide = start_wide_ref.shape[1] // 2
    start_wide_ref[...] = jnp.zeros_like(start_wide_ref)
    for r in range(blocks):
        for c in range(2):
            at = r * rows
            start_wide_ref[pl.ds(at, rows), pl.ds(c * wide, electrons)] = start_ref[r, c]
            at = c * orbitals + r * rows
            for piece_ref in piece_refs:
                height = piece_ref.shape[2]
                field_ref[pl.ds(at, height)] = piece_ref[r, c]
                at += height
    current = start_wide_ref[...]
    summed = current.astype(FULL)
    for order in range(1, TERMS + 1):
        product = dot(field_ref[...], current)
        top, low = product[:orbitals], product[orbitals:]
        following = jnp.concatenate(
            [top[:, :wide] - low[:, wide:], top[:, wide:] + low[:, :wide]], 1
        )
        following = following * (1.0 / order)
        summed = summed + following
        current = following.astype(HALF)

    high, low = split_half(summed)
    rows_first = ((0,), (0,))
    gram = dot(high, high, rows_first) + dot(high, low, rows_first) + dot(low, high, rows_first)
    gram_real = (gram[:wide, :wide] + gram[wide:, wide:]) * (1.0 / orbitals)
    gram_imag = (gram[:wide, wide:] - gram[wide:, :wide]) * (1.0 / orbitals)
    row = lax.broadcasted_iota(jnp.int32, (wide, wide), 0)
    column = lax.broadcasted_iota(jnp.int32, (wide, wide), 1)
    identity = jnp.where((row == column) & (row < electrons), 1.0, 0.0)
    scale = jnp.sum(gram_real * identity, axis=0, keepdims=True)
    scale = jnp.sum(scale, axis=1, keepdims=True) * (1.0 / electrons)

    def times(left, right):
        product = fine_dot(jnp.concatenate(left, 0), jnp.concatenate(right, 1))
        real = product[:wide, :wide] - product[wide:, wide:]
        return real, product[:wide, wide:] + product[wide:, :wide]

    iterate = (gram_real / scale, gram_imag / scale)
    root = None
    for sweep in range(NS_STEPS):
        real, imag = iterate if root is None else times(root, iterate)
        step = (1.5 * identity - 0.5 * real, -0.5 * imag)
        if sweep + 1 < NS_STEPS:
            iterate = times(iterate, step)
        root = step if root is None else times(step, root)
    inverse = lax.rsqrt(scale)
    root = jnp.concatenate([root[0] * inverse, root[1] * inverse], 1)
    product = fine_dot(jnp.concatenate([summed[:, :wide], summed[:, wide:]], 0), root)
    top, low = product[:orbitals], product[orbitals:]
    real = (top[:, :wide] - low[:, wide:]).astype(HALF)
    imag = (top[:, wide:] + low[:, :wide]).astype(HALF)
    for r in range(blocks):
        out_ref[r, 0] = real[r * rows : (r + 1) * rows, :electrons]
        out_ref[r, 1] = imag[r * rows : (r + 1) * rows, :electrons]


def walker_step(pieces, start):
    orbitals = pieces[0].shape[3]
    electrons = start.shape[3]
    wide = -(-electrons // LANES) * LANES
    return pl.pallas_call(
        functools.partial(walker_kernel, len(pieces), orbitals, electrons),
        out_shape=jax.ShapeDtypeStruct(start.shape, HALF),
        in_specs=[pl.BlockSpec(memory_space=VMEM)] * (len(pieces) + 1),
        out_specs=pl.BlockSpec(memory_space=VMEM),
        scratch_shapes=[VMEM((2 * orbitals, orbitals), HALF), VMEM((orbitals, 2 * wide), HALF)],
        compiler_params=pltpu.CompilerParams(vmem_limit_bytes=24 << 20),
        name="walker",
    )(*pieces, start)


def shift(value, axis, step):
    size = lax.axis_size(axis)
    return lax.ppermute(value, axis, [(i, (i + step) % size) for i in range(size)])


def gather_relative(value, axis):
    size = lax.axis_size(axis)
    return jnp.concatenate([value] + [shift(value, axis, -s) for s in range(1, size)], 0)


def scatter_sum(value, axis, dim):
    size = lax.axis_size(axis)
    here = lax.axis_index(axis)
    width = value.shape[dim] // size
    total = lax.dynamic_slice_in_dim(value, here * width, width, dim)
    for s in range(1, size):
        block = lax.dynamic_slice_in_dim(value, ((here + s) % size) * width, width, dim)
        total = total + shift(block, axis, s)
    return total


def gather_ordered(value, axis, dim):
    size = lax.axis_size(axis)
    here = lax.axis_index(axis)
    width = value.shape[dim]
    shape = list(value.shape)
    shape[dim] = width * size
    whole = jnp.zeros(shape, value.dtype)
    for s in range(size):
        block = value if s == 0 else shift(value, axis, s)
        whole = lax.dynamic_update_slice_in_dim(whole, block, ((here - s) % size) * width, dim)
    return whole


def exchange_sum(value, axis):
    size = lax.axis_size(axis)
    if size & (size - 1):
        return sum([shift(value, axis, s) for s in range(1, size)], value)
    step = 1
    while step < size:
        value = value + lax.ppermute(value, axis, [(i, i ^ step) for i in range(size)])
        step *= 2
    return value


def body(walkers, correlation_inverse, half_vectors, field_vectors, samples, source):
    local_walkers = walkers.shape[0]
    vectors, row_block, orbitals = field_vectors.shape
    electrons = correlation_inverse.shape[2]
    planes = lax.axis_size("walk")
    population = local_walkers * planes
    plane = lax.axis_index("walk")
    devices_rows = lax.axis_size(ROWS)
    sharers = devices_rows // local_walkers
    col_width = electrons // sharers
    tiled = row_block % (2 * TILE) == 0 and vectors % LANES == 0

    wanted = gather_relative(source, "walk")
    wanted = (wanted - plane * local_walkers) % population
    grid = walkers.reshape(local_walkers, 2, row_block, electrons)
    all_grid = gather_relative(grid.astype(HALF), "walk")
    picked = jnp.take(all_grid, wanted[:local_walkers], axis=0)
    theta = pl.pallas_call(
        theta_kernel,
        out_shape=jax.ShapeDtypeStruct(grid.shape, HALF),
        in_specs=[pl.BlockSpec(memory_space=VMEM)] * 2,
        out_specs=pl.BlockSpec(memory_space=VMEM),
        compiler_params=pltpu.CompilerParams(vmem_limit_bytes=24 << 20),
        name="theta",
    )(grid, correlation_inverse)
    theta = theta.reshape(local_walkers, 2, row_block * electrons)
    all_theta = gather_relative(theta, "walk")
    bias = jnp.einsum("wcj,gj->wcg", all_theta, half_vectors, preferred_element_type=FULL)
    bias = exchange_sum(scatter_sum(bias, "orb", 2), "chol")
    width = bias.shape[2]
    drawn = lax.dynamic_slice_in_dim(samples, lax.axis_index("orb") * width, width, 1)
    drawn = jnp.roll(drawn, -plane * local_walkers, axis=0)
    coefficient = jnp.stack([bias[:, 1], drawn - bias[:, 0]], 1).astype(HALF)
    coefficient = jnp.take(coefficient, wanted, axis=0)
    coefficient = gather_ordered(coefficient, "orb", 2)

    def to_owners(value):
        value = jnp.broadcast_to(value[:, None], (local_walkers, sharers) + value.shape[1:])
        value = value.reshape((devices_rows,) + value.shape[2:])
        return lax.all_to_all(value, ROWS, split_axis=0, concat_axis=0, tiled=True)

    columns = to_owners(picked)

    def add_planes(own, sent):
        total = own
        for s in range(1, planes):
            block = sent[(s - 1) * local_walkers : s * local_walkers]
            total = total + shift(block, "walk", s)
        return total.astype(HALF)

    pieces = []
    if tiled:
        spread = spread_coefficient(coefficient.reshape(population * 2, vectors))
        tiled_vectors = field_vectors.reshape(vectors, row_block // TILE, TILE, orbitals)
        rows = 2 * TILE
        for part in range(row_block // rows):
            own, sent = field_rows(spread, tiled_vectors, part, 2, local_walkers * 2)
            own = own.reshape(local_walkers, 2, rows, orbitals)
            sent = sent.reshape(population - local_walkers, 2, rows, orbitals)
            pieces.append(to_owners(add_planes(own, sent)))
    else:
        field = jnp.einsum(
            "wcg,gab->wcab", coefficient, field_vectors, preferred_element_type=FULL
        )
        own, sent = field[:local_walkers], field[local_walkers:].astype(HALF)
        whole = to_owners(add_planes(own, sent)).transpose(1, 0, 2, 3)
        pieces.append(whole.reshape(1, 2, orbitals, orbitals))
        columns = columns.transpose(1, 0, 2, 3).reshape(1, 2, orbitals, electrons)

    normalized = walker_step(pieces, columns)
    if not tiled:
        normalized = normalized.reshape(2, devices_rows, row_block, electrons)
        normalized = normalized.transpose(1, 0, 2, 3)
    if sharers > 1:
        share = lax.axis_index(ROWS) % sharers
        normalized = lax.dynamic_slice_in_dim(normalized, share * col_width, col_width, 3)
    returned = lax.all_to_all(normalized, ROWS, split_axis=0, concat_axis=0, tiled=True)
    if sharers > 1:
        returned = returned.reshape(local_walkers, sharers, 2, row_block, col_width)
        returned = returned.transpose(0, 2, 3, 1, 4)
    return returned.reshape(local_walkers, 2, row_block * electrons).astype(FULL)


def solution(mesh):
    placed = (
        P(("groups", "walk"), None, ("chol", "orb")),
        P(("groups", "walk"), None, None, None),
        P(("groups", "walk"), ("chol", "orb")),
        P(("groups", "walk"), ("chol", "orb"), None),
        P("groups", "walk"),
        P(("groups", "walk")),
    )
    return jax.shard_map(
        body,
        mesh=mesh,
        in_specs=placed,
        out_specs=P(("groups", "walk"), None, ("chol", "orb")),
        check_vma=False,
    )
```

time: 140 us -> 114 us (0.81)
  matrix products: 44.7 us -> 6.5 us
  Pallas kernels: 0 us -> 27.2 us
  local copies, waits for them, and re-layouts: 31.9 us -> 7.48 us
  blocking collectives: 10.7 us -> 21.4 us
  waiting for transfers between devices: 19.7 us -> 16.2 us
  other arithmetic: 1.64 us -> 4.06 us
    dot_general x43 -> x0, matrix products: 38.2 us -> none  [the longest x3 23 us: body(): jnp.einsum('wcg,gab->wcab', coefficient, vectors, preferred_element_type=...]
    pallas_call x0 -> x6, Pallas kernels: none -> 27.2 us  [the longest x3 21.3 us: field_rows(): pl.pallas_call(functools.partial(field_kernel, steps, mine), grid=(steps,...]
    slice x4 -> x0, local copies, waits for them, and re-layouts: 25.4 us -> none  [the longest x1 25.3 us: body(): lax.slice_in_dim(field_vectors, part * rows, (part + 1) * rows, axis=1)]
    all_to_all x0 -> x1, blocking collectives: none -> 10.7 us  [to_owners(): return lax.all_to_all(value, ROWS, split_axis=0, concat_axis=0, tiled=True)]
    all_to_all x4 -> x3, waiting for transfers between devices: 14.6 us -> 8.26 us  [to_owners(): return lax.all_to_all(value, ROWS, split_axis=0, concat_axis=0, tiled=True)]
    unnamed x6 -> x8, local copies, waits for them, and re-layouts: 1.07 us -> 3.33 us
    convert_element_type x4 -> x1, local copies, waits for them, and re-layouts: 3.2 us -> 1.09 us  [body(): returned.reshape(local_walkers, 2, row_block * electrons).astype(FULL)]
    ppermute x2, waiting for transfers between devices: 2.01 us -> 4.06 us  [exchange_sum(): lax.ppermute(value, axis, [(i, i ^ step) for i in range(size)])]
  transfers between devices with their start and end apart: 14 -> 13, of which waited for: 6 -> 5; matrix products, arithmetic and copies ran while one was open for 47% -> 10% of each run, Pallas kernels for 0% -> 20%
where the time goes in v2:
time: 114 us; the launch traced here: 113 us
  starting transfers between devices  30.1 us (26%)
  Pallas kernels  27.2 us (24%)
  blocking collectives  21.4 us (19%)
  waiting for transfers between devices  16.2 us (14%)
  local copies, waits for them, and re-layouts  7.48 us (7%)
  matrix products  6.5 us (6%)
  other arithmetic  4.06 us (4%)
    pallas_call x3, Pallas kernels, field_rows(): pl.pallas_call(functools.partial(field_kernel, steps, mine), grid=(steps,...  21.3 us
    all_to_all x3, starting transfers between devices, to_owners(): return lax.all_to_all(value, ROWS, split_axis=0, concat_axis=0, tiled=True)  16 us
    all_to_all x1, blocking collectives, body(): lax.all_to_all(normalized, ROWS, split_axis=0, concat_axis=0, tiled=True)  10.7 us
    all_to_all x1, blocking collectives, to_owners(): return lax.all_to_all(value, ROWS, split_axis=0, concat_axis=0, tiled=True)  10.7 us
    ppermute x8, starting transfers between devices, shift(): lax.ppermute(value, axis, [(i, (i + step) % size) for i in range(size)])  8.98 us
    all_to_all x3, waiting for transfers between devices, to_owners(): return lax.all_to_all(value, ROWS, split_axis=0, concat_axis=0, tiled=True)  8.26 us
    dot_general x1, matrix products, body(): jnp.einsum('wcj,gj->wcg', all_theta, half_vectors, preferred_element_type...  6.5 us
    ppermute x2, starting transfers between devices, exchange_sum(): lax.ppermute(value, axis, [(i, i ^ step) for i in range(size)])  5.1 us
  transfers between devices with their start and end apart: 13, of which 5 were waited for; matrix products, arithmetic and copies ran while one was open for 10% of the time, Pallas kernels for 20%

profile of v2, /device:TPU:0, one launch (start us, length us, event | category | flops | bytes accessed | tf_op | source)
XLA Modules:
  0.0 113.2 jit_solution(12557709340539151057)
XLA Ops:
  0.0 1.3 %reshape.122.grid_ref = f32[8,2,48,96]{3,2,1,0:T(8,128)S(1)} reshape(f32[8,2,4608]{2,1,0:T(2,128)} %param.6) | data formatting | bytes 589824 | tf_op jit(solution)/shard_map/reshape | solution.py:270
  1.3 1.1 copy-done.3
  2.4 0.5 theta.1
  2.9 0.3 reshape.123
  3.2 3.0 %collective-permute-start.1 = (bf16[8,2,4608]{2,0,1:T(8,128)(2,1)S(1)}, bf16[8,2,4608]{2,0,1:T(8,128)(2,1)S(1)}, u32[]{:S(2)}, u32[]{:S(2)}) collective-permute-start(bf16[8,2,4608]{2,0,1:T(8,128)(2,1)S(1)} %copy.10), channel_id=1, source_target_pairs={{0,2},{2,0},{1,3},{3,1},{4,6},{6,4},{5,7},{7,5},{8,10},{10,8},{9,1... | collective-permute-start | bytes 442376 | tf_op jit(solution)/shard_map/ppermute | solution.py:213
  6.2 0.1 collective-permute-start
  6.4 2.0 %collective-permute-start.9 = (bf16[8,2,48,96]{3,2,1,0:T(8,128)(2,1)S(1)}, bf16[8,2,48,96]{3,2,1,0:T(8,128)(2,1)S(1)}, u32[]{:S(2)}, u32[]{:S(2)}) collective-permute-start(bf16[8,2,48,96]{3,2,1,0:T(8,128)(2,1)S(1)} %convert_element_type.34), channel_id=1, source_target_pairs={{0,2},{2,0},{1,3},{3,1},{4,6},{6,4},{5,7},{7,5},{8,10},{10,8},{9,1... | collective-permute-start | bytes 442376 | tf_op jit(solution)/shard_map/ppermute | solution.py:213
  8.4 2.7 %collective-permute-done = s32[8]{0:T(128)S(1)} collective-permute-done((s32[8]{0:T(128)}, s32[8]{0:T(128)S(1)}, u32[]{:S(2)}, u32[]{:S(2)}) %collective-permute-start) | collective-permute-done | bytes 64 | tf_op jit(solution)/shard_map/ppermute | solution.py:213
  11.0 0.7 compare_and_fusion.1
  11.8 0.7 fusion.11
  12.5 0.0 collective-permute-done.1
  12.5 6.5 %fusion = f32[16,2,1024]{2,0,1:T(8,128)S(1)} fusion(bf16[1024,4608]{1,0:T(8,128)(2,1)} %param.8, bf16[8,2,4608]{2,0,1:T(8,128)(2,1)S(1)} %collective-permute-done.1, bf16[8,2,4608]{2,0,1:T(8,128)(2,1)S(1)} %copy.10), kind=kOutput, calls=%fused_computation.2 | convolution fusion | flops 302579712 | bytes 9863168 | tf_op jit(solution)/shard_map/wcj,gj->wcg/dot_general | solution.py:283
  19.1 0.1 collective-permute-start.2
  19.2 1.2 %collective-permute-done.2 = f32[16,2,512]{2,0,1:T(8,128)S(1)} collective-permute-done((f32[16,2,512]{2,0,1:T(8,128)S(1)}, f32[16,2,512]{2,0,1:T(8,128)S(1)}, u32[]{:S(2)}, u32[]{:S(2)}) %collective-permute-start.2) | collective-permute-done | bytes 65568 | tf_op jit(solution)/shard_map/ppermute | solution.py:213
  20.4 2.2 %collective-permute-start.3 = (f32[16,2,512]{2,0,1:T(8,128)S(1)}, f32[16,2,512]{2,0,1:T(8,128)S(1)}, u32[]{:S(2)}, u32[]{:S(2)}) collective-permute-start(f32[16,2,512]{2,0,1:T(8,128)S(1)} %dynamic-slice_add_fusion), channel_id=1, source_target_pairs={{0,4},{4,0},{8,12},{12,8},{1,5},{5,1},{9,13},{13,9},{2,6},{6,2},{1... | collective-permute-start | bytes 196616 | tf_op jit(solution)/shard_map/ppermute | solution.py:251
  22.6 2.4 %collective-permute-done.3 = f32[16,2,512]{2,0,1:T(8,128)S(1)} collective-permute-done((f32[16,2,512]{2,0,1:T(8,128)S(1)}, f32[16,2,512]{2,0,1:T(8,128)S(1)}, u32[]{:S(2)}, u32[]{:S(2)}) %collective-permute-start.3) | collective-permute-done | bytes 65568 | tf_op jit(solution)/shard_map/ppermute | solution.py:251
  25.0 2.9 %collective-permute-start.4 = (f32[16,2,512]{2,0,1:T(8,128)S(1)}, f32[16,2,512]{2,0,1:T(8,128)S(1)}, u32[]{:S(2)}, u32[]{:S(2)}) collective-permute-start(f32[16,2,512]{2,0,1:T(8,128)S(1)} %add.98), channel_id=1, source_target_pairs={{0,8},{4,12},{8,0},{12,4},{1,9},{5,13},{9,1},{13,5},{2,10},{6,14},... | collective-permute-start | bytes 196616 | tf_op jit(solution)/shard_map/ppermute | solution.py:251
  27.9 0.0 collective-permute-done.9
  27.9 0.1 pad_maximum_fusion
  28.0 0.6 gather_fusion.1
  28.6 1.6 %collective-permute-done.4 = f32[16,2,512]{2,0,1:T(8,128)S(1)} collective-permute-done((f32[16,2,512]{2,0,1:T(8,128)S(1)}, f32[16,2,512]{2,0,1:T(8,128)S(1)}, u32[]{:S(2)}, u32[]{:S(2)}) %collective-permute-start.4) | collective-permute-done | bytes 65568 | tf_op jit(solution)/shard_map/ppermute | solution.py:251
  30.4 0.6 gather_fusion
  31.0 0.1 constant_dynamic-update-slice_fusion.1
  31.2 0.1 collective-permute-start.5
  31.3 0.8 broadcast_select_fusion
  32.0 5.8 %all-to-all-start.3 = ((bf16[8,2,48,96]{3,2,1,0:T(8,128)(2,1)}), bf16[8,2,48,96]{3,2,1,0:T(8,128)(2,1)S(1)}, u32[]{:S(2)}, u32[]{:S(2)}) async-start(bf16[8,2,48,96]{3,2,1,0:T(8,128)(2,1)} %broadcast_select_fusion), calls=%async_computation.3 | async-start | bytes 393216 | tf_op jit(solution)/shard_map/all_to_all | solution.py:295
  37.9 0.0 collective-permute-done.5
  37.9 0.1 broadcast_bitcast_fusion.repeated_ref
  38.0 1.3 %spread.1.spread_ref = bf16[256,8192]{1,0:T(8,128)(2,1)S(1)} custom-call(bf16[256,1024]{1,0:T(8,128)(2,1)S(1)} %broadcast_bitcast_fusion.repeated_ref), custom_call_target="tpu_custom_call" | custom-call | tf_op jit(solution)/shard_map/spread/pallas_call | solution.py:64
  39.3 8.1 %field.3 = (f32[16,16,384]{2,1,0:T(8,128)S(1)}, bf16[16,16,384]{2,1,0:T(8,128)(2,1)S(1)}) custom-call(bf16[256,8192]{1,0:T(8,128)(2,1)S(1)} %spread.1.spread_ref, bf16[1024,6,8,384]{3,2,1,0:T(8,128)(2,1)} %bitcast.34), custom_call_target="tpu_custom_call" | custom-call | flops 3221225472 | bytes 12582912 | tf_op jit(solution)/shard_map/field/pallas_call | solution.py:108
  47.4 1.6 %collective-permute-start.6 = (bf16[8,2,16,384]{3,2,1,0:T(8,128)(2,1)S(1)}, bf16[8,2,16,384]{3,2,1,0:T(8,128)(2,1)S(1)}, u32[]{:S(2)}, u32[]{:S(2)}) collective-permute-start(bf16[8,2,16,384]{3,2,1,0:T(8,128)(2,1)S(1)} %bitcast.33), channel_id=1, source_target_pairs={{0,2},{2,0},{1,3},{3,1},{4,6},{6,4},{5,7},{7,5},{8,10},{10,8},{9,1... | collective-permute-start | bytes 589832 | tf_op jit(solution)/shard_map/ppermute | solution.py:213
  49.0 6.6 %field.4 = (f32[16,16,384]{2,1,0:T(8,128)S(1)}, bf16[16,16,384]{2,1,0:T(8,128)(2,1)S(1)}) custom-call(bf16[256,8192]{1,0:T(8,128)(2,1)S(1)} %spread.1.spread_ref, bf16[1024,6,8,384]{3,2,1,0:T(8,128)(2,1)} %bitcast.35), custom_call_target="tpu_custom_call" | custom-call | flops 3221225472 | bytes 12582912 | tf_op jit(solution)/shard_map/field/pallas_call | solution.py:108
  55.6 0.6 collective-permute-start.7
  56.2 0.0 collective-permute-done.6
  56.2 0.7 add_convert_fusion.2
  56.9 5.1 %all-to-all-start = ((bf16[8,2,16,384]{3,2,1,0:T(8,128)(2,1)}), bf16[8,2,16,384]{3,2,1,0:T(8,128)(2,1)S(1)}, u32[]{:S(2)}, u32[]{:S(2)}) async-start(bf16[8,2,16,384]{3,2,1,0:T(8,128)(2,1)} %add_convert_fusion.2), calls=%async_computation | async-start | bytes 393216 | tf_op jit(solution)/shard_map/all_to_all | solution.py:295
  62.0 2.2 %copy-done.2 = bf16[256,8192]{1,0:T(8,128)(2,1)S(1)} copy-done((bf16[256,8192]{1,0:T(8,128)(2,1)S(1)}, bf16[256,8192]{1,0:T(8,128)(2,1)}, u32[]{:S(2)}) %copy-start.2) | copy-done | bytes 4194328
  64.2 6.6 %field.5 = (f32[16,16,384]{2,1,0:T(8,128)S(1)}, bf16[16,16,384]{2,1,0:T(8,128)(2,1)S(1)}) custom-call(bf16[256,8192]{1,0:T(8,128)(2,1)S(1)} %copy-done.2, bf16[1024,6,8,384]{3,2,1,0:T(8,128)(2,1)} %bitcast.36), custom_call_target="tpu_custom_call" | custom-call | flops 3221225472 | bytes 12582912 | tf_op jit(solution)/shard_map/field/pallas_call | solution.py:108
  70.8 1.6 %collective-permute-start.8 = (bf16[8,2,16,384]{3,2,1,0:T(8,128)(2,1)S(1)}, bf16[8,2,16,384]{3,2,1,0:T(8,128)(2,1)S(1)}, u32[]{:S(2)}, u32[]{:S(2)}) collective-permute-start(bf16[8,2,16,384]{3,2,1,0:T(8,128)(2,1)S(1)} %bitcast.32), channel_id=1, source_target_pairs={{0,2},{2,0},{1,3},{3,1},{4,6},{6,4},{5,7},{7,5},{8,10},{10,8},{9,1... | collective-permute-start | bytes 589832 | tf_op jit(solution)/shard_map/ppermute | solution.py:213
  72.3 0.7 add_convert_fusion.1
  73.1 0.0 all-to-all-done.refs_0_
  73.1 5.1 %all-to-all-start.1 = ((bf16[8,2,16,384]{3,2,1,0:T(8,128)(2,1)}), bf16[8,2,16,384]{3,2,1,0:T(8,128)(2,1)S(1)}, u32[]{:S(2)}, u32[]{:S(2)}) async-start(bf16[8,2,16,384]{3,2,1,0:T(8,128)(2,1)} %add_convert_fusion.1), calls=%async_computation.1 | async-start | bytes 393216 | tf_op jit(solution)/shard_map/all_to_all | solution.py:295
  78.2 0.0 collective-permute-done.8
  78.2 8.2 %all-to-all-done.1.refs_1_ = bf16[8,2,16,384]{3,2,1,0:T(8,128)(2,1)S(1)} async-done(((bf16[8,2,16,384]{3,2,1,0:T(8,128)(2,1)}), bf16[8,2,16,384]{3,2,1,0:T(8,128)(2,1)S(1)}, u32[]{:S(2)}, u32[]{:S(2)}) %all-to-all-start.1) | async-done | bytes 196640 | tf_op jit(solution)/shard_map/all_to_all | solution.py:295
  86.5 10.7 %all_to_all.25.refs_2_ = bf16[8,2,16,384]{3,2,1,0:T(8,128)(2,1)S(1)} all-to-all(bf16[8,2,16,384]{3,2,1,0:T(8,128)(2,1)S(1)} %add_convert_fusion), channel_id=1, replica_groups=mesh['groups'=2,'chol'=4,'walk'=2,'orb'=2] {'chol','orb'}, dimensions={0} | all-to-all | bytes 393216 | tf_op jit(solution)/shard_map/all_to_all | solution.py:295
  97.2 4.2 %walker.1 = bf16[8,2,48,96]{3,2,1,0:T(8,128)(2,1)S(1)} custom-call(bf16[8,2,16,384]{3,2,1,0:T(8,128)(2,1)S(1)} %all-to-all-done.refs_0_, bf16[8,2,16,384]{3,2,1,0:T(8,128)(2,1)S(1)} %all-to-all-done.1.refs_1_, bf16[8,2,16,384]{3,2,1,0:T(8,128)(2,1)S(1)} %all_to_all.25.refs_2_, bf16[8,2,48,96]{3,2,1,0:T(8,128)(2,1)S(1)} %all-to-all-done.3.refs_3_), custom_call_target="tpu_custom_call" | custom-call | tf_op jit(solution)/shard_map/walker/pallas_call | solution.py:200
  101.4 10.7 %all_to_all.26 = bf16[8,2,48,96]{3,2,1,0:T(8,128)(2,1)S(1)} all-to-all(bf16[8,2,48,96]{3,2,1,0:T(8,128)(2,1)S(1)} %walker.1), channel_id=1, replica_groups=mesh['groups'=2,'chol'=4,'walk'=2,'orb'=2] {'chol','orb'}, dimensions={0} | all-to-all | bytes 294912 | tf_op jit(solution)/shard_map/all_to_all | solution.py:332
  112.1 1.1 reshape.133
  (26 shorter events, 0.4 us)
Async XLA Ops:
  0.0 8.4 %copy-start = (f32[16,1024]{1,0:T(8,128)S(1)}, f32[16,1024]{1,0:T(8,128)}, u32[]{:S(2)}) copy-start(f32[16,1024]{1,0:T(8,128)} %param.10) | copy-start | bytes 196612
  1.3 1.1 %copy-start.3 = (f32[8,2,96,96]{3,2,1,0:T(8,128)S(1)}, f32[8,2,96,96]{3,2,1,0:T(8,128)}, u32[]{:S(2)}) copy-start(f32[8,2,96,96]{3,2,1,0:T(8,128)} %inverse_ref.1) | copy-start | bytes 1769476
  3.2 9.3 %collective-permute-start.1 = (bf16[8,2,4608]{2,0,1:T(8,128)(2,1)S(1)}, bf16[8,2,4608]{2,0,1:T(8,128)(2,1)S(1)}, u32[]{:S(2)}, u32[]{:S(2)}) collective-permute-start(bf16[8,2,4608]{2,0,1:T(8,128)(2,1)S(1)} %copy.10), channel_id=1, source_target_pairs={{0,2},{2,0},{1,3},{3,1},{4,6},{6,4},{5,7},{7,5},{8,10},{10,8},{9,1... | collective-permute-start | bytes 442376 | tf_op jit(solution)/shard_map/ppermute | solution.py:213
  6.2 4.8 %collective-permute-start = (s32[8]{0:T(128)}, s32[8]{0:T(128)S(1)}, u32[]{:S(2)}, u32[]{:S(2)}) collective-permute-start(s32[8]{0:T(128)} %param.11), channel_id=1, source_target_pairs={{0,2},{2,0},{1,3},{3,1},{4,6},{6,4},{5,7},{7,5},{8,10},{10,8},{9,1... | collective-permute-start | bytes 104 | tf_op jit(solution)/shard_map/ppermute | solution.py:213
  6.4 21.6 %collective-permute-start.9 = (bf16[8,2,48,96]{3,2,1,0:T(8,128)(2,1)S(1)}, bf16[8,2,48,96]{3,2,1,0:T(8,128)(2,1)S(1)}, u32[]{:S(2)}, u32[]{:S(2)}) collective-permute-start(bf16[8,2,48,96]{3,2,1,0:T(8,128)(2,1)S(1)} %convert_element_type.34), channel_id=1, source_target_pairs={{0,2},{2,0},{1,3},{3,1},{4,6},{6,4},{5,7},{7,5},{8,10},{10,8},{9,1... | collective-permute-start | bytes 442376 | tf_op jit(solution)/shard_map/ppermute | solution.py:213
  19.1 1.3 %collective-permute-start.2 = (f32[16,2,512]{2,0,1:T(8,128)S(1)}, f32[16,2,512]{2,0,1:T(8,128)S(1)}, u32[]{:S(2)}, u32[]{:S(2)}) collective-permute-start(f32[16,2,512]{2,0,1:T(8,128)S(1)} %constant_dynamic-slice_fusion.1), channel_id=1, source_target_pairs={{0,1},{1,0},{2,3},{3,2},{4,5},{5,4},{6,7},{7,6},{8,9},{9,8},{10,11... | collective-permute-start | bytes 196616 | tf_op jit(solution)/shard_map/ppermute | solution.py:213
  20.4 4.6 %collective-permute-start.3 = (f32[16,2,512]{2,0,1:T(8,128)S(1)}, f32[16,2,512]{2,0,1:T(8,128)S(1)}, u32[]{:S(2)}, u32[]{:S(2)}) collective-permute-start(f32[16,2,512]{2,0,1:T(8,128)S(1)} %dynamic-slice_add_fusion), channel_id=1, source_target_pairs={{0,4},{4,0},{8,12},{12,8},{1,5},{5,1},{9,13},{13,9},{2,6},{6,2},{1... | collective-permute-start | bytes 196616 | tf_op jit(solution)/shard_map/ppermute | solution.py:251
  25.0 5.3 %collective-permute-start.4 = (f32[16,2,512]{2,0,1:T(8,128)S(1)}, f32[16,2,512]{2,0,1:T(8,128)S(1)}, u32[]{:S(2)}, u32[]{:S(2)}) collective-permute-start(f32[16,2,512]{2,0,1:T(8,128)S(1)} %add.98), channel_id=1, source_target_pairs={{0,8},{4,12},{8,0},{12,4},{1,9},{5,13},{9,1},{13,5},{2,10},{6,14},... | collective-permute-start | bytes 196616 | tf_op jit(solution)/shard_map/ppermute | solution.py:251
  31.2 6.7 %collective-permute-start.5 = (bf16[16,2,512]{2,1,0:T(2,128)(2,1)S(1)}, bf16[16,2,512]{2,1,0:T(2,128)(2,1)S(1)}, u32[]{:S(2)}, u32[]{:S(2)}) collective-permute-start(bf16[16,2,512]{2,1,0:T(2,128)(2,1)S(1)} %get-tuple-element.20), channel_id=1, source_target_pairs={{0,1},{1,0},{2,3},{3,2},{4,5},{5,4},{6,7},{7,6},{8,9},{9,8},{10,11... | collective-permute-start | bytes 98312 | tf_op jit(solution)/shard_map/ppermute | solution.py:213
  32.0 24.9 %all-to-all-start.3 = ((bf16[8,2,48,96]{3,2,1,0:T(8,128)(2,1)}), bf16[8,2,48,96]{3,2,1,0:T(8,128)(2,1)S(1)}, u32[]{:S(2)}, u32[]{:S(2)}) async-start(bf16[8,2,48,96]{3,2,1,0:T(8,128)(2,1)} %broadcast_select_fusion), calls=%async_computation.3 | async-start | bytes 393216 | tf_op jit(solution)/shard_map/all_to_all | solution.py:295
  39.3 9.7 %copy-start.1 = (bf16[256,8192]{1,0:T(8,128)(2,1)}, bf16[256,8192]{1,0:T(8,128)(2,1)S(1)}, u32[]{:S(2)}) copy-start(bf16[256,8192]{1,0:T(8,128)(2,1)S(1)} %spread.1.spread_ref) | copy-start | bytes 12582916
  47.4 8.8 %collective-permute-start.6 = (bf16[8,2,16,384]{3,2,1,0:T(8,128)(2,1)S(1)}, bf16[8,2,16,384]{3,2,1,0:T(8,128)(2,1)S(1)}, u32[]{:S(2)}, u32[]{:S(2)}) collective-permute-start(bf16[8,2,16,384]{3,2,1,0:T(8,128)(2,1)S(1)} %bitcast.33), channel_id=1, source_target_pairs={{0,2},{2,0},{1,3},{3,1},{4,6},{6,4},{5,7},{7,5},{8,10},{10,8},{9,1... | collective-permute-start | bytes 589832 | tf_op jit(solution)/shard_map/ppermute | solution.py:213
  55.6 16.8 %collective-permute-start.7 = (bf16[8,2,16,384]{3,2,1,0:T(8,128)(2,1)S(1)}, bf16[8,2,16,384]{3,2,1,0:T(8,128)(2,1)S(1)}, u32[]{:S(2)}, u32[]{:S(2)}) collective-permute-start(bf16[8,2,16,384]{3,2,1,0:T(8,128)(2,1)S(1)} %bitcast.31), channel_id=1, source_target_pairs={{0,2},{2,0},{1,3},{3,1},{4,6},{6,4},{5,7},{7,5},{8,10},{10,8},{9,1... | collective-permute-start | bytes 589832 | tf_op jit(solution)/shard_map/ppermute | solution.py:213
  56.9 16.2 %all-to-all-start = ((bf16[8,2,16,384]{3,2,1,0:T(8,128)(2,1)}), bf16[8,2,16,384]{3,2,1,0:T(8,128)(2,1)S(1)}, u32[]{:S(2)}, u32[]{:S(2)}) async-start(bf16[8,2,16,384]{3,2,1,0:T(8,128)(2,1)} %add_convert_fusion.2), calls=%async_computation | async-start | bytes 393216 | tf_op jit(solution)/shard_map/all_to_all | solution.py:295
  62.0 2.2 %copy-start.2 = (bf16[256,8192]{1,0:T(8,128)(2,1)S(1)}, bf16[256,8192]{1,0:T(8,128)(2,1)}, u32[]{:S(2)}) copy-start(bf16[256,8192]{1,0:T(8,128)(2,1)} %copy-done.1) | copy-start | bytes 12582916
  70.8 7.4 %collective-permute-start.8 = (bf16[8,2,16,384]{3,2,1,0:T(8,128)(2,1)S(1)}, bf16[8,2,16,384]{3,2,1,0:T(8,128)(2,1)S(1)}, u32[]{:S(2)}, u32[]{:S(2)}) collective-permute-start(bf16[8,2,16,384]{3,2,1,0:T(8,128)(2,1)S(1)} %bitcast.32), channel_id=1, source_target_pairs={{0,2},{2,0},{1,3},{3,1},{4,6},{6,4},{5,7},{7,5},{8,10},{10,8},{9,1... | collective-permute-start | bytes 589832 | tf_op jit(solution)/shard_map/ppermute | solution.py:213
  73.1 13.4 %all-to-all-start.1 = ((bf16[8,2,16,384]{3,2,1,0:T(8,128)(2,1)}), bf16[8,2,16,384]{3,2,1,0:T(8,128)(2,1)S(1)}, u32[]{:S(2)}, u32[]{:S(2)}) async-start(bf16[8,2,16,384]{3,2,1,0:T(8,128)(2,1)} %add_convert_fusion.1), calls=%async_computation.1 | async-start | bytes 393216 | tf_op jit(solution)/shard_map/all_to_all | solution.py:295

commit v3 on v2

v3 whole, which is shorter than its diff:
```python
import functools

import jax
import jax.numpy as jnp
from jax import lax
from jax.experimental import pallas as pl
from jax.experimental.pallas import tpu as pltpu
from jax.sharding import PartitionSpec as P


TERMS = 4
NS_STEPS = 2
ROWS = ("chol", "orb")
HALF = jnp.bfloat16
FULL = jnp.float32
LANES = 128
TILE = 8
SMALL = 8 << 20
VMEM = pltpu.VMEM


def split_half(value):
    high = value.astype(HALF)
    return high, (value - high.astype(FULL)).astype(HALF)


def dot(left, right, contract=((1,), (0,))):
    return lax.dot_general(left, right, (contract, ((), ())), preferred_element_type=FULL)


def fine_dot(left, right):
    left_high, left_low = split_half(left)
    right_high, right_low = split_half(right)
    height = left.shape[0]
    both = dot(jnp.concatenate([left_high, left_low], 0), right_high)
    return both[:height] + both[height:] + dot(left_high, right_low)


def theta_kernel(grid_ref, inverse_ref, theta_ref):
    rows = grid_ref.shape[2]
    for w in range(grid_ref.shape[0]):
        stacked = jnp.concatenate([grid_ref[w, 0], grid_ref[w, 1]], 0)
        by_real = fine_dot(stacked, inverse_ref[w, 0])
        by_imag = fine_dot(stacked, inverse_ref[w, 1])
        theta_ref[w, 0] = (by_real[:rows] - by_imag[rows:]).astype(HALF)
        theta_ref[w, 1] = (by_imag[:rows] + by_real[rows:]).astype(HALF)


def fill_spread(place_ref, own_ref, received_ref, spread_ref):
    count, half = own_ref.shape
    height = count * TILE
    wide = LANES * TILE
    row = lax.broadcasted_iota(jnp.int32, (LANES, wide), 0)
    column = lax.broadcasted_iota(jnp.int32, (LANES, wide), 1)
    copies = (column // TILE == row).astype(FULL).astype(HALF)
    a = lax.broadcasted_iota(jnp.int32, (height, wide), 0) % TILE
    b = lax.broadcasted_iota(jnp.int32, (height, wide), 1) % TILE
    keep = a == b
    row = lax.broadcasted_iota(jnp.int32, (height, count), 0)
    column = lax.broadcasted_iota(jnp.int32, (height, count), 1)
    repeats = (row // TILE == column).astype(FULL).astype(HALF)
    low = place_ref[1] == 0
    own, received = own_ref[...].astype(FULL), received_ref[...].astype(FULL)
    for part, values in enumerate((jnp.where(low, own, received), jnp.where(low, received, own))):
        values = dot(repeats, values.astype(HALF)).astype(HALF)
        for block in range(half // LANES):
            at = (part * half + block * LANES) * TILE
            wider = dot(values[:, block * LANES : (block + 1) * LANES], copies)
            spread_ref[:, at : at + wide] = jnp.where(keep, wider, 0.0).astype(HALF)


SCALARS = pl.BlockSpec(memory_space=pltpu.SMEM)
ARRAY = pl.BlockSpec(memory_space=VMEM)


def local_kernel(kernel, in_specs, out_shape, scratch_shapes=()):
    return pl.pallas_call(
        kernel,
        in_specs=in_specs,
        out_specs=jax.tree.map(lambda _: ARRAY, out_shape),
        out_shape=out_shape,
        scratch_shapes=list(scratch_shapes),
        compiler_params=pltpu.CompilerParams(vmem_limit_bytes=SMALL),
    )


def wanted_walker(place_ref, source_ref, others_ref, i, population):
    local = source_ref.shape[0]
    walker = source_ref[i] if i < local else others_ref[i - local]
    relative = walker - place_ref[0]
    return walker, jnp.where(relative < 0, relative + population, relative)


def pick_kernel(place_ref, source_ref, own_ref, received_ref, keep_ref, send_ref, all_ref):
    local = own_ref.shape[0]
    population = all_ref.shape[0]
    all_ref[:local] = own_ref[...]
    all_ref[local:] = received_ref[...]
    for t in range(local // 2):
        for target_ref, core in ((keep_ref, place_ref[1]), (send_ref, 1 - place_ref[1])):
            relative = source_ref[2 * t + core] - place_ref[0]
            relative = jnp.where(relative < 0, relative + population, relative)
            target_ref[t, 0] = all_ref[relative]


def split_kernel(step, place_ref, own_ref, received_ref, keep_ref, send_ref):
    senders = own_ref.shape[1]
    bit = (place_ref[2] // step) % 2
    for t in range(own_ref.shape[0] // 2):
        for target_ref, side in ((keep_ref, bit), (send_ref, 1 - bit)):
            target_ref[t, :senders] = own_ref[2 * t + side]
            target_ref[t, senders:] = received_ref[2 * t + side]


def bias_kernel(place_ref, own_ref, received_ref, vectors_ref, keep_ref, send_ref):
    angles = jnp.concatenate([own_ref[...], received_ref[...]], 0)
    bias = dot(vectors_ref[...], angles, ((1,), (1,))).T
    half = bias.shape[1] // 2
    first, second = bias[:, :half], bias[:, half:]
    low = place_ref[1] == 0
    keep_ref[...] = jnp.where(low, first, second)
    send_ref[...] = jnp.where(low, second, first)


def add_kernel(left_ref, right_ref, out_ref):
    out_ref[...] = left_ref[...] + right_ref[...]


def coefficient_kernel(
    place_ref, source_ref, others_ref, left_ref, right_ref, samples_ref, out_ref, bias_ref, row_ref
):
    bias_ref[...] = left_ref[...] + right_ref[...]
    count, half = bias_ref.shape
    lanes = pl.ds(pl.multiple_of(place_ref[1] * half, LANES), half)
    for i in range(count // 2):
        walker, relative = wanted_walker(place_ref, source_ref, others_ref, i, count // 2)
        row_ref[2 * i : 2 * i + 1] = bias_ref[pl.ds(2 * relative + 1, 1)]
        drawn = samples_ref[pl.ds(walker, 1), lanes]
        row_ref[2 * i + 1 : 2 * i + 2] = drawn - bias_ref[pl.ds(2 * relative, 1)]
    out_ref[...] = row_ref[...].astype(HALF)


def read_kernel(half_hbm, field_hbm, half_ref, chunk_ref, semaphores):
    tiles = chunk_ref.shape[1]
    copies = []
    for source_ref, target_ref in (
        (half_hbm, half_ref),
        (field_hbm.at[:, pl.ds(0, tiles)], chunk_ref),
    ):
        vectors = target_ref.shape[0]
        for block in range(vectors // LANES):
            group = pl.ds(block * LANES, LANES)
            semaphore = semaphores.at[len(copies)]
            copy = pltpu.make_async_copy(source_ref.at[group], target_ref.at[group], semaphore)
            copy.start()
            copies.append(copy)
    for copy in copies:
        copy.wait()


def read_early(half_vectors, tiled_vectors, tiles):
    vectors, _, _, orbitals = tiled_vectors.shape
    chunk = jax.ShapeDtypeStruct((vectors, tiles, TILE, orbitals), HALF)
    size = half_vectors.size + chunk.size
    return pl.pallas_call(
        read_kernel,
        in_specs=[pl.BlockSpec(memory_space=pltpu.HBM)] * 2,
        out_specs=[pl.BlockSpec(memory_space=VMEM)] * 2,
        out_shape=[VMEM(half_vectors.shape, HALF), VMEM(chunk.shape, HALF)],
        scratch_shapes=[pltpu.SemaphoreType.DMA((2 * (vectors // LANES),))],
        compiler_params=pltpu.CompilerParams(vmem_limit_bytes=36 << 20),
        cost_estimate=pl.CostEstimate(flops=0, bytes_accessed=2 * size, transcendentals=0),
        name="read",
    )(half_vectors, tiled_vectors)


def field_kernel(part, parts, mine, *refs):
    refs = list(refs)
    left_refs = [refs.pop(0) for _ in range(3 if part == 0 else 1)]
    chunk_ref, vectors_ref, own_ref, sent_ref = refs[:4]
    refs = refs[4:]
    spread_ref = refs.pop(0) if part == 0 else left_refs[0]
    vectors, tiles, _, orbitals = chunk_ref.shape
    count = spread_ref.shape[0] // TILE
    copies = []
    if part + 1 < parts:
        next_ref, semaphores = refs
        for block in range(vectors // LANES):
            group = pl.ds(block * LANES, LANES)
            copy = pltpu.make_async_copy(
                vectors_ref.at[group, pl.ds((part + 1) * tiles, tiles)],
                next_ref.at[group],
                semaphores.at[block],
            )
            copy.start()
            copies.append(copy)
    if part == 0:
        fill_spread(*left_refs, spread_ref)
    group = min(vectors, 4 * LANES)
    depth = group * TILE
    total = None
    for block in range(vectors // group):
        right = jnp.concatenate(
            [
                chunk_ref[block * group : (block + 1) * group, t].reshape(depth, orbitals)
                for t in range(tiles)
            ],
            1,
        )
        product = dot(spread_ref[:, block * depth : (block + 1) * depth], right)
        total = product if total is None else total + product
    for t in range(tiles):
        slab = total[:, t * orbitals : (t + 1) * orbitals].reshape(count, TILE, orbitals)
        own_ref[:, t * TILE : (t + 1) * TILE] = slab[:mine]
        sent_ref[:, t * TILE : (t + 1) * TILE] = slab[mine:].astype(HALF)
    for copy in copies:
        copy.wait()


def field_rows(left, chunk, tiled_vectors, part, parts, count, mine):
    vectors, tiles, _, orbitals = chunk.shape
    rows = tiles * TILE
    out_shape = [
        jax.ShapeDtypeStruct((mine, rows, orbitals), FULL),
        jax.ShapeDtypeStruct((count - mine, rows, orbitals), HALF),
    ]
    if part == 0:
        out_shape.append(jax.ShapeDtypeStruct((count * TILE, vectors * TILE), HALF))
    scratch = []
    if part + 1 < parts:
        out_shape.append(jax.ShapeDtypeStruct(chunk.shape, HALF))
        scratch.append(pltpu.SemaphoreType.DMA((vectors // LANES,)))
    left_specs = [SCALARS, ARRAY, ARRAY] if part == 0 else [ARRAY]
    own, sent, *rest = pl.pallas_call(
        functools.partial(field_kernel, part, parts, mine),
        in_specs=left_specs + [ARRAY, pl.BlockSpec(memory_space=pltpu.HBM)],
        out_specs=[ARRAY] * len(out_shape),
        out_shape=out_shape,
        scratch_shapes=scratch,
        compiler_params=pltpu.CompilerParams(vmem_limit_bytes=SMALL),
        cost_estimate=pl.CostEstimate(
            flops=2 * count * TILE * vectors * rows * orbitals,
            bytes_accessed=2 * vectors * rows * orbitals,
            transcendentals=0,
        ),
        name="field",
    )(*left, chunk, tiled_vectors)
    left = [rest.pop(0)] if part == 0 else left
    return own, sent, left, rest[0] if rest else None


def combine_kernel(chunks, *refs):
    own_refs, received_refs, out_ref = refs[:chunks], refs[chunks:-1], refs[-1]
    others = len(received_refs) // chunks
    rows = own_refs[0].shape[2]
    for c in range(chunks):
        total = own_refs[c][...]
        for received_ref in received_refs[c * others : (c + 1) * others]:
            total = total + received_ref[...].astype(FULL)
        out_ref[:, :, c * rows : (c + 1) * rows] = total.astype(HALF)


def combine(owns, received):
    chunks = len(owns)
    slots, parts, rows, orbitals = owns[0].shape
    return pl.pallas_call(
        functools.partial(combine_kernel, chunks),
        out_shape=jax.ShapeDtypeStruct((slots, parts, rows * chunks, orbitals), HALF),
        in_specs=[pl.BlockSpec(memory_space=VMEM)] * (chunks + len(received)),
        out_specs=pl.BlockSpec(memory_space=VMEM),
        compiler_params=pltpu.CompilerParams(vmem_limit_bytes=SMALL),
        name="combine",
    )(*owns, *received)


def walker_kernel(count, orbitals, electrons, rank_ref, field_piece_ref, *refs):
    start_refs = refs[:count]
    out_ref, field_ref, start_wide_ref = refs[count:]
    blocks, _, rows, _ = field_piece_ref.shape
    wide = start_wide_ref.shape[1] // 2
    start_wide_ref[...] = jnp.zeros_like(start_wide_ref)
    for r in range(blocks):
        for c in range(2):
            field_ref[pl.ds(c * orbitals + r * rows, rows)] = field_piece_ref[r, c]
    block = 0
    for start_ref in start_refs:
        for d in range(start_ref.shape[0]):
            at = pl.multiple_of((rank_ref[0] ^ block) * rows, 2 * TILE)
            for c in range(2):
                start_wide_ref[pl.ds(at, rows), pl.ds(c * wide, electrons)] = start_ref[d, c]
            block += 1
    current = start_wide_ref[...]
    summed = current.astype(FULL)
    for order in range(1, TERMS + 1):
        product = dot(field_ref[...], current)
        top, low = product[:orbitals], product[orbitals:]
        following = jnp.concatenate(
            [top[:, :wide] - low[:, wide:], top[:, wide:] + low[:, :wide]], 1
        )
        following = following * (1.0 / order)
        summed = summed + following
        current = following.astype(HALF)

    high, low = split_half(summed)
    rows_first = ((0,), (0,))
    gram = dot(high, high, rows_first) + dot(high, low, rows_first) + dot(low, high, rows_first)
    gram_real = (gram[:wide, :wide] + gram[wide:, wide:]) * (1.0 / orbitals)
    gram_imag = (gram[:wide, wide:] - gram[wide:, :wide]) * (1.0 / orbitals)
    row = lax.broadcasted_iota(jnp.int32, (wide, wide), 0)
    column = lax.broadcasted_iota(jnp.int32, (wide, wide), 1)
    identity = jnp.where((row == column) & (row < electrons), 1.0, 0.0)
    scale = jnp.sum(gram_real * identity, axis=0, keepdims=True)
    scale = jnp.sum(scale, axis=1, keepdims=True) * (1.0 / electrons)

    def times(left, right):
        product = fine_dot(jnp.concatenate(left, 0), jnp.concatenate(right, 1))
        real = product[:wide, :wide] - product[wide:, wide:]
        return real, product[:wide, wide:] + product[wide:, :wide]

    iterate = (gram_real / scale, gram_imag / scale)
    root = None
    for sweep in range(NS_STEPS):
        real, imag = iterate if root is None else times(root, iterate)
        step = (1.5 * identity - 0.5 * real, -0.5 * imag)
        if sweep + 1 < NS_STEPS:
            iterate = times(iterate, step)
        root = step if root is None else times(step, root)
    inverse = lax.rsqrt(scale)
    root = jnp.concatenate([root[0] * inverse, root[1] * inverse], 1)
    product = fine_dot(jnp.concatenate([summed[:, :wide], summed[:, wide:]], 0), root)
    top, low = product[:orbitals], product[orbitals:]
    real = (top[:, :wide] - low[:, wide:]).astype(HALF)
    imag = (top[:, wide:] + low[:, :wide]).astype(HALF)
    for r in range(blocks):
        out_ref[r, 0] = real[r * rows : (r + 1) * rows, :electrons]
        out_ref[r, 1] = imag[r * rows : (r + 1) * rows, :electrons]


def walker_step(rank, field, starts):
    blocks, parts, rows, orbitals = field.shape
    electrons = starts[0].shape[3]
    wide = -(-electrons // LANES) * LANES
    return local_kernel(
        functools.partial(walker_kernel, len(starts), orbitals, electrons),
        [SCALARS] + [ARRAY] * (1 + len(starts)),
        jax.ShapeDtypeStruct((blocks, parts, rows, electrons), HALF),
        [VMEM((2 * orbitals, orbitals), HALF), VMEM((orbitals, 2 * wide), HALF)],
    )(rank, field, *starts)


def shift(value, axis, step):
    size = lax.axis_size(axis)
    return lax.ppermute(value, axis, [(i, (i + step) % size) for i in range(size)])


def scatter_sum(value, axis, dim):
    size = lax.axis_size(axis)
    here = lax.axis_index(axis)
    width = value.shape[dim] // size
    total = lax.dynamic_slice_in_dim(value, here * width, width, dim)
    for s in range(1, size):
        block = lax.dynamic_slice_in_dim(value, ((here + s) % size) * width, width, dim)
        total = total + shift(block, axis, s)
    return total


def gather_ordered(value, axis, dim):
    size = lax.axis_size(axis)
    here = lax.axis_index(axis)
    width = value.shape[dim]
    shape = list(value.shape)
    shape[dim] = width * size
    whole = jnp.zeros(shape, value.dtype)
    for s in range(size):
        block = value if s == 0 else shift(value, axis, s)
        whole = lax.dynamic_update_slice_in_dim(whole, block, ((here - s) % size) * width, dim)
    return whole


def exchange_sum(value, axis):
    size = lax.axis_size(axis)
    if size & (size - 1):
        return sum([shift(value, axis, s) for s in range(1, size)], value)
    step = 1
    while step < size:
        value = value + lax.ppermute(value, axis, [(i, i ^ step) for i in range(size)])
        step *= 2
    return value


def whole_step(walkers, correlation_inverse, half_vectors, field_vectors, samples, source):
    local = walkers.shape[0]
    vectors, row_block, orbitals = field_vectors.shape
    electrons = correlation_inverse.shape[2]
    planes = lax.axis_size("walk")
    population = local * planes
    count = population * 2
    devices_rows = lax.axis_size(ROWS)
    sharers = devices_rows // local
    first = lax.axis_index("walk") * local
    core = lax.axis_index("orb")
    chol = lax.axis_size("chol")
    half = vectors // 2
    fast = (
        row_block % (2 * TILE) == 0
        and vectors % (2 * LANES) == 0
        and lax.axis_size("orb") == 2
        and planes > 1
        and sharers == 1
        and chol & (chol - 1) == 0
    )

    def to_owners(value):
        value = jnp.broadcast_to(value[:, None], (local, sharers) + value.shape[1:])
        value = value.reshape((devices_rows,) + value.shape[2:])
        return lax.all_to_all(value, ROWS, split_axis=0, concat_axis=0, tiled=True)

    def others(value):
        return jnp.concatenate([shift(value, "walk", -s) for s in range(1, planes)], 0)

    def from_planes(sent):
        blocks = [sent[s * local : (s + 1) * local] for s in range(planes - 1)]
        return [shift(block, "walk", s + 1) for s, block in enumerate(blocks)]

    other_source = others(source)
    place = jnp.stack([first, core, lax.axis_index("chol")]).astype(jnp.int32)
    rank = lax.axis_index(ROWS).astype(jnp.int32).reshape(1)
    grid = walkers.reshape(local, 2, row_block, electrons)
    theta = local_kernel(
        theta_kernel, [ARRAY] * 2, jax.ShapeDtypeStruct(grid.shape, HALF)
    )(grid, correlation_inverse)
    theta = theta.reshape(local * 2, row_block * electrons)
    other_theta = others(theta)
    start = grid.astype(HALF)
    other_start = others(start)

    if fast:
        tiled_vectors = field_vectors.reshape(vectors, row_block // TILE, TILE, orbitals)
        half_vectors, chunk = read_early(half_vectors, tiled_vectors, 2)
        part_shape = jax.ShapeDtypeStruct((count, half), FULL)
        bias, sent = local_kernel(
            bias_kernel, [SCALARS] + [ARRAY] * 3, [part_shape] * 2
        )(place, theta, other_theta, half_vectors)
        received = shift(sent, "orb", 1)
        add = local_kernel(add_kernel, [ARRAY] * 2, part_shape)
        block = (2, row_block, electrons)
        slots = jax.ShapeDtypeStruct((local // 2, 1) + block, HALF)
        keep, sent = local_kernel(
            pick_kernel,
            [SCALARS] * 2 + [ARRAY] * 2,
            [slots] * 2,
            [VMEM((population,) + block, HALF)],
        )(place, source, start, other_start)
        passed = shift(sent, "orb", 1)
        step = 1
        while step < chol:
            pairs = [(i, i ^ step) for i in range(chol)]
            bias = add(bias, received)
            received = lax.ppermute(bias, "chol", pairs)
            slots = jax.ShapeDtypeStruct((keep.shape[0] // 2, keep.shape[1] * 2) + block, HALF)
            keep, sent = local_kernel(
                functools.partial(split_kernel, step), [SCALARS] + [ARRAY] * 2, [slots] * 2
            )(place, keep, passed)
            passed = lax.ppermute(sent, "chol", pairs)
            step *= 2
        coefficient = local_kernel(
            coefficient_kernel,
            [SCALARS] * 3 + [ARRAY] * 3,
            jax.ShapeDtypeStruct((count, half), HALF),
            [VMEM((count, half), FULL)] * 2,
        )(place, source, other_source, bias, received, samples)
        other_half = shift(coefficient, "orb", 1)
        rows = 2 * TILE
        parts = row_block // rows
        owns, received = [], []
        left = [place, coefficient, other_half]
        for part in range(parts):
            own, sent, left, chunk = field_rows(
                left, chunk, tiled_vectors, part, parts, count, local * 2
            )
            owns.append(own.reshape(local, 2, rows, orbitals))
            sent = sent.reshape(population - local, 2, rows, orbitals)
            received += from_planes(sent)
        field = to_owners(combine(owns, received))
        starts = [keep[0], passed[0]]
    else:
        wanted = jnp.concatenate([source, other_source], 0)
        relative = jnp.where(wanted < first, wanted - first + population, wanted - first)
        all_start = jnp.concatenate([start, other_start], 0)
        picked = all_start.at[relative[:local]].get(mode="promise_in_bounds")
        columns = to_owners(picked)
        angles = jnp.concatenate([theta, other_theta], 0)
        bias = jnp.einsum("ij,gj->ig", angles, half_vectors, preferred_element_type=FULL)
        bias = bias.reshape(population, 2, vectors)
        bias = exchange_sum(scatter_sum(bias, "orb", 2), "chol")
        bias = bias.at[relative].get(mode="promise_in_bounds")
        width = bias.shape[2]
        drawn = lax.dynamic_slice_in_dim(samples, core * width, width, 1)
        drawn = drawn.at[wanted].get(mode="promise_in_bounds")
        coefficient = jnp.stack([bias[:, 1], drawn - bias[:, 0]], 1).astype(HALF)
        coefficient = gather_ordered(coefficient, "orb", 2)
        field = jnp.einsum(
            "wcg,gab->wcab", coefficient, field_vectors, preferred_element_type=FULL
        )
        total = field[:local]
        for block in from_planes(field[local:].astype(HALF)):
            total = total + block
        field = to_owners(total.astype(HALF)).transpose(1, 0, 2, 3)
        field = field.reshape(1, 2, orbitals, orbitals)
        starts = [columns.transpose(1, 0, 2, 3).reshape(1, 2, orbitals, electrons)]
        rank = jnp.zeros((1,), jnp.int32)

    normalized = walker_step(rank, field, starts)
    if not fast:
        normalized = normalized.reshape(2, devices_rows, row_block, electrons)
        normalized = normalized.transpose(1, 0, 2, 3)
    if sharers > 1:
        share = lax.axis_index(ROWS) % sharers
        width = electrons // sharers
        normalized = lax.dynamic_slice_in_dim(normalized, share * width, width, 3)
    returned = lax.all_to_all(normalized, ROWS, split_axis=0, concat_axis=0, tiled=True)
    if sharers > 1:
        returned = returned.reshape(local, sharers, 2, row_block, width)
        returned = returned.transpose(0, 2, 3, 1, 4)
    return returned.reshape(local, 2, row_block * electrons).astype(FULL)


def solution(mesh):
    placed = (
        P(("groups", "walk"), None, ("chol", "orb")),
        P(("groups", "walk"), None, None, None),
        P(("groups", "walk"), ("chol", "orb")),
        P(("groups", "walk"), ("chol", "orb"), None),
        P("groups", "walk"),
        P(("groups", "walk")),
    )
    return jax.shard_map(
        whole_step,
        mesh=mesh,
        in_specs=placed,
        out_specs=P(("groups", "walk"), None, ("chol", "orb")),
        check_vma=False,
    )
```

time: 114 us -> 108 us (0.947)
  waiting for transfers between devices: 16.2 us -> 35.4 us
  starting transfers between devices: 30.1 us -> 19.6 us
  Pallas kernels: 27.2 us -> 36.7 us
  blocking collectives: 21.4 us -> 12 us
  matrix products: 6.5 us -> 0 us
  other arithmetic: 4.06 us -> 0.11 us
  local copies, waits for them, and re-layouts: 7.48 us -> 3.68 us
    ppermute x8 -> x9, waiting for transfers between devices: 3.91 us -> 21.5 us  [shift(): lax.ppermute(value, axis, [(i, (i + step) % size) for i in range(size)])]
    all_to_all x3 -> x1, starting transfers between devices: 16 us -> 4.47 us  [to_owners(): return lax.all_to_all(value, ROWS, split_axis=0, concat_axis=0, tiled=True)]
    ppermute x2 -> x4, waiting for transfers between devices: 4.06 us -> 13.9 us  [the longest x2 11.2 us: whole_step(): passed = lax.ppermute(sent, 'chol', pairs)]
    pallas_call x6 -> x14, Pallas kernels: 27.2 us -> 36.7 us  [the longest x3 17.8 us: field_rows(): pl.pallas_call(functools.partial(field_kernel, part, parts, mine), in_spe...]
    all_to_all x2 -> x1, blocking collectives: 21.4 us -> 12 us  [whole_step(): lax.all_to_all(normalized, ROWS, split_axis=0, concat_axis=0, tiled=True)]
    all_to_all x3 -> x1, waiting for transfers between devices: 8.26 us -> 0.01 us  [to_owners(): return lax.all_to_all(value, ROWS, split_axis=0, concat_axis=0, tiled=True)]
    dot_general x1 -> x0, matrix products: 6.5 us -> none  [body(): jnp.einsum('wcj,gj->wcg', all_theta, half_vectors, preferred_element_type...]
    unnamed x8 -> x6, local copies, waits for them, and re-layouts: 3.33 us -> 1.14 us
  transfers between devices with their start and end apart: 13 -> 14, of which waited for: 5 -> 10; matrix products, arithmetic and copies ran while one was open for 10% -> 0% of each run, Pallas kernels for 20% -> 17%
where the time goes in v3:
time: 108 us
  Pallas kernels  36.7 us (34%)
  waiting for transfers between devices  35.4 us (33%)
  starting transfers between devices  19.6 us (18%)
  blocking collectives  12 us (11%)
  local copies, waits for them, and re-layouts  3.68 us (3%)
    ppermute x9, waiting for transfers between devices, shift(): lax.ppermute(value, axis, [(i, (i + step) % size) for i in range(size)])  21.5 us
    pallas_call x3, Pallas kernels, field_rows(): pl.pallas_call(functools.partial(field_kernel, part, parts, mine), in_spe...  17.8 us
    all_to_all x1, blocking collectives, whole_step(): lax.all_to_all(normalized, ROWS, split_axis=0, concat_axis=0, tiled=True)  12 us
    ppermute x2, waiting for transfers between devices, whole_step(): passed = lax.ppermute(sent, 'chol', pairs)  11.2 us
    ppermute x9, starting transfers between devices, shift(): lax.ppermute(value, axis, [(i, (i + step) % size) for i in range(size)])  8.02 us
    pallas_call x1, Pallas kernels, read_early(): pl.pallas_call(read_kernel, in_specs=[pl.BlockSpec(memory_space=pltpu.HBM...  7.54 us
    all_to_all x1, starting transfers between devices, to_owners(): return lax.all_to_all(value, ROWS, split_axis=0, concat_axis=0, tiled=True)  4.47 us
    ppermute x2, starting transfers between devices, whole_step(): received = lax.ppermute(bias, 'chol', pairs)  4.3 us
  transfers between devices with their start and end apart: 14, of which 10 were waited for; matrix products, arithmetic and copies ran while one was open for 0% of the time, Pallas kernels for 17%

profile of v3, /device:TPU:0, one launch (start us, length us, event | category | flops | bytes accessed | tf_op | source)
XLA Modules:
  0.0 107.7 jit_solution(2708518831050733081)
XLA Ops:
  0.0 1.2 %reshape.34.grid_ref = f32[8,2,48,96]{3,2,1,0:T(8,128)S(1)} reshape(f32[8,2,4608]{2,1,0:T(2,128)} %param.6) | data formatting | bytes 589824 | tf_op jit(solution)/shard_map/reshape | solution.py:428
  1.3 1.1 %copy-done = f32[8,2,96,96]{3,2,1,0:T(8,128)S(1)} copy-done((f32[8,2,96,96]{3,2,1,0:T(8,128)S(1)}, f32[8,2,96,96]{3,2,1,0:T(8,128)}, u32[]{:S(2)}) %copy-start) | copy-done | bytes 589848
  2.4 0.5 shard_map.64
  2.8 0.2 reshape.35.own_ref
  3.1 3.0 %collective-permute-start.1 = (bf16[16,4608]{1,0:T(8,128)(2,1)S(1)}, bf16[16,4608]{1,0:T(8,128)(2,1)S(1)}, u32[]{:S(2)}, u32[]{:S(2)}) collective-permute-start(bf16[16,4608]{1,0:T(8,128)(2,1)S(1)} %reshape.35.own_ref), channel_id=1, source_target_pairs={{0,2},{2,0},{1,3},{3,1},{4,6},{6,4},{5,7},{7,5},{8,10},{10,8},{9,1... | collective-permute-start | bytes 442376 | tf_op jit(solution)/shard_map/ppermute | solution.py:353
  6.1 7.5 %read.1 = (bf16[1024,4608]{1,0:T(8,128)(2,1)S(1)}, bf16[1024,2,8,384]{3,2,1,0:T(8,128)(2,1)S(1)}) custom-call(bf16[1024,4608]{1,0:T(8,128)(2,1)} %half_hbm.1, bf16[1024,6,8,384]{3,2,1,0:T(8,128)(2,1)} %bitcast.25), custom_call_target="tpu_custom_call" | custom-call | bytes 22020096 | tf_op jit(solution)/shard_map/read/pallas_call | solution.py:165
  13.6 0.1 pad_add_fusion.place_ref.refs_0_
  13.7 0.0 collective-permute-done.1.received_ref
  13.7 3.1 %shard_map.65 = (f32[32,512]{1,0:T(8,128)S(1)}, f32[32,512]{1,0:T(8,128)S(1)}) custom-call(s32[3]{0:T(128)S(1)} %pad_add_fusion.place_ref.refs_0_, bf16[16,4608]{1,0:T(8,128)(2,1)S(1)} %reshape.35.own_ref, bf16[16,4608]{1,0:T(8,128)(2,1)S(1)} %collective-permute-done.1.received_ref, bf16[1024,4608]{1,0:T(8,128)(2,1)S(1)} %get-tuple-element.24.vectors_ref), custom_call_target="tpu_custom_call" | custom-call | tf_op jit(solution)/shard_map/pallas_call | solution.py:441
  16.9 0.1 collective-permute-start.2
  16.9 1.2 %collective-permute-done.2.right_ref = f32[32,512]{1,0:T(8,128)S(1)} collective-permute-done((f32[32,512]{1,0:T(8,128)S(1)}, f32[32,512]{1,0:T(8,128)S(1)}, u32[]{:S(2)}, u32[]{:S(2)}) %collective-permute-start.2) | collective-permute-done | bytes 65568 | tf_op jit(solution)/shard_map/ppermute | solution.py:353
  18.2 1.6 %collective-permute-start.3 = (f32[32,512]{1,0:T(8,128)S(1)}, f32[32,512]{1,0:T(8,128)S(1)}, u32[]{:S(2)}, u32[]{:S(2)}) collective-permute-start(f32[32,512]{1,0:T(8,128)S(1)} %shard_map.66.left_ref), channel_id=1, source_target_pairs={{0,4},{4,0},{8,12},{12,8},{1,5},{5,1},{9,13},{13,9},{2,6},{6,2},{1... | collective-permute-start | bytes 196616 | tf_op jit(solution)/shard_map/ppermute | solution.py:459
  19.8 2.7 %collective-permute-done.3.right_ref = f32[32,512]{1,0:T(8,128)S(1)} collective-permute-done((f32[32,512]{1,0:T(8,128)S(1)}, f32[32,512]{1,0:T(8,128)S(1)}, u32[]{:S(2)}, u32[]{:S(2)}) %collective-permute-start.3) | collective-permute-done | bytes 65568 | tf_op jit(solution)/shard_map/ppermute | solution.py:459
  22.5 2.7 %collective-permute-start.4 = (f32[32,512]{1,0:T(8,128)S(1)}, f32[32,512]{1,0:T(8,128)S(1)}, u32[]{:S(2)}, u32[]{:S(2)}) collective-permute-start(f32[32,512]{1,0:T(8,128)S(1)} %shard_map.67.left_ref), channel_id=1, source_target_pairs={{0,8},{4,12},{8,0},{12,4},{1,9},{5,13},{9,1},{13,5},{2,10},{6,14},... | collective-permute-start | bytes 196616 | tf_op jit(solution)/shard_map/ppermute | solution.py:459
  25.2 0.0 copy-done.2
  25.2 0.5 collective-permute-start
  25.7 3.0 %collective-permute-done.others_ref = s32[8]{0:T(128)S(1)} collective-permute-done((s32[8]{0:T(128)S(1)}, s32[8]{0:T(128)S(1)}, u32[]{:S(2)}, u32[]{:S(2)}) %collective-permute-start) | collective-permute-done | bytes 64 | tf_op jit(solution)/shard_map/ppermute | solution.py:353
  28.8 0.0 collective-permute-done.4.right_ref
  28.8 0.0 copy-done.1
  28.8 0.7 shard_map.68.refs_1_
  29.4 0.1 collective-permute-start.5
  29.5 1.2 %collective-permute-done.5.refs_2_ = bf16[32,512]{1,0:T(8,128)(2,1)S(1)} collective-permute-done((bf16[32,512]{1,0:T(8,128)(2,1)S(1)}, bf16[32,512]{1,0:T(8,128)(2,1)S(1)}, u32[]{:S(2)}, u32[]{:S(2)}) %collective-permute-start.5) | collective-permute-done | bytes 32800 | tf_op jit(solution)/shard_map/ppermute | solution.py:353
  30.7 8.8 %field.3 = (f32[16,16,384]{2,1,0:T(8,128)S(1)}, bf16[16,16,384]{2,1,0:T(8,128)(2,1)S(1)}, bf16[256,8192]{1,0:T(8,128)(2,1)S(1)}, bf16[1024,2,8,384]{3,2,1,0:T(8,128)(2,1)S(1)}) custom-call(s32[3]{0:T(128)S(1)} %pad_add_fusion.place_ref.refs_0_, bf16[32,512]{1,0:T(8,128)(2,1)S(1)} %shard_map.68.refs_1_, bf16[32,512]{1,0:T(8,128)(2,1)S(1)} %collective-permute-done.5.refs_2_, ...), custom_call_target="tpu_custom_call" | custom-call | flops 3221225472 | bytes 12582912 | tf_op jit(solution)/shard_map/field/pallas_call | solution.py:234
  39.5 0.6 collective-permute-start.6
  40.1 5.3 %field.4 = (f32[16,16,384]{2,1,0:T(8,128)S(1)}, bf16[16,16,384]{2,1,0:T(8,128)(2,1)S(1)}, bf16[1024,2,8,384]{3,2,1,0:T(8,128)(2,1)S(1)}) custom-call(bf16[256,8192]{1,0:T(8,128)(2,1)S(1)} %get-tuple-element.29.refs_0_, bf16[1024,2,8,384]{3,2,1,0:T(8,128)(2,1)S(1)} %get-tuple-element.30.refs_1_, bf16[1024,6,8,384]{3,2,1,0:T(8,128)(2,1)} %bitcast.27), custom_call_target="tpu_custom_call" | custom-call | flops 3221225472 | bytes 12582912 | tf_op jit(solution)/shard_map/field/pallas_call | solution.py:234
  45.5 3.7 %field.5 = (f32[16,16,384]{2,1,0:T(8,128)S(1)}, bf16[16,16,384]{2,1,0:T(8,128)(2,1)S(1)}) custom-call(bf16[256,8192]{1,0:T(8,128)(2,1)S(1)} %get-tuple-element.29.refs_0_, bf16[1024,2,8,384]{3,2,1,0:T(8,128)(2,1)S(1)} %get-tuple-element.32.refs_1_, bf16[1024,6,8,384]{3,2,1,0:T(8,128)(2,1)} %bitcast.28), custom_call_target="tpu_custom_call" | custom-call | flops 3221225472 | bytes 12582912 | tf_op jit(solution)/shard_map/field/pallas_call | solution.py:234
  49.2 1.5 %collective-permute-start.8 = (bf16[8,2,16,384]{3,2,1,0:T(8,128)(2,1)S(1)}, bf16[8,2,16,384]{3,2,1,0:T(8,128)(2,1)S(1)}, u32[]{:S(2)}, u32[]{:S(2)}) collective-permute-start(bf16[8,2,16,384]{3,2,1,0:T(8,128)(2,1)S(1)} %bitcast.24), channel_id=1, source_target_pairs={{0,2},{2,0},{1,3},{3,1},{4,6},{6,4},{5,7},{7,5},{8,10},{10,8},{9,1... | collective-permute-start | bytes 589832 | tf_op jit(solution)/shard_map/ppermute | solution.py:353
  50.7 0.5 collective-permute-start.7
  51.3 0.0 collective-permute-done.6.refs_3_
  51.3 5.7 %collective-permute-done.8.refs_5_ = bf16[8,2,16,384]{3,2,1,0:T(8,128)(2,1)S(1)} collective-permute-done((bf16[8,2,16,384]{3,2,1,0:T(8,128)(2,1)S(1)}, bf16[8,2,16,384]{3,2,1,0:T(8,128)(2,1)S(1)}, u32[]{:S(2)}, u32[]{:S(2)}) %collective-permute-start.8) | collective-permute-done | bytes 196640 | tf_op jit(solution)/shard_map/ppermute | solution.py:353
  57.0 3.1 %collective-permute-done.7.refs_4_ = bf16[8,2,16,384]{3,2,1,0:T(8,128)(2,1)S(1)} collective-permute-done((bf16[8,2,16,384]{3,2,1,0:T(8,128)(2,1)S(1)}, bf16[8,2,16,384]{3,2,1,0:T(8,128)(2,1)S(1)}, u32[]{:S(2)}, u32[]{:S(2)}) %collective-permute-start.7) | collective-permute-done | bytes 196640 | tf_op jit(solution)/shard_map/ppermute | solution.py:353
  60.1 1.0 combine.1
  61.1 4.5 %all-to-all-start = ((bf16[8,2,48,384]{3,2,1,0:T(8,128)(2,1)}), bf16[8,2,48,384]{3,2,1,0:T(8,128)(2,1)S(1)}, u32[]{:S(2)}, u32[]{:S(2)}) async-start(bf16[8,2,48,384]{3,2,1,0:T(8,128)(2,1)} %combine.1), calls=%async_computation | async-start | bytes 1179648 | tf_op jit(solution)/shard_map/all_to_all | solution.py:416
  65.6 1.5 %collective-permute-start.9 = (bf16[8,2,48,96]{3,2,1,0:T(8,128)(2,1)S(1)}, bf16[8,2,48,96]{3,2,1,0:T(8,128)(2,1)S(1)}, u32[]{:S(2)}, u32[]{:S(2)}) collective-permute-start(bf16[8,2,48,96]{3,2,1,0:T(8,128)(2,1)S(1)} %convert_element_type.9.own_ref), channel_id=1, source_target_pairs={{0,2},{2,0},{1,3},{3,1},{4,6},{6,4},{5,7},{7,5},{8,10},{10,8},{9,1... | collective-permute-start | bytes 442376 | tf_op jit(solution)/shard_map/ppermute | solution.py:353
  67.1 5.8 %collective-permute-done.9.received_ref = bf16[8,2,48,96]{3,2,1,0:T(8,128)(2,1)S(1)} collective-permute-done((bf16[8,2,48,96]{3,2,1,0:T(8,128)(2,1)S(1)}, bf16[8,2,48,96]{3,2,1,0:T(8,128)(2,1)S(1)}, u32[]{:S(2)}, u32[]{:S(2)}) %collective-permute-start.9) | collective-permute-done | bytes 147488 | tf_op jit(solution)/shard_map/ppermute | solution.py:353
  73.0 0.7 shard_map.69
  73.6 0.1 collective-permute-start.10
  73.7 1.3 %collective-permute-done.10.received_ref = bf16[4,1,2,48,96]{4,3,2,1,0:T(8,128)(2,1)S(1)} collective-permute-done((bf16[4,1,2,48,96]{4,3,2,1,0:T(8,128)(2,1)S(1)}, bf16[4,1,2,48,96]{4,3,2,1,0:T(8,128)(2,1)S(1)}, u32[]{:S(2)}, u32[]{:S(2)}) %collective-permute-start.10) | collective-permute-done | bytes 73760 | tf_op jit(solution)/shard_map/ppermute | solution.py:353
  75.0 0.6 shard_map.70
  75.6 1.7 %collective-permute-start.11 = (bf16[2,2,2,48,96]{4,3,2,1,0:T(8,128)(2,1)S(1)}, bf16[2,2,2,48,96]{4,3,2,1,0:T(8,128)(2,1)S(1)}, u32[]{:S(2)}, u32[]{:S(2)}) collective-permute-start(bf16[2,2,2,48,96]{4,3,2,1,0:T(8,128)(2,1)S(1)} %get-tuple-element.40), channel_id=1, source_target_pairs={{0,4},{4,0},{8,12},{12,8},{1,5},{5,1},{9,13},{13,9},{2,6},{6,2},{1... | collective-permute-start | bytes 221192 | tf_op jit(solution)/shard_map/ppermute | solution.py:464
  77.3 5.3 %collective-permute-done.11.received_ref = bf16[2,2,2,48,96]{4,3,2,1,0:T(8,128)(2,1)S(1)} collective-permute-done((bf16[2,2,2,48,96]{4,3,2,1,0:T(8,128)(2,1)S(1)}, bf16[2,2,2,48,96]{4,3,2,1,0:T(8,128)(2,1)S(1)}, u32[]{:S(2)}, u32[]{:S(2)}) %collective-permute-start.11) | collective-permute-done | bytes 73760 | tf_op jit(solution)/shard_map/ppermute | solution.py:464
  82.6 0.6 shard_map.71
  83.2 1.2 %collective-permute-start.12 = (bf16[1,4,2,48,96]{4,3,2,1,0:T(8,128)(2,1)S(1)}, bf16[1,4,2,48,96]{4,3,2,1,0:T(8,128)(2,1)S(1)}, u32[]{:S(2)}, u32[]{:S(2)}) collective-permute-start(bf16[1,4,2,48,96]{4,3,2,1,0:T(8,128)(2,1)S(1)} %get-tuple-element.42), channel_id=1, source_target_pairs={{0,8},{4,12},{8,0},{12,4},{1,9},{5,13},{9,1},{13,5},{2,10},{6,14},... | collective-permute-start | bytes 221192 | tf_op jit(solution)/shard_map/ppermute | solution.py:464
  84.4 5.9 %collective-permute-done.12 = bf16[1,4,2,48,96]{4,3,2,1,0:T(8,128)(2,1)S(1)} collective-permute-done((bf16[1,4,2,48,96]{4,3,2,1,0:T(8,128)(2,1)S(1)}, bf16[1,4,2,48,96]{4,3,2,1,0:T(8,128)(2,1)S(1)}, u32[]{:S(2)}, u32[]{:S(2)}) %collective-permute-start.12) | collective-permute-done | bytes 73760 | tf_op jit(solution)/shard_map/ppermute | solution.py:464
  90.3 0.0 all-to-all-done.field_piece_ref
  90.3 4.2 %shard_map.72 = bf16[8,2,48,96]{3,2,1,0:T(8,128)(2,1)S(1)} custom-call(s32[1]{0:T(128)} %bitcast.rank_ref, bf16[8,2,48,384]{3,2,1,0:T(8,128)(2,1)S(1)} %all-to-all-done.field_piece_ref, bf16[4,2,48,96]{3,2,1,0:T(8,128)(2,1)S(1)} %bitcast.20, bf16[4,2,48,96]{3,2,1,0:T(8,128)(2,1)S(1)} %bitcast.21), custom_call_target="tpu_custom_call" | custom-call | tf_op jit(solution)/shard_map/pallas_call | solution.py:343
  94.5 12.0 %all_to_all.10 = bf16[8,2,48,96]{3,2,1,0:T(8,128)(2,1)S(1)} all-to-all(bf16[8,2,48,96]{3,2,1,0:T(8,128)(2,1)S(1)} %shard_map.72), channel_id=1, replica_groups=mesh['groups'=2,'chol'=4,'walk'=2,'orb'=2] {'chol','orb'}, dimensions={0} | all-to-all | bytes 294912 | tf_op jit(solution)/shard_map/all_to_all | solution.py:521
  106.6 1.1 %reshape.43 = f32[8,2,4608]{2,1,0:T(2,128)} reshape(bf16[8,2,48,96]{3,2,1,0:T(8,128)(2,1)S(1)} %all_to_all.10) | data formatting | bytes 442368 | tf_op jit(solution)/shard_map/convert_element_type | solution.py:525
  (6 shorter events, 0.1 us)
Async XLA Ops:
  1.2 1.1 %copy-start = (f32[8,2,96,96]{3,2,1,0:T(8,128)S(1)}, f32[8,2,96,96]{3,2,1,0:T(8,128)}, u32[]{:S(2)}) copy-start(f32[8,2,96,96]{3,2,1,0:T(8,128)} %inverse_ref.1) | copy-start | bytes 1769476
  3.1 10.7 %collective-permute-start.1 = (bf16[16,4608]{1,0:T(8,128)(2,1)S(1)}, bf16[16,4608]{1,0:T(8,128)(2,1)S(1)}, u32[]{:S(2)}, u32[]{:S(2)}) collective-permute-start(bf16[16,4608]{1,0:T(8,128)(2,1)S(1)} %reshape.35.own_ref), channel_id=1, source_target_pairs={{0,2},{2,0},{1,3},{3,1},{4,6},{6,4},{5,7},{7,5},{8,10},{10,8},{9,1... | collective-permute-start | bytes 442376 | tf_op jit(solution)/shard_map/ppermute | solution.py:353
  6.1 19.1 %copy-start.2 = (s32[8]{0:T(128)S(1)}, s32[8]{0:T(128)}, u32[]{:S(2)}) copy-start(s32[8]{0:T(128)} %source_ref.3) | copy-start | bytes 100
  6.1 22.7 %copy-start.1 = (f32[16,1024]{1,0:T(8,128)S(1)}, f32[16,1024]{1,0:T(8,128)}, u32[]{:S(2)}) copy-start(f32[16,1024]{1,0:T(8,128)} %samples_ref.1) | copy-start | bytes 196612
  16.9 1.3 %collective-permute-start.2 = (f32[32,512]{1,0:T(8,128)S(1)}, f32[32,512]{1,0:T(8,128)S(1)}, u32[]{:S(2)}, u32[]{:S(2)}) collective-permute-start(f32[32,512]{1,0:T(8,128)S(1)} %get-tuple-element.26), channel_id=1, source_target_pairs={{0,1},{1,0},{2,3},{3,2},{4,5},{5,4},{6,7},{7,6},{8,9},{9,8},{10,11... | collective-permute-start | bytes 196616 | tf_op jit(solution)/shard_map/ppermute | solution.py:353
  18.2 4.3 %collective-permute-start.3 = (f32[32,512]{1,0:T(8,128)S(1)}, f32[32,512]{1,0:T(8,128)S(1)}, u32[]{:S(2)}, u32[]{:S(2)}) collective-permute-start(f32[32,512]{1,0:T(8,128)S(1)} %shard_map.66.left_ref), channel_id=1, source_target_pairs={{0,4},{4,0},{8,12},{12,8},{1,5},{5,1},{9,13},{13,9},{2,6},{6,2},{1... | collective-permute-start | bytes 196616 | tf_op jit(solution)/shard_map/ppermute | solution.py:459
  22.5 6.2 %collective-permute-start.4 = (f32[32,512]{1,0:T(8,128)S(1)}, f32[32,512]{1,0:T(8,128)S(1)}, u32[]{:S(2)}, u32[]{:S(2)}) collective-permute-start(f32[32,512]{1,0:T(8,128)S(1)} %shard_map.67.left_ref), channel_id=1, source_target_pairs={{0,8},{4,12},{8,0},{12,4},{1,9},{5,13},{9,1},{13,5},{2,10},{6,14},... | collective-permute-start | bytes 196616 | tf_op jit(solution)/shard_map/ppermute | solution.py:459
  25.2 3.6 %collective-permute-start = (s32[8]{0:T(128)S(1)}, s32[8]{0:T(128)S(1)}, u32[]{:S(2)}, u32[]{:S(2)}) collective-permute-start(s32[8]{0:T(128)S(1)} %copy-done.2), channel_id=1, source_target_pairs={{0,2},{2,0},{1,3},{3,1},{4,6},{6,4},{5,7},{7,5},{8,10},{10,8},{9,1... | collective-permute-start | bytes 104 | tf_op jit(solution)/shard_map/ppermute | solution.py:353
  29.4 1.3 %collective-permute-start.5 = (bf16[32,512]{1,0:T(8,128)(2,1)S(1)}, bf16[32,512]{1,0:T(8,128)(2,1)S(1)}, u32[]{:S(2)}, u32[]{:S(2)}) collective-permute-start(bf16[32,512]{1,0:T(8,128)(2,1)S(1)} %shard_map.68.refs_1_), channel_id=1, source_target_pairs={{0,1},{1,0},{2,3},{3,2},{4,5},{5,4},{6,7},{7,6},{8,9},{9,8},{10,11... | collective-permute-start | bytes 98312 | tf_op jit(solution)/shard_map/ppermute | solution.py:353
  39.5 11.7 %collective-permute-start.6 = (bf16[8,2,16,384]{3,2,1,0:T(8,128)(2,1)S(1)}, bf16[8,2,16,384]{3,2,1,0:T(8,128)(2,1)S(1)}, u32[]{:S(2)}, u32[]{:S(2)}) collective-permute-start(bf16[8,2,16,384]{3,2,1,0:T(8,128)(2,1)S(1)} %bitcast.22), channel_id=1, source_target_pairs={{0,2},{2,0},{1,3},{3,1},{4,6},{6,4},{5,7},{7,5},{8,10},{10,8},{9,1... | collective-permute-start | bytes 589832 | tf_op jit(solution)/shard_map/ppermute | solution.py:353
  49.2 7.8 %collective-permute-start.8 = (bf16[8,2,16,384]{3,2,1,0:T(8,128)(2,1)S(1)}, bf16[8,2,16,384]{3,2,1,0:T(8,128)(2,1)S(1)}, u32[]{:S(2)}, u32[]{:S(2)}) collective-permute-start(bf16[8,2,16,384]{3,2,1,0:T(8,128)(2,1)S(1)} %bitcast.24), channel_id=1, source_target_pairs={{0,2},{2,0},{1,3},{3,1},{4,6},{6,4},{5,7},{7,5},{8,10},{10,8},{9,1... | collective-permute-start | bytes 589832 | tf_op jit(solution)/shard_map/ppermute | solution.py:353
  50.7 9.4 %collective-permute-start.7 = (bf16[8,2,16,384]{3,2,1,0:T(8,128)(2,1)S(1)}, bf16[8,2,16,384]{3,2,1,0:T(8,128)(2,1)S(1)}, u32[]{:S(2)}, u32[]{:S(2)}) collective-permute-start(bf16[8,2,16,384]{3,2,1,0:T(8,128)(2,1)S(1)} %bitcast.23), channel_id=1, source_target_pairs={{0,2},{2,0},{1,3},{3,1},{4,6},{6,4},{5,7},{7,5},{8,10},{10,8},{9,1... | collective-permute-start | bytes 589832 | tf_op jit(solution)/shard_map/ppermute | solution.py:353
  61.1 29.2 %all-to-all-start = ((bf16[8,2,48,384]{3,2,1,0:T(8,128)(2,1)}), bf16[8,2,48,384]{3,2,1,0:T(8,128)(2,1)S(1)}, u32[]{:S(2)}, u32[]{:S(2)}) async-start(bf16[8,2,48,384]{3,2,1,0:T(8,128)(2,1)} %combine.1), calls=%async_computation | async-start | bytes 1179648 | tf_op jit(solution)/shard_map/all_to_all | solution.py:416
  65.6 7.4 %collective-permute-start.9 = (bf16[8,2,48,96]{3,2,1,0:T(8,128)(2,1)S(1)}, bf16[8,2,48,96]{3,2,1,0:T(8,128)(2,1)S(1)}, u32[]{:S(2)}, u32[]{:S(2)}) collective-permute-start(bf16[8,2,48,96]{3,2,1,0:T(8,128)(2,1)S(1)} %convert_element_type.9.own_ref), channel_id=1, source_target_pairs={{0,2},{2,0},{1,3},{3,1},{4,6},{6,4},{5,7},{7,5},{8,10},{10,8},{9,1... | collective-permute-start | bytes 442376 | tf_op jit(solution)/shard_map/ppermute | solution.py:353
  73.6 1.4 %collective-permute-start.10 = (bf16[4,1,2,48,96]{4,3,2,1,0:T(8,128)(2,1)S(1)}, bf16[4,1,2,48,96]{4,3,2,1,0:T(8,128)(2,1)S(1)}, u32[]{:S(2)}, u32[]{:S(2)}) collective-permute-start(bf16[4,1,2,48,96]{4,3,2,1,0:T(8,128)(2,1)S(1)} %get-tuple-element.38), channel_id=1, source_target_pairs={{0,1},{1,0},{2,3},{3,2},{4,5},{5,4},{6,7},{7,6},{8,9},{9,8},{10,11... | collective-permute-start | bytes 221192 | tf_op jit(solution)/shard_map/ppermute | solution.py:353
  75.6 7.0 %collective-permute-start.11 = (bf16[2,2,2,48,96]{4,3,2,1,0:T(8,128)(2,1)S(1)}, bf16[2,2,2,48,96]{4,3,2,1,0:T(8,128)(2,1)S(1)}, u32[]{:S(2)}, u32[]{:S(2)}) collective-permute-start(bf16[2,2,2,48,96]{4,3,2,1,0:T(8,128)(2,1)S(1)} %get-tuple-element.40), channel_id=1, source_target_pairs={{0,4},{4,0},{8,12},{12,8},{1,5},{5,1},{9,13},{13,9},{2,6},{6,2},{1... | collective-permute-start | bytes 221192 | tf_op jit(solution)/shard_map/ppermute | solution.py:464
  83.2 7.0 %collective-permute-start.12 = (bf16[1,4,2,48,96]{4,3,2,1,0:T(8,128)(2,1)S(1)}, bf16[1,4,2,48,96]{4,3,2,1,0:T(8,128)(2,1)S(1)}, u32[]{:S(2)}, u32[]{:S(2)}) collective-permute-start(bf16[1,4,2,48,96]{4,3,2,1,0:T(8,128)(2,1)S(1)} %get-tuple-element.42), channel_id=1, source_target_pairs={{0,8},{4,12},{8,0},{12,4},{1,9},{5,13},{9,1},{13,5},{2,10},{6,14},... | collective-permute-start | bytes 221192 | tf_op jit(solution)/shard_map/ppermute | solution.py:464

commit v4 on v3

--- a/solution.py
+++ b/solution.py
@@ -16,6 +16,8 @@
 LANES = 128
 TILE = 8
 SMALL = 8 << 20
+TINY = 2 << 20
+READ_LIMIT = 36 << 20
 VMEM = pltpu.VMEM
 
 
@@ -46,41 +48,42 @@
         theta_ref[w, 1] = (by_imag[:rows] + by_real[rows:]).astype(HALF)
 
 
-def fill_spread(place_ref, own_ref, received_ref, spread_ref):
+def fill_spread(place_ref, own_ref, received_ref, spread_ref, values_ref):
     count, half = own_ref.shape
     height = count * TILE
     wide = LANES * TILE
+    row = lax.broadcasted_iota(jnp.int32, (height, count), 0)
+    column = lax.broadcasted_iota(jnp.int32, (height, count), 1)
+    repeats = (row // TILE == column).astype(FULL).astype(HALF)
+    low = place_ref[1] == 0
+    own, received = own_ref[...].astype(FULL), received_ref[...].astype(FULL)
+    values_ref[:, :half] = dot(repeats, jnp.where(low, own, received).astype(HALF)).astype(HALF)
+    values_ref[:, half:] = dot(repeats, jnp.where(low, received, own).astype(HALF)).astype(HALF)
     row = lax.broadcasted_iota(jnp.int32, (LANES, wide), 0)
     column = lax.broadcasted_iota(jnp.int32, (LANES, wide), 1)
     copies = (column // TILE == row).astype(FULL).astype(HALF)
     a = lax.broadcasted_iota(jnp.int32, (height, wide), 0) % TILE
     b = lax.broadcasted_iota(jnp.int32, (height, wide), 1) % TILE
-    keep = a == b
-    row = lax.broadcasted_iota(jnp.int32, (height, count), 0)
-    column = lax.broadcasted_iota(jnp.int32, (height, count), 1)
-    repeats = (row // TILE == column).astype(FULL).astype(HALF)
-    low = place_ref[1] == 0
-    own, received = own_ref[...].astype(FULL), received_ref[...].astype(FULL)
-    for part, values in enumerate((jnp.where(low, own, received), jnp.where(low, received, own))):
-        values = dot(repeats, values.astype(HALF)).astype(HALF)
-        for block in range(half // LANES):
-            at = (part * half + block * LANES) * TILE
-            wider = dot(values[:, block * LANES : (block + 1) * LANES], copies)
-            spread_ref[:, at : at + wide] = jnp.where(keep, wider, 0.0).astype(HALF)
+
+    @pl.loop(0, 2 * half // LANES)
+    def _(block):
+        values = values_ref[:, pl.ds(pl.multiple_of(block * LANES, LANES), LANES)]
+        wider = jnp.where(a == b, dot(values, copies), 0.0).astype(HALF)
+        spread_ref[:, pl.ds(pl.multiple_of(block * wide, wide), wide)] = wider
 
 
 SCALARS = pl.BlockSpec(memory_space=pltpu.SMEM)
 ARRAY = pl.BlockSpec(memory_space=VMEM)
 
 
-def local_kernel(kernel, in_specs, out_shape, scratch_shapes=()):
+def local_kernel(kernel, in_specs, out_shape, scratch_shapes=(), limit=TINY):
     return pl.pallas_call(
         kernel,
         in_specs=in_specs,
         out_specs=jax.tree.map(lambda _: ARRAY, out_shape),
         out_shape=out_shape,
         scratch_shapes=list(scratch_shapes),
-        compiler_params=pltpu.CompilerParams(vmem_limit_bytes=SMALL),
+        compiler_params=pltpu.CompilerParams(vmem_limit_bytes=limit),
     )
 
 
@@ -112,7 +115,28 @@
             target_ref[t, senders:] = received_ref[2 * t + side]
 
 
-def bias_kernel(place_ref, own_ref, received_ref, vectors_ref, keep_ref, send_ref):
+def start_reading(pairs, semaphores):
+    copies = []
+    for source_ref, target_ref in pairs:
+        for block in range(target_ref.shape[0] // LANES):
+            group = pl.ds(block * LANES, LANES)
+            semaphore = semaphores.at[len(copies)]
+            copy = pltpu.make_async_copy(source_ref.at[group], target_ref.at[group], semaphore)
+            copy.start()
+            copies.append(copy)
+    return copies
+
+
+def unit_of(field_hbm, target_ref, unit):
+    height, tiles = target_ref.shape[:2]
+    rows = pl.ds(unit % 2 * height, height)
+    return field_hbm.at[rows, pl.ds(unit // 2 * tiles, tiles)], target_ref
+
+
+def bias_kernel(
+    place_ref, own_ref, received_ref, vectors_ref, field_hbm, keep_ref, send_ref, unit_ref, semaphores
+):
+    copies = start_reading([unit_of(field_hbm, unit_ref, 1)], semaphores)
     angles = jnp.concatenate([own_ref[...], received_ref[...]], 0)
     bias = dot(vectors_ref[...], angles, ((1,), (1,))).T
     half = bias.shape[1] // 2
@@ -120,16 +144,20 @@
     low = place_ref[1] == 0
     keep_ref[...] = jnp.where(low, first, second)
     send_ref[...] = jnp.where(low, second, first)
-
-
-def add_kernel(left_ref, right_ref, out_ref):
-    out_ref[...] = left_ref[...] + right_ref[...]
+    for copy in copies:
+        copy.wait()
+
+
+def add_kernel(left_ref, right_ref, out_ref, rounded_ref):
+    total = left_ref[...] + right_ref[...].astype(FULL)
+    out_ref[...] = total
+    rounded_ref[...] = total.astype(HALF)
 
 
 def coefficient_kernel(
     place_ref, source_ref, others_ref, left_ref, right_ref, samples_ref, out_ref, bias_ref, row_ref
 ):
-    bias_ref[...] = left_ref[...] + right_ref[...]
+    bias_ref[...] = left_ref[...] + right_ref[...].astype(FULL)
     count, half = bias_ref.shape
     lanes = pl.ds(pl.multiple_of(place_ref[1] * half, LANES), half)
     for i in range(count // 2):
@@ -140,72 +168,47 @@
     out_ref[...] = row_ref[...].astype(HALF)
 
 
-def read_kernel(half_hbm, field_hbm, half_ref, chunk_ref, semaphores):
-    tiles = chunk_ref.shape[1]
-    copies = []
-    for source_ref, target_ref in (
-        (half_hbm, half_ref),
-        (field_hbm.at[:, pl.ds(0, tiles)], chunk_ref),
-    ):
-        vectors = target_ref.shape[0]
-        for block in range(vectors // LANES):
-            group = pl.ds(block * LANES, LANES)
-            semaphore = semaphores.at[len(copies)]
-            copy = pltpu.make_async_copy(source_ref.at[group], target_ref.at[group], semaphore)
-            copy.start()
-            copies.append(copy)
-    for copy in copies:
+def read_kernel(half_hbm, field_hbm, half_ref, unit_ref, semaphores):
+    pairs = [(half_hbm, half_ref), unit_of(field_hbm, unit_ref, 0)]
+    for copy in start_reading(pairs, semaphores):
         copy.wait()
 
 
-def read_early(half_vectors, tiled_vectors, tiles):
-    vectors, _, _, orbitals = tiled_vectors.shape
-    chunk = jax.ShapeDtypeStruct((vectors, tiles, TILE, orbitals), HALF)
-    size = half_vectors.size + chunk.size
+def read_early(half_vectors, tiled_vectors, unit_shape):
     return pl.pallas_call(
         read_kernel,
-        in_specs=[pl.BlockSpec(memory_space=pltpu.HBM)] * 2,
-        out_specs=[pl.BlockSpec(memory_space=VMEM)] * 2,
-        out_shape=[VMEM(half_vectors.shape, HALF), VMEM(chunk.shape, HALF)],
-        scratch_shapes=[pltpu.SemaphoreType.DMA((2 * (vectors // LANES),))],
-        compiler_params=pltpu.CompilerParams(vmem_limit_bytes=36 << 20),
-        cost_estimate=pl.CostEstimate(flops=0, bytes_accessed=2 * size, transcendentals=0),
+        in_specs=[pl.BlockSpec(memory_space=pl.ANY)] * 2,
+        out_specs=[ARRAY] * 2,
+        out_shape=[jax.ShapeDtypeStruct(half_vectors.shape, HALF), unit_shape],
+        scratch_shapes=[
+            pltpu.SemaphoreType.DMA(((half_vectors.shape[0] + unit_shape.shape[0]) // LANES,))
+        ],
+        compiler_params=pltpu.CompilerParams(vmem_limit_bytes=READ_LIMIT),
         name="read",
     )(half_vectors, tiled_vectors)
 
 
-def field_kernel(part, parts, mine, *refs):
+def field_kernel(part, wanted, mine, *refs):
     refs = list(refs)
     left_refs = [refs.pop(0) for _ in range(3 if part == 0 else 1)]
-    chunk_ref, vectors_ref, own_ref, sent_ref = refs[:4]
-    refs = refs[4:]
+    unit_refs, field_hbm, own_ref, sent_ref = refs[:2], refs[2], refs[3], refs[4]
+    refs = refs[5:]
     spread_ref = refs.pop(0) if part == 0 else left_refs[0]
-    vectors, tiles, _, orbitals = chunk_ref.shape
+    values_ref = refs.pop() if part == 0 else None
+    copies = []
+    if wanted:
+        semaphores = refs.pop()
+        pairs = [unit_of(field_hbm, ref, unit) for ref, unit in zip(refs, wanted)]
+        copies = start_reading(pairs, semaphores)
+    if part == 0:
+        fill_spread(*left_refs, spread_ref, values_ref)
+    height, tiles, _, orbitals = unit_refs[0].shape
     count = spread_ref.shape[0] // TILE
-    copies = []
-    if part + 1 < parts:
-        next_ref, semaphores = refs
-        for block in range(vectors // LANES):
-            group = pl.ds(block * LANES, LANES)
-            copy = pltpu.make_async_copy(
-                vectors_ref.at[group, pl.ds((part + 1) * tiles, tiles)],
-                next_ref.at[group],
-                semaphores.at[block],
-            )
-            copy.start()
-            copies.append(copy)
-    if part == 0:
-        fill_spread(*left_refs, spread_ref)
-    group = min(vectors, 4 * LANES)
-    depth = group * TILE
+    depth = height * TILE
     total = None
-    for block in range(vectors // group):
+    for block, unit_ref in enumerate(unit_refs):
         right = jnp.concatenate(
-            [
-                chunk_ref[block * group : (block + 1) * group, t].reshape(depth, orbitals)
-                for t in range(tiles)
-            ],
-            1,
+            [unit_ref[:, t].reshape(depth, orbitals) for t in range(tiles)], 1
         )
         product = dot(spread_ref[:, block * depth : (block + 1) * depth], right)
         total = product if total is None else total + product
@@ -217,8 +220,9 @@
         copy.wait()
 
 
-def field_rows(left, chunk, tiled_vectors, part, parts, count, mine):
-    vectors, tiles, _, orbitals = chunk.shape
+def field_rows(left, units, tiled_vectors, part, wanted, count, mine):
+    height, tiles, _, orbitals = units[0].shape
+    vectors = 2 * height
     rows = tiles * TILE
     out_shape = [
         jax.ShapeDtypeStruct((mine, rows, orbitals), FULL),
@@ -226,14 +230,16 @@
     ]
     if part == 0:
         out_shape.append(jax.ShapeDtypeStruct((count * TILE, vectors * TILE), HALF))
+    out_shape += [jax.ShapeDtypeStruct(units[0].shape, HALF) for _ in wanted]
     scratch = []
-    if part + 1 < parts:
-        out_shape.append(jax.ShapeDtypeStruct(chunk.shape, HALF))
-        scratch.append(pltpu.SemaphoreType.DMA((vectors // LANES,)))
+    if wanted:
+        scratch.append(pltpu.SemaphoreType.DMA((len(wanted) * height // LANES,)))
+    if part == 0:
+        scratch.append(VMEM((count * TILE, vectors), HALF))
     left_specs = [SCALARS, ARRAY, ARRAY] if part == 0 else [ARRAY]
     own, sent, *rest = pl.pallas_call(
-        functools.partial(field_kernel, part, parts, mine),
-        in_specs=left_specs + [ARRAY, pl.BlockSpec(memory_space=pltpu.HBM)],
+        functools.partial(field_kernel, part, wanted, mine),
+        in_specs=left_specs + [ARRAY] * 2 + [pl.BlockSpec(memory_space=pltpu.HBM)],
         out_specs=[ARRAY] * len(out_shape),
         out_shape=out_shape,
         scratch_shapes=scratch,
@@ -244,9 +250,9 @@
             transcendentals=0,
         ),
         name="field",
-    )(*left, chunk, tiled_vectors)
+    )(*left, *units, tiled_vectors)
     left = [rest.pop(0)] if part == 0 else left
-    return own, sent, left, rest[0] if rest else None
+    return own, sent, left, rest
 
 
 def combine_kernel(chunks, *refs):
@@ -345,6 +351,7 @@
         [SCALARS] + [ARRAY] * (1 + len(starts)),
         jax.ShapeDtypeStruct((blocks, parts, rows, electrons), HALF),
         [VMEM((2 * orbitals, orbitals), HALF), VMEM((orbitals, 2 * wide), HALF)],
+        SMALL,
     )(rank, field, *starts)
 
 
@@ -427,7 +434,7 @@
     rank = lax.axis_index(ROWS).astype(jnp.int32).reshape(1)
     grid = walkers.reshape(local, 2, row_block, electrons)
     theta = local_kernel(
-        theta_kernel, [ARRAY] * 2, jax.ShapeDtypeStruct(grid.shape, HALF)
+        theta_kernel, [ARRAY] * 2, jax.ShapeDtypeStruct(grid.shape, HALF), limit=SMALL
     )(grid, correlation_inverse)
     theta = theta.reshape(local * 2, row_block * electrons)
     other_theta = others(theta)
@@ -436,13 +443,8 @@
 
     if fast:
         tiled_vectors = field_vectors.reshape(vectors, row_block // TILE, TILE, orbitals)
-        half_vectors, chunk = read_early(half_vectors, tiled_vectors, 2)
-        part_shape = jax.ShapeDtypeStruct((count, half), FULL)
-        bias, sent = local_kernel(
-            bias_kernel, [SCALARS] + [ARRAY] * 3, [part_shape] * 2
-        )(place, theta, other_theta, half_vectors)
-        received = shift(sent, "orb", 1)
-        add = local_kernel(add_kernel, [ARRAY] * 2, part_shape)
+        unit_shape = jax.ShapeDtypeStruct((half, 2, TILE, orbitals), HALF)
+        half_vectors, unit = read_early(half_vectors, tiled_vectors, unit_shape)
         block = (2, row_block, electrons)
         slots = jax.ShapeDtypeStruct((local // 2, 1) + block, HALF)
         keep, sent = local_kernel(
@@ -452,11 +454,23 @@
             [VMEM((population,) + block, HALF)],
         )(place, source, start, other_start)
         passed = shift(sent, "orb", 1)
+        part_shape = jax.ShapeDtypeStruct((count, half), FULL)
+        bias, sent, other_unit = local_kernel(
+            bias_kernel,
+            [SCALARS] + [ARRAY] * 3 + [pl.BlockSpec(memory_space=pltpu.HBM)],
+            [part_shape, part_shape, unit_shape],
+            [pltpu.SemaphoreType.DMA((half // LANES,))],
+            SMALL,
+        )(place, theta, other_theta, half_vectors, tiled_vectors)
+        units = [unit, other_unit]
+        received = shift(sent, "orb", 1)
+        rounded_shape = jax.ShapeDtypeStruct(part_shape.shape, HALF)
+        add = local_kernel(add_kernel, [ARRAY] * 2, [part_shape, rounded_shape])
         step = 1
         while step < chol:
             pairs = [(i, i ^ step) for i in range(chol)]
-            bias = add(bias, received)
-            received = lax.ppermute(bias, "chol", pairs)
+            bias, rounded = add(bias, received)
+            received = lax.ppermute(rounded, "chol", pairs)
             slots = jax.ShapeDtypeStruct((keep.shape[0] // 2, keep.shape[1] * 2) + block, HALF)
             keep, sent = local_kernel(
                 functools.partial(split_kernel, step), [SCALARS] + [ARRAY] * 2, [slots] * 2
@@ -475,9 +489,12 @@
         owns, received = [], []
         left = [place, coefficient, other_half]
         for part in range(parts):
-            own, sent, left, chunk = field_rows(
-                left, chunk, tiled_vectors, part, parts, count, local * 2
+            have = 2 * part + len(units)
+            wanted = range(have, max(have, min(2 * parts, 2 * part + 5)))
+            own, sent, left, further = field_rows(
+                left, units[:2], tiled_vectors, part, wanted, count, local * 2
             )
+            units = units[2:] + further
             owns.append(own.reshape(local, 2, rows, orbitals))
             sent = sent.reshape(population - local, 2, rows, orbitals)
             received += from_planes(sent)

time: 108 us -> 103 us (0.954)
  Pallas kernels: 36.7 us -> 32.9 us
    pallas_call x7, Pallas kernels: 28.5 us -> 24.8 us  [the longest x3 14.7 us: field_rows(): pl.pallas_call(functools.partial(field_kernel, part, wanted, mine), in_sp...]
  transfers between devices with their start and end apart: 14 -> 14, of which waited for: 10 -> 10; matrix products, arithmetic and copies ran while one was open for 0% -> 0% of each run, Pallas kernels for 17% -> 15%
where the time goes in v4:
time: 103 us
  waiting for transfers between devices  35 us (34%)
  Pallas kernels  32.9 us (32%)
  starting transfers between devices  18.9 us (18%)
  blocking collectives  12.1 us (12%)
  local copies, waits for them, and re-layouts  3.68 us (4%)
    ppermute x9, waiting for transfers between devices, shift(): lax.ppermute(value, axis, [(i, (i + step) % size) for i in range(size)])  21.5 us
    pallas_call x3, Pallas kernels, field_rows(): pl.pallas_call(functools.partial(field_kernel, part, wanted, mine), in_sp...  14.7 us
    all_to_all x1, blocking collectives, whole_step(): lax.all_to_all(normalized, ROWS, split_axis=0, concat_axis=0, tiled=True)  12.1 us
    ppermute x2, waiting for transfers between devices, whole_step(): passed = lax.ppermute(sent, 'chol', pairs)  11.2 us
    ppermute x9, starting transfers between devices, shift(): lax.ppermute(value, axis, [(i, (i + step) % size) for i in range(size)])  8.02 us
    pallas_call x1, Pallas kernels, read_early(): pl.pallas_call(read_kernel, in_specs=[pl.BlockSpec(memory_space=pl.ANY)]...  5.66 us
    pallas_call x1, Pallas kernels, whole_step(): local_kernel(bias_kernel, [SCALARS] + [ARRAY] * 3 + [pl.BlockSpec(memory_...  4.42 us
    ppermute x2, starting transfers between devices, whole_step(): received = lax.ppermute(rounded, 'chol', pairs)  4.3 us
  transfers between devices with their start and end apart: 14, of which 10 were waited for; matrix products, arithmetic and copies ran while one was open for 0% of the time, Pallas kernels for 15%

profile of v4, /device:TPU:0, one launch (start us, length us, event | category | flops | bytes accessed | tf_op | source)
XLA Modules:
  0.0 102.9 jit_solution(4879758372555505626)
XLA Ops:
  0.0 1.2 %reshape.34.grid_ref = f32[8,2,48,96]{3,2,1,0:T(8,128)S(1)} reshape(f32[8,2,4608]{2,1,0:T(2,128)} %param.6) | data formatting | bytes 589824 | tf_op jit(solution)/shard_map/reshape | solution.py:435
  1.3 1.1 %copy-done = f32[8,2,96,96]{3,2,1,0:T(8,128)S(1)} copy-done((f32[8,2,96,96]{3,2,1,0:T(8,128)S(1)}, f32[8,2,96,96]{3,2,1,0:T(8,128)}, u32[]{:S(2)}) %copy-start) | copy-done | bytes 589848
  2.4 0.5 shard_map.64
  2.8 0.2 reshape.35.own_ref
  3.1 3.0 %collective-permute-start.1 = (bf16[16,4608]{1,0:T(8,128)(2,1)S(1)}, bf16[16,4608]{1,0:T(8,128)(2,1)S(1)}, u32[]{:S(2)}, u32[]{:S(2)}) collective-permute-start(bf16[16,4608]{1,0:T(8,128)(2,1)S(1)} %reshape.35.own_ref), channel_id=1, source_target_pairs={{0,2},{2,0},{1,3},{3,1},{4,6},{6,4},{5,7},{7,5},{8,10},{10,8},{9,1... | collective-permute-start | bytes 442376 | tf_op jit(solution)/shard_map/ppermute | solution.py:360
  6.1 5.7 %read.1 = (bf16[1024,4608]{1,0:T(8,128)(2,1)S(1)}, bf16[512,2,8,384]{3,2,1,0:T(8,128)(2,1)S(1)}) custom-call(bf16[1024,4608]{1,0:T(8,128)(2,1)} %half_hbm.1, bf16[1024,6,8,384]{3,2,1,0:T(8,128)(2,1)} %bitcast.25), custom_call_target="tpu_custom_call" | custom-call | tf_op jit(solution)/shard_map/read/pallas_call | solution.py:178
  11.8 0.1 pad_add_fusion.place_ref.refs_0_
  11.8 0.0 collective-permute-done.1.received_ref
  11.8 4.4 %shard_map.65 = (f32[32,512]{1,0:T(8,128)S(1)}, f32[32,512]{1,0:T(8,128)S(1)}, bf16[512,2,8,384]{3,2,1,0:T(8,128)(2,1)S(1)}) custom-call(s32[3]{0:T(128)S(1)} %pad_add_fusion.place_ref.refs_0_, bf16[16,4608]{1,0:T(8,128)(2,1)S(1)} %reshape.35.own_ref, bf16[16,4608]{1,0:T(8,128)(2,1)S(1)} %collective-permute-done.1.received_ref, ...), custom_call_target="tpu_custom_call" | custom-call | tf_op jit(solution)/shard_map/pallas_call | solution.py:458
  16.3 0.1 collective-permute-start.2
  16.4 1.2 %collective-permute-done.2.right_ref = f32[32,512]{1,0:T(8,128)S(1)} collective-permute-done((f32[32,512]{1,0:T(8,128)S(1)}, f32[32,512]{1,0:T(8,128)S(1)}, u32[]{:S(2)}, u32[]{:S(2)}) %collective-permute-start.2) | collective-permute-done | bytes 65568 | tf_op jit(solution)/shard_map/ppermute | solution.py:360
  17.6 1.6 %collective-permute-start.3 = (bf16[32,512]{1,0:T(8,128)(2,1)S(1)}, bf16[32,512]{1,0:T(8,128)(2,1)S(1)}, u32[]{:S(2)}, u32[]{:S(2)}) collective-permute-start(bf16[32,512]{1,0:T(8,128)(2,1)S(1)} %get-tuple-element.35), channel_id=1, source_target_pairs={{0,4},{4,0},{8,12},{12,8},{1,5},{5,1},{9,13},{13,9},{2,6},{6,2},{1... | collective-permute-start | bytes 98312 | tf_op jit(solution)/shard_map/ppermute | solution.py:473
  19.3 2.3 %collective-permute-done.3.right_ref = bf16[32,512]{1,0:T(8,128)(2,1)S(1)} collective-permute-done((bf16[32,512]{1,0:T(8,128)(2,1)S(1)}, bf16[32,512]{1,0:T(8,128)(2,1)S(1)}, u32[]{:S(2)}, u32[]{:S(2)}) %collective-permute-start.3) | collective-permute-done | bytes 32800 | tf_op jit(solution)/shard_map/ppermute | solution.py:473
  21.6 2.7 %collective-permute-start.4 = (bf16[32,512]{1,0:T(8,128)(2,1)S(1)}, bf16[32,512]{1,0:T(8,128)(2,1)S(1)}, u32[]{:S(2)}, u32[]{:S(2)}) collective-permute-start(bf16[32,512]{1,0:T(8,128)(2,1)S(1)} %get-tuple-element.37), channel_id=1, source_target_pairs={{0,8},{4,12},{8,0},{12,4},{1,9},{5,13},{9,1},{13,5},{2,10},{6,14},... | collective-permute-start | bytes 98312 | tf_op jit(solution)/shard_map/ppermute | solution.py:473
  24.3 0.0 copy-done.2
  24.3 0.5 collective-permute-start
  24.8 3.0 %collective-permute-done.others_ref = s32[8]{0:T(128)S(1)} collective-permute-done((s32[8]{0:T(128)S(1)}, s32[8]{0:T(128)S(1)}, u32[]{:S(2)}, u32[]{:S(2)}) %collective-permute-start) | collective-permute-done | bytes 64 | tf_op jit(solution)/shard_map/ppermute | solution.py:360
  27.8 0.0 collective-permute-done.4.right_ref
  27.8 0.0 copy-done.1
  27.8 0.7 shard_map.68.refs_1_
  28.5 0.1 collective-permute-start.5
  28.6 1.2 %collective-permute-done.5.refs_2_ = bf16[32,512]{1,0:T(8,128)(2,1)S(1)} collective-permute-done((bf16[32,512]{1,0:T(8,128)(2,1)S(1)}, bf16[32,512]{1,0:T(8,128)(2,1)S(1)}, u32[]{:S(2)}, u32[]{:S(2)}) %collective-permute-start.5) | collective-permute-done | bytes 32800 | tf_op jit(solution)/shard_map/ppermute | solution.py:360
  29.8 7.2 %field.3 = (f32[16,16,384]{2,1,0:T(8,128)S(1)}, bf16[16,16,384]{2,1,0:T(8,128)(2,1)S(1)}, bf16[256,8192]{1,0:T(8,128)(2,1)S(1)}, bf16[512,2,8,384]{3,2,1,0:T(8,1...) custom-call(s32[3]{0:T(128)S(1)} %pad_add_fusion.place_ref.refs_0_, ...), custom_call_target="tpu_custom_call" | custom-call | flops 3221225472 | bytes 12582912 | tf_op jit(solution)/shard_map/field/pallas_call | solution.py:240
  36.9 0.6 collective-permute-start.6
  37.5 4.1 %field.4 = (f32[16,16,384]{2,1,0:T(8,128)S(1)}, bf16[16,16,384]{2,1,0:T(8,128)(2,1)S(1)}, bf16[512,2,8,384]{3,2,1,0:T(8,128)(2,1)S(1)}) custom-call(bf16[256,8192]{1,0:T(8,128)(2,1)S(1)} %get-tuple-element.41.refs_0_, bf16[512,2,8,384]{3,2,1,0:T(8,128)(2,1)S(1)} %get-tuple-element.42.refs_1_, bf16[512,2,8,384]{3,2,1,0:T(8,128)(2,1)S(1)} %get-tuple-element.43.refs_2_, ...), custom_call_target="tpu_custom_call" | custom-call | flops 3221225472 | bytes 12582912 | tf_op jit(solution)/shard_map/field/pallas_call | solution.py:240
  41.6 3.4 %field.5 = (f32[16,16,384]{2,1,0:T(8,128)S(1)}, bf16[16,16,384]{2,1,0:T(8,128)(2,1)S(1)}) custom-call(bf16[256,8192]{1,0:T(8,128)(2,1)S(1)} %get-tuple-element.41.refs_0_, bf16[512,2,8,384]{3,2,1,0:T(8,128)(2,1)S(1)} %get-tuple-element.45.refs_1_, bf16[512,2,8,384]{3,2,1,0:T(8,128)(2,1)S(1)} %get-tuple-element.46.refs_2_, bf16[1024,6,8,384]{3,2,1,0:T(8,128)(2,1)} %bitcast.29), custom_call_target="tpu_custom_call" | custom-call | flops 3221225472 | bytes 12582912 | tf_op jit(solution)/shard_map/field/pallas_call | solution.py:240
  45.1 1.6 %collective-permute-start.8 = (bf16[8,2,16,384]{3,2,1,0:T(8,128)(2,1)S(1)}, bf16[8,2,16,384]{3,2,1,0:T(8,128)(2,1)S(1)}, u32[]{:S(2)}, u32[]{:S(2)}) collective-permute-start(bf16[8,2,16,384]{3,2,1,0:T(8,128)(2,1)S(1)} %bitcast.24), channel_id=1, source_target_pairs={{0,2},{2,0},{1,3},{3,1},{4,6},{6,4},{5,7},{7,5},{8,10},{10,8},{9,1... | collective-permute-start | bytes 589832 | tf_op jit(solution)/shard_map/ppermute | solution.py:360
  46.6 0.5 collective-permute-start.7
  47.2 0.0 collective-permute-done.6.refs_3_
  47.2 5.7 %collective-permute-done.8.refs_5_ = bf16[8,2,16,384]{3,2,1,0:T(8,128)(2,1)S(1)} collective-permute-done((bf16[8,2,16,384]{3,2,1,0:T(8,128)(2,1)S(1)}, bf16[8,2,16,384]{3,2,1,0:T(8,128)(2,1)S(1)}, u32[]{:S(2)}, u32[]{:S(2)}) %collective-permute-start.8) | collective-permute-done | bytes 196640 | tf_op jit(solution)/shard_map/ppermute | solution.py:360
  52.9 3.1 %collective-permute-done.7.refs_4_ = bf16[8,2,16,384]{3,2,1,0:T(8,128)(2,1)S(1)} collective-permute-done((bf16[8,2,16,384]{3,2,1,0:T(8,128)(2,1)S(1)}, bf16[8,2,16,384]{3,2,1,0:T(8,128)(2,1)S(1)}, u32[]{:S(2)}, u32[]{:S(2)}) %collective-permute-start.7) | collective-permute-done | bytes 196640 | tf_op jit(solution)/shard_map/ppermute | solution.py:360
  56.0 1.0 combine.1
  57.0 3.8 %all-to-all-start = ((bf16[8,2,48,384]{3,2,1,0:T(8,128)(2,1)}), bf16[8,2,48,384]{3,2,1,0:T(8,128)(2,1)S(1)}, u32[]{:S(2)}, u32[]{:S(2)}) async-start(bf16[8,2,48,384]{3,2,1,0:T(8,128)(2,1)} %combine.1), calls=%async_computation | async-start | bytes 1179648 | tf_op jit(solution)/shard_map/all_to_all | solution.py:423
  60.8 1.6 %collective-permute-start.9 = (bf16[8,2,48,96]{3,2,1,0:T(8,128)(2,1)S(1)}, bf16[8,2,48,96]{3,2,1,0:T(8,128)(2,1)S(1)}, u32[]{:S(2)}, u32[]{:S(2)}) collective-permute-start(bf16[8,2,48,96]{3,2,1,0:T(8,128)(2,1)S(1)} %convert_element_type.9.own_ref), channel_id=1, source_target_pairs={{0,2},{2,0},{1,3},{3,1},{4,6},{6,4},{5,7},{7,5},{8,10},{10,8},{9,1... | collective-permute-start | bytes 442376 | tf_op jit(solution)/shard_map/ppermute | solution.py:360
  62.4 5.8 %collective-permute-done.9.received_ref = bf16[8,2,48,96]{3,2,1,0:T(8,128)(2,1)S(1)} collective-permute-done((bf16[8,2,48,96]{3,2,1,0:T(8,128)(2,1)S(1)}, bf16[8,2,48,96]{3,2,1,0:T(8,128)(2,1)S(1)}, u32[]{:S(2)}, u32[]{:S(2)}) %collective-permute-start.9) | collective-permute-done | bytes 147488 | tf_op jit(solution)/shard_map/ppermute | solution.py:360
  68.2 0.7 shard_map.69
  68.8 0.1 collective-permute-start.10
  68.9 1.3 %collective-permute-done.10.received_ref = bf16[4,1,2,48,96]{4,3,2,1,0:T(8,128)(2,1)S(1)} collective-permute-done((bf16[4,1,2,48,96]{4,3,2,1,0:T(8,128)(2,1)S(1)}, bf16[4,1,2,48,96]{4,3,2,1,0:T(8,128)(2,1)S(1)}, u32[]{:S(2)}, u32[]{:S(2)}) %collective-permute-start.10) | collective-permute-done | bytes 73760 | tf_op jit(solution)/shard_map/ppermute | solution.py:360
  70.2 0.6 shard_map.70
  70.8 1.7 %collective-permute-start.11 = (bf16[2,2,2,48,96]{4,3,2,1,0:T(8,128)(2,1)S(1)}, bf16[2,2,2,48,96]{4,3,2,1,0:T(8,128)(2,1)S(1)}, u32[]{:S(2)}, u32[]{:S(2)}) collective-permute-start(bf16[2,2,2,48,96]{4,3,2,1,0:T(8,128)(2,1)S(1)} %get-tuple-element.54), channel_id=1, source_target_pairs={{0,4},{4,0},{8,12},{12,8},{1,5},{5,1},{9,13},{13,9},{2,6},{6,2},{1... | collective-permute-start | bytes 221192 | tf_op jit(solution)/shard_map/ppermute | solution.py:478
  72.5 5.3 %collective-permute-done.11.received_ref = bf16[2,2,2,48,96]{4,3,2,1,0:T(8,128)(2,1)S(1)} collective-permute-done((bf16[2,2,2,48,96]{4,3,2,1,0:T(8,128)(2,1)S(1)}, bf16[2,2,2,48,96]{4,3,2,1,0:T(8,128)(2,1)S(1)}, u32[]{:S(2)}, u32[]{:S(2)}) %collective-permute-start.11) | collective-permute-done | bytes 73760 | tf_op jit(solution)/shard_map/ppermute | solution.py:478
  77.8 0.6 shard_map.71
  78.4 1.2 %collective-permute-start.12 = (bf16[1,4,2,48,96]{4,3,2,1,0:T(8,128)(2,1)S(1)}, bf16[1,4,2,48,96]{4,3,2,1,0:T(8,128)(2,1)S(1)}, u32[]{:S(2)}, u32[]{:S(2)}) collective-permute-start(bf16[1,4,2,48,96]{4,3,2,1,0:T(8,128)(2,1)S(1)} %get-tuple-element.56), channel_id=1, source_target_pairs={{0,8},{4,12},{8,0},{12,4},{1,9},{5,13},{9,1},{13,5},{2,10},{6,14},... | collective-permute-start | bytes 221192 | tf_op jit(solution)/shard_map/ppermute | solution.py:478
  79.6 5.9 %collective-permute-done.12 = bf16[1,4,2,48,96]{4,3,2,1,0:T(8,128)(2,1)S(1)} collective-permute-done((bf16[1,4,2,48,96]{4,3,2,1,0:T(8,128)(2,1)S(1)}, bf16[1,4,2,48,96]{4,3,2,1,0:T(8,128)(2,1)S(1)}, u32[]{:S(2)}, u32[]{:S(2)}) %collective-permute-start.12) | collective-permute-done | bytes 73760 | tf_op jit(solution)/shard_map/ppermute | solution.py:478
  85.5 0.0 all-to-all-done.field_piece_ref
  85.5 4.2 %shard_map.72 = bf16[8,2,48,96]{3,2,1,0:T(8,128)(2,1)S(1)} custom-call(s32[1]{0:T(128)} %bitcast.rank_ref, bf16[8,2,48,384]{3,2,1,0:T(8,128)(2,1)S(1)} %all-to-all-done.field_piece_ref, bf16[4,2,48,96]{3,2,1,0:T(8,128)(2,1)S(1)} %bitcast.20, bf16[4,2,48,96]{3,2,1,0:T(8,128)(2,1)S(1)} %bitcast.21), custom_call_target="tpu_custom_call" | custom-call | tf_op jit(solution)/shard_map/pallas_call | solution.py:349
  89.7 12.1 %all_to_all.10 = bf16[8,2,48,96]{3,2,1,0:T(8,128)(2,1)S(1)} all-to-all(bf16[8,2,48,96]{3,2,1,0:T(8,128)(2,1)S(1)} %shard_map.72), channel_id=1, replica_groups=mesh['groups'=2,'chol'=4,'walk'=2,'orb'=2] {'chol','orb'}, dimensions={0} | all-to-all | bytes 294912 | tf_op jit(solution)/shard_map/all_to_all | solution.py:538
  101.8 1.1 %reshape.43 = f32[8,2,4608]{2,1,0:T(2,128)} reshape(bf16[8,2,48,96]{3,2,1,0:T(8,128)(2,1)S(1)} %all_to_all.10) | data formatting | bytes 442368 | tf_op jit(solution)/shard_map/convert_element_type | solution.py:542
  (6 shorter events, 0.1 us)
Async XLA Ops:
  1.2 1.1 %copy-start = (f32[8,2,96,96]{3,2,1,0:T(8,128)S(1)}, f32[8,2,96,96]{3,2,1,0:T(8,128)}, u32[]{:S(2)}) copy-start(f32[8,2,96,96]{3,2,1,0:T(8,128)} %inverse_ref.1) | copy-start | bytes 1769476
  3.1 8.8 %collective-permute-start.1 = (bf16[16,4608]{1,0:T(8,128)(2,1)S(1)}, bf16[16,4608]{1,0:T(8,128)(2,1)S(1)}, u32[]{:S(2)}, u32[]{:S(2)}) collective-permute-start(bf16[16,4608]{1,0:T(8,128)(2,1)S(1)} %reshape.35.own_ref), channel_id=1, source_target_pairs={{0,2},{2,0},{1,3},{3,1},{4,6},{6,4},{5,7},{7,5},{8,10},{10,8},{9,1... | collective-permute-start | bytes 442376 | tf_op jit(solution)/shard_map/ppermute | solution.py:360
  11.8 12.4 %copy-start.2 = (s32[8]{0:T(128)S(1)}, s32[8]{0:T(128)}, u32[]{:S(2)}) copy-start(s32[8]{0:T(128)} %source_ref.3) | copy-start | bytes 100
  11.8 16.0 %copy-start.1 = (f32[16,1024]{1,0:T(8,128)S(1)}, f32[16,1024]{1,0:T(8,128)}, u32[]{:S(2)}) copy-start(f32[16,1024]{1,0:T(8,128)} %samples_ref.1) | copy-start | bytes 196612
  16.3 1.3 %collective-permute-start.2 = (f32[32,512]{1,0:T(8,128)S(1)}, f32[32,512]{1,0:T(8,128)S(1)}, u32[]{:S(2)}, u32[]{:S(2)}) collective-permute-start(f32[32,512]{1,0:T(8,128)S(1)} %get-tuple-element.33), channel_id=1, source_target_pairs={{0,1},{1,0},{2,3},{3,2},{4,5},{5,4},{6,7},{7,6},{8,9},{9,8},{10,11... | collective-permute-start | bytes 196616 | tf_op jit(solution)/shard_map/ppermute | solution.py:360
  17.6 4.0 %collective-permute-start.3 = (bf16[32,512]{1,0:T(8,128)(2,1)S(1)}, bf16[32,512]{1,0:T(8,128)(2,1)S(1)}, u32[]{:S(2)}, u32[]{:S(2)}) collective-permute-start(bf16[32,512]{1,0:T(8,128)(2,1)S(1)} %get-tuple-element.35), channel_id=1, source_target_pairs={{0,4},{4,0},{8,12},{12,8},{1,5},{5,1},{9,13},{13,9},{2,6},{6,2},{1... | collective-permute-start | bytes 98312 | tf_op jit(solution)/shard_map/ppermute | solution.py:473
  21.6 6.2 %collective-permute-start.4 = (bf16[32,512]{1,0:T(8,128)(2,1)S(1)}, bf16[32,512]{1,0:T(8,128)(2,1)S(1)}, u32[]{:S(2)}, u32[]{:S(2)}) collective-permute-start(bf16[32,512]{1,0:T(8,128)(2,1)S(1)} %get-tuple-element.37), channel_id=1, source_target_pairs={{0,8},{4,12},{8,0},{12,4},{1,9},{5,13},{9,1},{13,5},{2,10},{6,14},... | collective-permute-start | bytes 98312 | tf_op jit(solution)/shard_map/ppermute | solution.py:473
  24.3 3.6 %collective-permute-start = (s32[8]{0:T(128)S(1)}, s32[8]{0:T(128)S(1)}, u32[]{:S(2)}, u32[]{:S(2)}) collective-permute-start(s32[8]{0:T(128)S(1)} %copy-done.2), channel_id=1, source_target_pairs={{0,2},{2,0},{1,3},{3,1},{4,6},{6,4},{5,7},{7,5},{8,10},{10,8},{9,1... | collective-permute-start | bytes 104 | tf_op jit(solution)/shard_map/ppermute | solution.py:360
  28.5 1.3 %collective-permute-start.5 = (bf16[32,512]{1,0:T(8,128)(2,1)S(1)}, bf16[32,512]{1,0:T(8,128)(2,1)S(1)}, u32[]{:S(2)}, u32[]{:S(2)}) collective-permute-start(bf16[32,512]{1,0:T(8,128)(2,1)S(1)} %shard_map.68.refs_1_), channel_id=1, source_target_pairs={{0,1},{1,0},{2,3},{3,2},{4,5},{5,4},{6,7},{7,6},{8,9},{9,8},{10,11... | collective-permute-start | bytes 98312 | tf_op jit(solution)/shard_map/ppermute | solution.py:360
  36.9 10.2 %collective-permute-start.6 = (bf16[8,2,16,384]{3,2,1,0:T(8,128)(2,1)S(1)}, bf16[8,2,16,384]{3,2,1,0:T(8,128)(2,1)S(1)}, u32[]{:S(2)}, u32[]{:S(2)}) collective-permute-start(bf16[8,2,16,384]{3,2,1,0:T(8,128)(2,1)S(1)} %bitcast.22), channel_id=1, source_target_pairs={{0,2},{2,0},{1,3},{3,1},{4,6},{6,4},{5,7},{7,5},{8,10},{10,8},{9,1... | collective-permute-start | bytes 589832 | tf_op jit(solution)/shard_map/ppermute | solution.py:360
  45.1 7.8 %collective-permute-start.8 = (bf16[8,2,16,384]{3,2,1,0:T(8,128)(2,1)S(1)}, bf16[8,2,16,384]{3,2,1,0:T(8,128)(2,1)S(1)}, u32[]{:S(2)}, u32[]{:S(2)}) collective-permute-start(bf16[8,2,16,384]{3,2,1,0:T(8,128)(2,1)S(1)} %bitcast.24), channel_id=1, source_target_pairs={{0,2},{2,0},{1,3},{3,1},{4,6},{6,4},{5,7},{7,5},{8,10},{10,8},{9,1... | collective-permute-start | bytes 589832 | tf_op jit(solution)/shard_map/ppermute | solution.py:360
  46.6 9.4 %collective-permute-start.7 = (bf16[8,2,16,384]{3,2,1,0:T(8,128)(2,1)S(1)}, bf16[8,2,16,384]{3,2,1,0:T(8,128)(2,1)S(1)}, u32[]{:S(2)}, u32[]{:S(2)}) collective-permute-start(bf16[8,2,16,384]{3,2,1,0:T(8,128)(2,1)S(1)} %bitcast.23), channel_id=1, source_target_pairs={{0,2},{2,0},{1,3},{3,1},{4,6},{6,4},{5,7},{7,5},{8,10},{10,8},{9,1... | collective-permute-start | bytes 589832 | tf_op jit(solution)/shard_map/ppermute | solution.py:360
  57.0 28.5 %all-to-all-start = ((bf16[8,2,48,384]{3,2,1,0:T(8,128)(2,1)}), bf16[8,2,48,384]{3,2,1,0:T(8,128)(2,1)S(1)}, u32[]{:S(2)}, u32[]{:S(2)}) async-start(bf16[8,2,48,384]{3,2,1,0:T(8,128)(2,1)} %combine.1), calls=%async_computation | async-start | bytes 1179648 | tf_op jit(solution)/shard_map/all_to_all | solution.py:423
  60.8 7.4 %collective-permute-start.9 = (bf16[8,2,48,96]{3,2,1,0:T(8,128)(2,1)S(1)}, bf16[8,2,48,96]{3,2,1,0:T(8,128)(2,1)S(1)}, u32[]{:S(2)}, u32[]{:S(2)}) collective-permute-start(bf16[8,2,48,96]{3,2,1,0:T(8,128)(2,1)S(1)} %convert_element_type.9.own_ref), channel_id=1, source_target_pairs={{0,2},{2,0},{1,3},{3,1},{4,6},{6,4},{5,7},{7,5},{8,10},{10,8},{9,1... | collective-permute-start | bytes 442376 | tf_op jit(solution)/shard_map/ppermute | solution.py:360
  68.8 1.4 %collective-permute-start.10 = (bf16[4,1,2,48,96]{4,3,2,1,0:T(8,128)(2,1)S(1)}, bf16[4,1,2,48,96]{4,3,2,1,0:T(8,128)(2,1)S(1)}, u32[]{:S(2)}, u32[]{:S(2)}) collective-permute-start(bf16[4,1,2,48,96]{4,3,2,1,0:T(8,128)(2,1)S(1)} %get-tuple-element.52), channel_id=1, source_target_pairs={{0,1},{1,0},{2,3},{3,2},{4,5},{5,4},{6,7},{7,6},{8,9},{9,8},{10,11... | collective-permute-start | bytes 221192 | tf_op jit(solution)/shard_map/ppermute | solution.py:360
  70.8 7.0 %collective-permute-start.11 = (bf16[2,2,2,48,96]{4,3,2,1,0:T(8,128)(2,1)S(1)}, bf16[2,2,2,48,96]{4,3,2,1,0:T(8,128)(2,1)S(1)}, u32[]{:S(2)}, u32[]{:S(2)}) collective-permute-start(bf16[2,2,2,48,96]{4,3,2,1,0:T(8,128)(2,1)S(1)} %get-tuple-element.54), channel_id=1, source_target_pairs={{0,4},{4,0},{8,12},{12,8},{1,5},{5,1},{9,13},{13,9},{2,6},{6,2},{1... | collective-permute-start | bytes 221192 | tf_op jit(solution)/shard_map/ppermute | solution.py:478
  78.4 7.0 %collective-permute-start.12 = (bf16[1,4,2,48,96]{4,3,2,1,0:T(8,128)(2,1)S(1)}, bf16[1,4,2,48,96]{4,3,2,1,0:T(8,128)(2,1)S(1)}, u32[]{:S(2)}, u32[]{:S(2)}) collective-permute-start(bf16[1,4,2,48,96]{4,3,2,1,0:T(8,128)(2,1)S(1)} %get-tuple-element.56), channel_id=1, source_target_pairs={{0,8},{4,12},{8,0},{12,4},{1,9},{5,13},{9,1},{13,5},{2,10},{6,14},... | collective-permute-start | bytes 221192 | tf_op jit(solution)/shard_map/ppermute | solution.py:478

commit v5 on v4

--- a/solution.py
+++ b/solution.py
@@ -62,14 +62,16 @@
     row = lax.broadcasted_iota(jnp.int32, (LANES, wide), 0)
     column = lax.broadcasted_iota(jnp.int32, (LANES, wide), 1)
     copies = (column // TILE == row).astype(FULL).astype(HALF)
-    a = lax.broadcasted_iota(jnp.int32, (height, wide), 0) % TILE
-    b = lax.broadcasted_iota(jnp.int32, (height, wide), 1) % TILE
+    a = lax.broadcasted_iota(jnp.int32, (TILE, wide), 0)
+    b = lax.broadcasted_iota(jnp.int32, (TILE, wide), 1) % TILE
+    keep = a == b
 
     @pl.loop(0, 2 * half // LANES)
     def _(block):
         values = values_ref[:, pl.ds(pl.multiple_of(block * LANES, LANES), LANES)]
-        wider = jnp.where(a == b, dot(values, copies), 0.0).astype(HALF)
-        spread_ref[:, pl.ds(pl.multiple_of(block * wide, wide), wide)] = wider
+        wider = dot(values, copies).reshape(count, TILE, wide)
+        wider = jnp.where(keep[None], wider, 0.0).reshape(height, wide)
+        spread_ref[:, pl.ds(pl.multiple_of(block * wide, wide), wide)] = wider.astype(HALF)
 
 
 SCALARS = pl.BlockSpec(memory_space=pltpu.SMEM)
@@ -133,10 +135,7 @@
     return field_hbm.at[rows, pl.ds(unit // 2 * tiles, tiles)], target_ref
 
 
-def bias_kernel(
-    place_ref, own_ref, received_ref, vectors_ref, field_hbm, keep_ref, send_ref, unit_ref, semaphores
-):
-    copies = start_reading([unit_of(field_hbm, unit_ref, 1)], semaphores)
+def bias_kernel(place_ref, own_ref, received_ref, vectors_ref, keep_ref, send_ref):
     angles = jnp.concatenate([own_ref[...], received_ref[...]], 0)
     bias = dot(vectors_ref[...], angles, ((1,), (1,))).T
     half = bias.shape[1] // 2
@@ -144,7 +143,10 @@
     low = place_ref[1] == 0
     keep_ref[...] = jnp.where(low, first, second)
     send_ref[...] = jnp.where(low, second, first)
-    for copy in copies:
+
+
+def late_kernel(order_ref, field_hbm, unit_ref, semaphores):
+    for copy in start_reading([unit_of(field_hbm, unit_ref, 1)], semaphores):
         copy.wait()
 
 
@@ -279,15 +281,12 @@
     )(*owns, *received)
 
 
-def walker_kernel(count, orbitals, electrons, rank_ref, field_piece_ref, *refs):
+def walker_kernel(count, orbitals, electrons, rank_ref, field_ref, *refs):
     start_refs = refs[:count]
-    out_ref, field_ref, start_wide_ref = refs[count:]
-    blocks, _, rows, _ = field_piece_ref.shape
+    out_ref, start_wide_ref = refs[count:]
+    blocks, _, rows, _ = field_ref.shape
     wide = start_wide_ref.shape[1] // 2
     start_wide_ref[...] = jnp.zeros_like(start_wide_ref)
-    for r in range(blocks):
-        for c in range(2):
-            field_ref[pl.ds(c * orbitals + r * rows, rows)] = field_piece_ref[r, c]
     block = 0
     for start_ref in start_refs:
         for d in range(start_ref.shape[0]):
@@ -298,8 +297,10 @@
     current = start_wide_ref[...]
     summed = current.astype(FULL)
     for order in range(1, TERMS + 1):
-        product = dot(field_ref[...], current)
-        top, low = product[:orbitals], product[orbitals:]
+        product = dot(field_ref[...].reshape(2 * orbitals, orbitals), current)
+        product = product.reshape(blocks, 2, rows, 2 * wide)
+        top = product[:, 0].reshape(orbitals, 2 * wide)
+        low = product[:, 1].reshape(orbitals, 2 * wide)
         following = jnp.concatenate(
             [top[:, :wide] - low[:, wide:], top[:, wide:] + low[:, :wide]], 1
         )
@@ -307,9 +308,8 @@
         summed = summed + following
         current = following.astype(HALF)
 
-    high, low = split_half(summed)
-    rows_first = ((0,), (0,))
-    gram = dot(high, high, rows_first) + dot(high, low, rows_first) + dot(low, high, rows_first)
+    rounded = summed.astype(HALF)
+    gram = dot(rounded, rounded, ((0,), (0,)))
     gram_real = (gram[:wide, :wide] + gram[wide:, wide:]) * (1.0 / orbitals)
     gram_imag = (gram[:wide, wide:] - gram[wide:, :wide]) * (1.0 / orbitals)
     row = lax.broadcasted_iota(jnp.int32, (wide, wide), 0)
@@ -333,7 +333,7 @@
         root = step if root is None else times(step, root)
     inverse = lax.rsqrt(scale)
     root = jnp.concatenate([root[0] * inverse, root[1] * inverse], 1)
-    product = fine_dot(jnp.concatenate([summed[:, :wide], summed[:, wide:]], 0), root)
+    product = dot(jnp.concatenate([rounded[:, :wide], rounded[:, wide:]], 0), root.astype(HALF))
     top, low = product[:orbitals], product[orbitals:]
     real = (top[:, :wide] - low[:, wide:]).astype(HALF)
     imag = (top[:, wide:] + low[:, :wide]).astype(HALF)
@@ -350,7 +350,7 @@
         functools.partial(walker_kernel, len(starts), orbitals, electrons),
         [SCALARS] + [ARRAY] * (1 + len(starts)),
         jax.ShapeDtypeStruct((blocks, parts, rows, electrons), HALF),
-        [VMEM((2 * orbitals, orbitals), HALF), VMEM((orbitals, 2 * wide), HALF)],
+        [VMEM((orbitals, 2 * wide), HALF)],
         SMALL,
     )(rank, field, *starts)
 
@@ -455,14 +455,10 @@
         )(place, source, start, other_start)
         passed = shift(sent, "orb", 1)
         part_shape = jax.ShapeDtypeStruct((count, half), FULL)
-        bias, sent, other_unit = local_kernel(
-            bias_kernel,
-            [SCALARS] + [ARRAY] * 3 + [pl.BlockSpec(memory_space=pltpu.HBM)],
-            [part_shape, part_shape, unit_shape],
-            [pltpu.SemaphoreType.DMA((half // LANES,))],
-            SMALL,
-        )(place, theta, other_theta, half_vectors, tiled_vectors)
-        units = [unit, other_unit]
+        bias, sent = local_kernel(
+            bias_kernel, [SCALARS] + [ARRAY] * 3, [part_shape, part_shape], limit=SMALL
+        )(place, theta, other_theta, half_vectors)
+        hbm = pl.BlockSpec(memory_space=pltpu.HBM)
         received = shift(sent, "orb", 1)
         rounded_shape = jax.ShapeDtypeStruct(part_shape.shape, HALF)
         add = local_kernel(add_kernel, [ARRAY] * 2, [part_shape, rounded_shape])
@@ -477,6 +473,14 @@
             )(place, keep, passed)
             passed = lax.ppermute(sent, "chol", pairs)
             step *= 2
+        other_unit = local_kernel(
+            late_kernel,
+            [hbm, hbm],
+            unit_shape,
+            [pltpu.SemaphoreType.DMA((half // LANES,))],
+            3 * SMALL,
+        )(bias, tiled_vectors)
+        units = [unit, other_unit]
         coefficient = local_kernel(
             coefficient_kernel,
             [SCALARS] * 3 + [ARRAY] * 3,

time: 103 us -> 103 us (level)
    pallas_call x1 -> x2, Pallas kernels: 4.42 us -> 6.04 us  [the longest x1 3.14 us: whole_step(): local_kernel(bias_kernel, [SCALARS] + [ARRAY] * 3, [part_shape, part_shap...]
  transfers between devices with their start and end apart: 14 -> 14, of which waited for: 10 -> 9; matrix products, arithmetic and copies ran while one was open for 0% -> 0% of each run, Pallas kernels for 15% -> 17%
where the time goes in v5:
time: 103 us
  waiting for transfers between devices  34.2 us (33%)
  Pallas kernels  33.9 us (33%)
  starting transfers between devices  18.9 us (18%)
  blocking collectives  12.1 us (12%)
  local copies, waits for them, and re-layouts  3.69 us (4%)
    ppermute x9, waiting for transfers between devices, shift(): lax.ppermute(value, axis, [(i, (i + step) % size) for i in range(size)])  20.6 us
    pallas_call x3, Pallas kernels, field_rows(): pl.pallas_call(functools.partial(field_kernel, part, wanted, mine), in_sp...  14.7 us
    all_to_all x1, blocking collectives, whole_step(): lax.all_to_all(normalized, ROWS, split_axis=0, concat_axis=0, tiled=True)  12.1 us
    ppermute x2, waiting for transfers between devices, whole_step(): passed = lax.ppermute(sent, 'chol', pairs)  11.2 us
    ppermute x9, starting transfers between devices, shift(): lax.ppermute(value, axis, [(i, (i + step) % size) for i in range(size)])  8 us
    pallas_call x1, Pallas kernels, read_early(): pl.pallas_call(read_kernel, in_specs=[pl.BlockSpec(memory_space=pl.ANY)]...  5.66 us
    ppermute x2, starting transfers between devices, whole_step(): received = lax.ppermute(rounded, 'chol', pairs)  4.3 us
    all_to_all x1, starting transfers between devices, to_owners(): return lax.all_to_all(value, ROWS, split_axis=0, concat_axis=0, tiled=True)  3.76 us
  transfers between devices with their start and end apart: 14, of which 9 were waited for; matrix products, arithmetic and copies ran while one was open for 0% of the time, Pallas kernels for 17%

profile of v5, /device:TPU:0, one launch (start us, length us, event | category | flops | bytes accessed | tf_op | source)
XLA Modules:
  0.0 103.0 jit_solution(10602791791069453369)
XLA Ops:
  0.0 1.2 %reshape.34.grid_ref = f32[8,2,48,96]{3,2,1,0:T(8,128)S(1)} reshape(f32[8,2,4608]{2,1,0:T(2,128)} %param.6) | data formatting | bytes 589824 | tf_op jit(solution)/shard_map/reshape | solution.py:435
  1.3 1.1 %copy-done = f32[8,2,96,96]{3,2,1,0:T(8,128)S(1)} copy-done((f32[8,2,96,96]{3,2,1,0:T(8,128)S(1)}, f32[8,2,96,96]{3,2,1,0:T(8,128)}, u32[]{:S(2)}) %copy-start) | copy-done | bytes 589848
  2.4 0.5 shard_map.64
  2.8 0.2 reshape.35.own_ref
  3.1 3.0 %collective-permute-start.1 = (bf16[16,4608]{1,0:T(8,128)(2,1)S(1)}, bf16[16,4608]{1,0:T(8,128)(2,1)S(1)}, u32[]{:S(2)}, u32[]{:S(2)}) collective-permute-start(bf16[16,4608]{1,0:T(8,128)(2,1)S(1)} %reshape.35.own_ref), channel_id=1, source_target_pairs={{0,2},{2,0},{1,3},{3,1},{4,6},{6,4},{5,7},{7,5},{8,10},{10,8},{9,1... | collective-permute-start | bytes 442376 | tf_op jit(solution)/shard_map/ppermute | solution.py:360
  6.1 5.7 %read.1 = (bf16[1024,4608]{1,0:T(8,128)(2,1)S(1)}, bf16[512,2,8,384]{3,2,1,0:T(8,128)(2,1)S(1)}) custom-call(bf16[1024,4608]{1,0:T(8,128)(2,1)} %half_hbm.1, bf16[1024,6,8,384]{3,2,1,0:T(8,128)(2,1)} %bitcast.25), custom_call_target="tpu_custom_call" | custom-call | tf_op jit(solution)/shard_map/read/pallas_call | solution.py:180
  11.8 0.0 copy-start.2
  11.8 0.0 copy-start.1
  11.8 0.1 pad_add_fusion.place_ref.refs_0_
  11.9 0.0 collective-permute-done.1.received_ref
  11.9 3.1 %shard_map.65 = (f32[32,512]{1,0:T(8,128)S(1)}, f32[32,512]{1,0:T(8,128)S(1)}) custom-call(s32[3]{0:T(128)S(1)} %pad_add_fusion.place_ref.refs_0_, bf16[16,4608]{1,0:T(8,128)(2,1)S(1)} %reshape.35.own_ref, bf16[16,4608]{1,0:T(8,128)(2,1)S(1)} %collective-permute-done.1.received_ref, bf16[1024,4608]{1,0:T(8,128)(2,1)S(1)} %get-tuple-element.30.vectors_ref), custom_call_target="tpu_custom_call" | custom-call | tf_op jit(solution)/shard_map/pallas_call | solution.py:458
  15.0 0.1 collective-permute-start.2
  15.1 1.2 %collective-permute-done.2.right_ref = f32[32,512]{1,0:T(8,128)S(1)} collective-permute-done((f32[32,512]{1,0:T(8,128)S(1)}, f32[32,512]{1,0:T(8,128)S(1)}, u32[]{:S(2)}, u32[]{:S(2)}) %collective-permute-start.2) | collective-permute-done | bytes 65568 | tf_op jit(solution)/shard_map/ppermute | solution.py:360
  16.3 1.6 %collective-permute-start.3 = (bf16[32,512]{1,0:T(8,128)(2,1)S(1)}, bf16[32,512]{1,0:T(8,128)(2,1)S(1)}, u32[]{:S(2)}, u32[]{:S(2)}) collective-permute-start(bf16[32,512]{1,0:T(8,128)(2,1)S(1)} %get-tuple-element.34), channel_id=1, source_target_pairs={{0,4},{4,0},{8,12},{12,8},{1,5},{5,1},{9,13},{13,9},{2,6},{6,2},{1... | collective-permute-start | bytes 98312 | tf_op jit(solution)/shard_map/ppermute | solution.py:469
  18.0 2.3 %collective-permute-done.3.right_ref = bf16[32,512]{1,0:T(8,128)(2,1)S(1)} collective-permute-done((bf16[32,512]{1,0:T(8,128)(2,1)S(1)}, bf16[32,512]{1,0:T(8,128)(2,1)S(1)}, u32[]{:S(2)}, u32[]{:S(2)}) %collective-permute-start.3) | collective-permute-done | bytes 32800 | tf_op jit(solution)/shard_map/ppermute | solution.py:469
  20.3 2.7 %collective-permute-start.4 = (bf16[32,512]{1,0:T(8,128)(2,1)S(1)}, bf16[32,512]{1,0:T(8,128)(2,1)S(1)}, u32[]{:S(2)}, u32[]{:S(2)}) collective-permute-start(bf16[32,512]{1,0:T(8,128)(2,1)S(1)} %get-tuple-element.36), channel_id=1, source_target_pairs={{0,8},{4,12},{8,0},{12,4},{1,9},{5,13},{9,1},{13,5},{2,10},{6,14},... | collective-permute-start | bytes 98312 | tf_op jit(solution)/shard_map/ppermute | solution.py:469
  23.0 0.5 collective-permute-start
  23.5 3.0 %collective-permute-done.others_ref = s32[8]{0:T(128)S(1)} collective-permute-done((s32[8]{0:T(128)S(1)}, s32[8]{0:T(128)S(1)}, u32[]{:S(2)}, u32[]{:S(2)}) %collective-permute-start) | collective-permute-done | bytes 64 | tf_op jit(solution)/shard_map/ppermute | solution.py:360
  26.5 0.0 collective-permute-done.4.right_ref
  26.6 0.7 shard_map.68.refs_1_
  27.2 0.1 collective-permute-start.5
  27.3 2.9 %shard_map.69.refs_4_ = bf16[512,2,8,384]{3,2,1,0:T(8,128)(2,1)S(1)} custom-call(f32[32,512]{1,0:T(8,128)S(1)} %get-tuple-element.35.left_ref.order_ref, bf16[1024,6,8,384]{3,2,1,0:T(8,128)(2,1)} %bitcast.26), custom_call_target="tpu_custom_call" | custom-call | tf_op jit(solution)/shard_map/pallas_call | solution.py:476
  30.2 0.0 collective-permute-done.5.refs_2_
  30.2 7.2 %field.3 = (f32[16,16,384]{2,1,0:T(8,128)S(1)}, bf16[16,16,384]{2,1,0:T(8,128)(2,1)S(1)}, bf16[256,8192]{1,0:T(8,128)(2,1)S(1)}, bf16[512,2,8,384]{3,2,1,0:T(8,1...) custom-call(s32[3]{0:T(128)S(1)} %pad_add_fusion.place_ref.refs_0_, ...), custom_call_target="tpu_custom_call" | custom-call | flops 3221225472 | bytes 12582912 | tf_op jit(solution)/shard_map/field/pallas_call | solution.py:242
  37.4 0.6 collective-permute-start.6
  38.0 4.1 %field.4 = (f32[16,16,384]{2,1,0:T(8,128)S(1)}, bf16[16,16,384]{2,1,0:T(8,128)(2,1)S(1)}, bf16[512,2,8,384]{3,2,1,0:T(8,128)(2,1)S(1)}) custom-call(bf16[256,8192]{1,0:T(8,128)(2,1)S(1)} %get-tuple-element.39.refs_0_, bf16[512,2,8,384]{3,2,1,0:T(8,128)(2,1)S(1)} %get-tuple-element.40.refs_1_, bf16[512,2,8,384]{3,2,1,0:T(8,128)(2,1)S(1)} %get-tuple-element.41.refs_2_, ...), custom_call_target="tpu_custom_call" | custom-call | flops 3221225472 | bytes 12582912 | tf_op jit(solution)/shard_map/field/pallas_call | solution.py:242
  42.0 3.4 %field.5 = (f32[16,16,384]{2,1,0:T(8,128)S(1)}, bf16[16,16,384]{2,1,0:T(8,128)(2,1)S(1)}) custom-call(bf16[256,8192]{1,0:T(8,128)(2,1)S(1)} %get-tuple-element.39.refs_0_, bf16[512,2,8,384]{3,2,1,0:T(8,128)(2,1)S(1)} %get-tuple-element.43.refs_1_, bf16[512,2,8,384]{3,2,1,0:T(8,128)(2,1)S(1)} %get-tuple-element.44.refs_2_, bf16[1024,6,8,384]{3,2,1,0:T(8,128)(2,1)} %bitcast.29), custom_call_target="tpu_custom_call" | custom-call | flops 3221225472 | bytes 12582912 | tf_op jit(solution)/shard_map/field/pallas_call | solution.py:242
  45.5 1.6 %collective-permute-start.8 = (bf16[8,2,16,384]{3,2,1,0:T(8,128)(2,1)S(1)}, bf16[8,2,16,384]{3,2,1,0:T(8,128)(2,1)S(1)}, u32[]{:S(2)}, u32[]{:S(2)}) collective-permute-start(bf16[8,2,16,384]{3,2,1,0:T(8,128)(2,1)S(1)} %bitcast.24), channel_id=1, source_target_pairs={{0,2},{2,0},{1,3},{3,1},{4,6},{6,4},{5,7},{7,5},{8,10},{10,8},{9,1... | collective-permute-start | bytes 589832 | tf_op jit(solution)/shard_map/ppermute | solution.py:360
  47.1 0.5 collective-permute-start.7
  47.6 0.0 collective-permute-done.6.refs_3_
  47.6 5.7 %collective-permute-done.8.refs_5_ = bf16[8,2,16,384]{3,2,1,0:T(8,128)(2,1)S(1)} collective-permute-done((bf16[8,2,16,384]{3,2,1,0:T(8,128)(2,1)S(1)}, bf16[8,2,16,384]{3,2,1,0:T(8,128)(2,1)S(1)}, u32[]{:S(2)}, u32[]{:S(2)}) %collective-permute-start.8) | collective-permute-done | bytes 196640 | tf_op jit(solution)/shard_map/ppermute | solution.py:360
  53.3 3.5 %collective-permute-done.7.refs_4_ = bf16[8,2,16,384]{3,2,1,0:T(8,128)(2,1)S(1)} collective-permute-done((bf16[8,2,16,384]{3,2,1,0:T(8,128)(2,1)S(1)}, bf16[8,2,16,384]{3,2,1,0:T(8,128)(2,1)S(1)}, u32[]{:S(2)}, u32[]{:S(2)}) %collective-permute-start.7) | collective-permute-done | bytes 196640 | tf_op jit(solution)/shard_map/ppermute | solution.py:360
  56.8 1.0 combine.1
  57.8 3.8 %all-to-all-start = ((bf16[8,2,48,384]{3,2,1,0:T(8,128)(2,1)}), bf16[8,2,48,384]{3,2,1,0:T(8,128)(2,1)S(1)}, u32[]{:S(2)}, u32[]{:S(2)}) async-start(bf16[8,2,48,384]{3,2,1,0:T(8,128)(2,1)} %combine.1), calls=%async_computation | async-start | bytes 1179648 | tf_op jit(solution)/shard_map/all_to_all | solution.py:423
  61.5 1.6 %collective-permute-start.9 = (bf16[8,2,48,96]{3,2,1,0:T(8,128)(2,1)S(1)}, bf16[8,2,48,96]{3,2,1,0:T(8,128)(2,1)S(1)}, u32[]{:S(2)}, u32[]{:S(2)}) collective-permute-start(bf16[8,2,48,96]{3,2,1,0:T(8,128)(2,1)S(1)} %convert_element_type.9.own_ref), channel_id=1, source_target_pairs={{0,2},{2,0},{1,3},{3,1},{4,6},{6,4},{5,7},{7,5},{8,10},{10,8},{9,1... | collective-permute-start | bytes 442376 | tf_op jit(solution)/shard_map/ppermute | solution.py:360
  63.1 5.8 %collective-permute-done.9.received_ref = bf16[8,2,48,96]{3,2,1,0:T(8,128)(2,1)S(1)} collective-permute-done((bf16[8,2,48,96]{3,2,1,0:T(8,128)(2,1)S(1)}, bf16[8,2,48,96]{3,2,1,0:T(8,128)(2,1)S(1)}, u32[]{:S(2)}, u32[]{:S(2)}) %collective-permute-start.9) | collective-permute-done | bytes 147488 | tf_op jit(solution)/shard_map/ppermute | solution.py:360
  68.9 0.7 shard_map.70
  69.6 0.1 collective-permute-start.10
  69.7 1.3 %collective-permute-done.10.received_ref = bf16[4,1,2,48,96]{4,3,2,1,0:T(8,128)(2,1)S(1)} collective-permute-done((bf16[4,1,2,48,96]{4,3,2,1,0:T(8,128)(2,1)S(1)}, bf16[4,1,2,48,96]{4,3,2,1,0:T(8,128)(2,1)S(1)}, u32[]{:S(2)}, u32[]{:S(2)}) %collective-permute-start.10) | collective-permute-done | bytes 73760 | tf_op jit(solution)/shard_map/ppermute | solution.py:360
  71.0 0.6 shard_map.71
  71.6 1.7 %collective-permute-start.11 = (bf16[2,2,2,48,96]{4,3,2,1,0:T(8,128)(2,1)S(1)}, bf16[2,2,2,48,96]{4,3,2,1,0:T(8,128)(2,1)S(1)}, u32[]{:S(2)}, u32[]{:S(2)}) collective-permute-start(bf16[2,2,2,48,96]{4,3,2,1,0:T(8,128)(2,1)S(1)} %get-tuple-element.52), channel_id=1, source_target_pairs={{0,4},{4,0},{8,12},{12,8},{1,5},{5,1},{9,13},{13,9},{2,6},{6,2},{1... | collective-permute-start | bytes 221192 | tf_op jit(solution)/shard_map/ppermute | solution.py:474
  73.3 5.3 %collective-permute-done.11.received_ref = bf16[2,2,2,48,96]{4,3,2,1,0:T(8,128)(2,1)S(1)} collective-permute-done((bf16[2,2,2,48,96]{4,3,2,1,0:T(8,128)(2,1)S(1)}, bf16[2,2,2,48,96]{4,3,2,1,0:T(8,128)(2,1)S(1)}, u32[]{:S(2)}, u32[]{:S(2)}) %collective-permute-start.11) | collective-permute-done | bytes 73760 | tf_op jit(solution)/shard_map/ppermute | solution.py:474
  78.6 0.6 shard_map.72
  79.2 1.2 %collective-permute-start.12 = (bf16[1,4,2,48,96]{4,3,2,1,0:T(8,128)(2,1)S(1)}, bf16[1,4,2,48,96]{4,3,2,1,0:T(8,128)(2,1)S(1)}, u32[]{:S(2)}, u32[]{:S(2)}) collective-permute-start(bf16[1,4,2,48,96]{4,3,2,1,0:T(8,128)(2,1)S(1)} %get-tuple-element.54), channel_id=1, source_target_pairs={{0,8},{4,12},{8,0},{12,4},{1,9},{5,13},{9,1},{13,5},{2,10},{6,14},... | collective-permute-start | bytes 221192 | tf_op jit(solution)/shard_map/ppermute | solution.py:474
  80.3 5.9 %collective-permute-done.12 = bf16[1,4,2,48,96]{4,3,2,1,0:T(8,128)(2,1)S(1)} collective-permute-done((bf16[1,4,2,48,96]{4,3,2,1,0:T(8,128)(2,1)S(1)}, bf16[1,4,2,48,96]{4,3,2,1,0:T(8,128)(2,1)S(1)}, u32[]{:S(2)}, u32[]{:S(2)}) %collective-permute-start.12) | collective-permute-done | bytes 73760 | tf_op jit(solution)/shard_map/ppermute | solution.py:474
  86.2 3.6 %shard_map.73 = bf16[8,2,48,96]{3,2,1,0:T(8,128)(2,1)S(1)} custom-call(s32[1]{0:T(128)} %bitcast.rank_ref, bf16[8,2,48,384]{3,2,1,0:T(8,128)(2,1)S(1)} %all-to-all-done.field_ref, bf16[4,2,48,96]{3,2,1,0:T(8,128)(2,1)S(1)} %bitcast.20, bf16[4,2,48,96]{3,2,1,0:T(8,128)(2,1)S(1)} %bitcast.21), custom_call_target="tpu_custom_call" | custom-call | tf_op jit(solution)/shard_map/pallas_call | solution.py:349
  89.8 12.1 %all_to_all.10 = bf16[8,2,48,96]{3,2,1,0:T(8,128)(2,1)S(1)} all-to-all(bf16[8,2,48,96]{3,2,1,0:T(8,128)(2,1)S(1)} %shard_map.73), channel_id=1, replica_groups=mesh['groups'=2,'chol'=4,'walk'=2,'orb'=2] {'chol','orb'}, dimensions={0} | all-to-all | bytes 294912 | tf_op jit(solution)/shard_map/all_to_all | solution.py:542
  101.9 1.1 %reshape.43 = f32[8,2,4608]{2,1,0:T(2,128)} reshape(bf16[8,2,48,96]{3,2,1,0:T(8,128)(2,1)S(1)} %all_to_all.10) | data formatting | bytes 442368 | tf_op jit(solution)/shard_map/convert_element_type | solution.py:546
  (7 shorter events, 0.1 us)
Async XLA Ops:
  1.2 1.1 %copy-start = (f32[8,2,96,96]{3,2,1,0:T(8,128)S(1)}, f32[8,2,96,96]{3,2,1,0:T(8,128)}, u32[]{:S(2)}) copy-start(f32[8,2,96,96]{3,2,1,0:T(8,128)} %inverse_ref.1) | copy-start | bytes 1769476
  3.1 8.8 %collective-permute-start.1 = (bf16[16,4608]{1,0:T(8,128)(2,1)S(1)}, bf16[16,4608]{1,0:T(8,128)(2,1)S(1)}, u32[]{:S(2)}, u32[]{:S(2)}) collective-permute-start(bf16[16,4608]{1,0:T(8,128)(2,1)S(1)} %reshape.35.own_ref), channel_id=1, source_target_pairs={{0,2},{2,0},{1,3},{3,1},{4,6},{6,4},{5,7},{7,5},{8,10},{10,8},{9,1... | collective-permute-start | bytes 442376 | tf_op jit(solution)/shard_map/ppermute | solution.py:360
  11.8 11.2 %copy-start.2 = (s32[8]{0:T(128)S(1)}, s32[8]{0:T(128)}, u32[]{:S(2)}) copy-start(s32[8]{0:T(128)} %source_ref.3) | copy-start | bytes 100
  11.8 14.8 %copy-start.1 = (f32[16,1024]{1,0:T(8,128)S(1)}, f32[16,1024]{1,0:T(8,128)}, u32[]{:S(2)}) copy-start(f32[16,1024]{1,0:T(8,128)} %samples_ref.1) | copy-start | bytes 196612
  15.0 1.3 %collective-permute-start.2 = (f32[32,512]{1,0:T(8,128)S(1)}, f32[32,512]{1,0:T(8,128)S(1)}, u32[]{:S(2)}, u32[]{:S(2)}) collective-permute-start(f32[32,512]{1,0:T(8,128)S(1)} %get-tuple-element.32), channel_id=1, source_target_pairs={{0,1},{1,0},{2,3},{3,2},{4,5},{5,4},{6,7},{7,6},{8,9},{9,8},{10,11... | collective-permute-start | bytes 196616 | tf_op jit(solution)/shard_map/ppermute | solution.py:360
  16.3 4.0 %collective-permute-start.3 = (bf16[32,512]{1,0:T(8,128)(2,1)S(1)}, bf16[32,512]{1,0:T(8,128)(2,1)S(1)}, u32[]{:S(2)}, u32[]{:S(2)}) collective-permute-start(bf16[32,512]{1,0:T(8,128)(2,1)S(1)} %get-tuple-element.34), channel_id=1, source_target_pairs={{0,4},{4,0},{8,12},{12,8},{1,5},{5,1},{9,13},{13,9},{2,6},{6,2},{1... | collective-permute-start | bytes 98312 | tf_op jit(solution)/shard_map/ppermute | solution.py:469
  20.3 6.2 %collective-permute-start.4 = (bf16[32,512]{1,0:T(8,128)(2,1)S(1)}, bf16[32,512]{1,0:T(8,128)(2,1)S(1)}, u32[]{:S(2)}, u32[]{:S(2)}) collective-permute-start(bf16[32,512]{1,0:T(8,128)(2,1)S(1)} %get-tuple-element.36), channel_id=1, source_target_pairs={{0,8},{4,12},{8,0},{12,4},{1,9},{5,13},{9,1},{13,5},{2,10},{6,14},... | collective-permute-start | bytes 98312 | tf_op jit(solution)/shard_map/ppermute | solution.py:469
  23.0 3.6 %collective-permute-start = (s32[8]{0:T(128)S(1)}, s32[8]{0:T(128)S(1)}, u32[]{:S(2)}, u32[]{:S(2)}) collective-permute-start(s32[8]{0:T(128)S(1)} %copy-done.2), channel_id=1, source_target_pairs={{0,2},{2,0},{1,3},{3,1},{4,6},{6,4},{5,7},{7,5},{8,10},{10,8},{9,1... | collective-permute-start | bytes 104 | tf_op jit(solution)/shard_map/ppermute | solution.py:360
  27.2 3.0 %collective-permute-start.5 = (bf16[32,512]{1,0:T(8,128)(2,1)S(1)}, bf16[32,512]{1,0:T(8,128)(2,1)S(1)}, u32[]{:S(2)}, u32[]{:S(2)}) collective-permute-start(bf16[32,512]{1,0:T(8,128)(2,1)S(1)} %shard_map.68.refs_1_), channel_id=1, source_target_pairs={{0,1},{1,0},{2,3},{3,2},{4,5},{5,4},{6,7},{7,6},{8,9},{9,8},{10,11... | collective-permute-start | bytes 98312 | tf_op jit(solution)/shard_map/ppermute | solution.py:360
  37.4 10.2 %collective-permute-start.6 = (bf16[8,2,16,384]{3,2,1,0:T(8,128)(2,1)S(1)}, bf16[8,2,16,384]{3,2,1,0:T(8,128)(2,1)S(1)}, u32[]{:S(2)}, u32[]{:S(2)}) collective-permute-start(bf16[8,2,16,384]{3,2,1,0:T(8,128)(2,1)S(1)} %bitcast.22), channel_id=1, source_target_pairs={{0,2},{2,0},{1,3},{3,1},{4,6},{6,4},{5,7},{7,5},{8,10},{10,8},{9,1... | collective-permute-start | bytes 589832 | tf_op jit(solution)/shard_map/ppermute | solution.py:360
  45.5 7.8 %collective-permute-start.8 = (bf16[8,2,16,384]{3,2,1,0:T(8,128)(2,1)S(1)}, bf16[8,2,16,384]{3,2,1,0:T(8,128)(2,1)S(1)}, u32[]{:S(2)}, u32[]{:S(2)}) collective-permute-start(bf16[8,2,16,384]{3,2,1,0:T(8,128)(2,1)S(1)} %bitcast.24), channel_id=1, source_target_pairs={{0,2},{2,0},{1,3},{3,1},{4,6},{6,4},{5,7},{7,5},{8,10},{10,8},{9,1... | collective-permute-start | bytes 589832 | tf_op jit(solution)/shard_map/ppermute | solution.py:360
  47.1 9.7 %collective-permute-start.7 = (bf16[8,2,16,384]{3,2,1,0:T(8,128)(2,1)S(1)}, bf16[8,2,16,384]{3,2,1,0:T(8,128)(2,1)S(1)}, u32[]{:S(2)}, u32[]{:S(2)}) collective-permute-start(bf16[8,2,16,384]{3,2,1,0:T(8,128)(2,1)S(1)} %bitcast.23), channel_id=1, source_target_pairs={{0,2},{2,0},{1,3},{3,1},{4,6},{6,4},{5,7},{7,5},{8,10},{10,8},{9,1... | collective-permute-start | bytes 589832 | tf_op jit(solution)/shard_map/ppermute | solution.py:360
  57.8 28.5 %all-to-all-start = ((bf16[8,2,48,384]{3,2,1,0:T(8,128)(2,1)}), bf16[8,2,48,384]{3,2,1,0:T(8,128)(2,1)S(1)}, u32[]{:S(2)}, u32[]{:S(2)}) async-start(bf16[8,2,48,384]{3,2,1,0:T(8,128)(2,1)} %combine.1), calls=%async_computation | async-start | bytes 1179648 | tf_op jit(solution)/shard_map/all_to_all | solution.py:423
  61.5 7.4 %collective-permute-start.9 = (bf16[8,2,48,96]{3,2,1,0:T(8,128)(2,1)S(1)}, bf16[8,2,48,96]{3,2,1,0:T(8,128)(2,1)S(1)}, u32[]{:S(2)}, u32[]{:S(2)}) collective-permute-start(bf16[8,2,48,96]{3,2,1,0:T(8,128)(2,1)S(1)} %convert_element_type.9.own_ref), channel_id=1, source_target_pairs={{0,2},{2,0},{1,3},{3,1},{4,6},{6,4},{5,7},{7,5},{8,10},{10,8},{9,1... | collective-permute-start | bytes 442376 | tf_op jit(solution)/shard_map/ppermute | solution.py:360
  69.6 1.4 %collective-permute-start.10 = (bf16[4,1,2,48,96]{4,3,2,1,0:T(8,128)(2,1)S(1)}, bf16[4,1,2,48,96]{4,3,2,1,0:T(8,128)(2,1)S(1)}, u32[]{:S(2)}, u32[]{:S(2)}) collective-permute-start(bf16[4,1,2,48,96]{4,3,2,1,0:T(8,128)(2,1)S(1)} %get-tuple-element.50), channel_id=1, source_target_pairs={{0,1},{1,0},{2,3},{3,2},{4,5},{5,4},{6,7},{7,6},{8,9},{9,8},{10,11... | collective-permute-start | bytes 221192 | tf_op jit(solution)/shard_map/ppermute | solution.py:360
  71.6 7.0 %collective-permute-start.11 = (bf16[2,2,2,48,96]{4,3,2,1,0:T(8,128)(2,1)S(1)}, bf16[2,2,2,48,96]{4,3,2,1,0:T(8,128)(2,1)S(1)}, u32[]{:S(2)}, u32[]{:S(2)}) collective-permute-start(bf16[2,2,2,48,96]{4,3,2,1,0:T(8,128)(2,1)S(1)} %get-tuple-element.52), channel_id=1, source_target_pairs={{0,4},{4,0},{8,12},{12,8},{1,5},{5,1},{9,13},{13,9},{2,6},{6,2},{1... | collective-permute-start | bytes 221192 | tf_op jit(solution)/shard_map/ppermute | solution.py:474
  79.2 7.0 %collective-permute-start.12 = (bf16[1,4,2,48,96]{4,3,2,1,0:T(8,128)(2,1)S(1)}, bf16[1,4,2,48,96]{4,3,2,1,0:T(8,128)(2,1)S(1)}, u32[]{:S(2)}, u32[]{:S(2)}) collective-permute-start(bf16[1,4,2,48,96]{4,3,2,1,0:T(8,128)(2,1)S(1)} %get-tuple-element.54), channel_id=1, source_target_pairs={{0,8},{4,12},{8,0},{12,4},{1,9},{5,13},{9,1},{13,5},{2,10},{6,14},... | collective-permute-start | bytes 221192 | tf_op jit(solution)/shard_map/ppermute | solution.py:474

commit v6 on v5

--- a/solution.py
+++ b/solution.py
@@ -17,6 +17,7 @@
 TILE = 8
 SMALL = 8 << 20
 TINY = 2 << 20
+LINES_LIMIT = 56250000
 READ_LIMIT = 36 << 20
 VMEM = pltpu.VMEM
 
@@ -42,6 +43,47 @@
     rows = grid_ref.shape[2]
     for w in range(grid_ref.shape[0]):
         stacked = jnp.concatenate([grid_ref[w, 0], grid_ref[w, 1]], 0)
+        by_real = fine_dot(stacked, inverse_ref[w, 0])
+        by_imag = fine_dot(stacked, inverse_ref[w, 1])
+        theta_ref[w, 0] = (by_real[:rows] - by_imag[rows:]).astype(HALF)
+        theta_ref[w, 1] = (by_imag[:rows] + by_real[rows:]).astype(HALF)
+
+
+def narrow_rows(first, second, third):
+    lane = lax.broadcasted_iota(jnp.int32, first.shape, 1)
+    part = LANES // 4
+    return (
+        first,
+        jnp.where(lane < part, pltpu.roll(first, part, 1), pltpu.roll(second, part, 1)),
+        jnp.where(lane < 2 * part, pltpu.roll(second, 2 * part, 1), pltpu.roll(third, 2 * part, 1)),
+        pltpu.roll(third, 3 * part, 1),
+    )
+
+
+def lines_kernel(
+    walkers_hbm, inverse_hbm, theta_ref, start_ref, walkers_ref, inverse_ref, rows_ref, semaphores
+):
+    first = pltpu.make_async_copy(walkers_hbm, walkers_ref, semaphores.at[0])
+    first.start()
+    copy = pltpu.make_async_copy(inverse_hbm, inverse_ref, semaphores.at[1])
+    copy.start()
+    first.wait()
+    count, _, rows, electrons = theta_ref.shape
+    for c in range(2):
+        for k in range(rows // 4):
+            lines = [
+                walkers_ref[:, c, (3 * k + t) * LANES : (3 * k + t + 1) * LANES] for t in range(3)
+            ]
+            for s, narrow in enumerate(narrow_rows(*lines)):
+                rows_ref[c, pl.ds(4 * k + s, count, stride=rows)] = narrow
+    for w in range(count):
+        for c in range(2):
+            start_ref[w, c] = rows_ref[c, w * rows : (w + 1) * rows, :electrons].astype(HALF)
+    copy.wait()
+    for w in range(count):
+        stacked = jnp.concatenate(
+            [rows_ref[c, w * rows : (w + 1) * rows, :electrons] for c in range(2)], 0
+        )
         by_real = fine_dot(stacked, inverse_ref[w, 0])
         by_imag = fine_dot(stacked, inverse_ref[w, 1])
         theta_ref[w, 0] = (by_real[:rows] - by_imag[rows:]).astype(HALF)
@@ -432,13 +474,29 @@
     other_source = others(source)
     place = jnp.stack([first, core, lax.axis_index("chol")]).astype(jnp.int32)
     rank = lax.axis_index(ROWS).astype(jnp.int32).reshape(1)
-    grid = walkers.reshape(local, 2, row_block, electrons)
-    theta = local_kernel(
-        theta_kernel, [ARRAY] * 2, jax.ShapeDtypeStruct(grid.shape, HALF), limit=SMALL
-    )(grid, correlation_inverse)
+    grid_shape = (local, 2, row_block, electrons)
+    half_grid = jax.ShapeDtypeStruct(grid_shape, HALF)
+    if fast and 4 * electrons == 3 * LANES and row_block % TILE == 0:
+        theta, start = local_kernel(
+            lines_kernel,
+            [pl.BlockSpec(memory_space=pltpu.HBM)] * 2,
+            [half_grid] * 2,
+            [
+                VMEM(walkers.shape, FULL),
+                VMEM(correlation_inverse.shape, FULL),
+                VMEM((2, local * row_block, LANES), FULL),
+                pltpu.SemaphoreType.DMA((2,)),
+            ],
+            LINES_LIMIT,
+        )(walkers, correlation_inverse)
+    else:
+        grid = walkers.reshape(grid_shape)
+        start = grid.astype(HALF)
+        theta = local_kernel(theta_kernel, [ARRAY] * 2, half_grid, limit=SMALL)(
+            grid, correlation_inverse
+        )
     theta = theta.reshape(local * 2, row_block * electrons)
     other_theta = others(theta)
-    start = grid.astype(HALF)
     other_start = others(start)
 
     if fast:

time: 103 us -> 102 us (level)
  local copies, waits for them, and re-layouts: 3.69 us -> 1.31 us
  Pallas kernels: 33.9 us -> 35.5 us
    pallas_call x1, Pallas kernels: 0.45 us -> 2.02 us  [whole_step(): local_kernel(lines_kernel, [pl.BlockSpec(memory_space=pltpu.HBM)] * 2, [h...]
    reshape x1 -> x0, local copies, waits for them, and re-layouts: 1.25 us -> none  [whole_step(): grid = walkers.reshape(local, 2, row_block, electrons)]
    unnamed x6, local copies, waits for them, and re-layouts: 1.15 us -> 0.02 us
  transfers between devices with their start and end apart: 14 -> 14, of which waited for: 9 -> 9; matrix products, arithmetic and copies ran while one was open for 0% -> 0% of each run, Pallas kernels for 17% -> 18%
where the time goes in v6:
time: 102 us
  Pallas kernels  35.5 us (35%)
  waiting for transfers between devices  34 us (33%)
  starting transfers between devices  19 us (19%)
  blocking collectives  12.1 us (12%)
  local copies, waits for them, and re-layouts  1.31 us (1%)
    ppermute x9, waiting for transfers between devices, shift(): lax.ppermute(value, axis, [(i, (i + step) % size) for i in range(size)])  20.5 us
    pallas_call x3, Pallas kernels, field_rows(): pl.pallas_call(functools.partial(field_kernel, part, wanted, mine), in_sp...  14.7 us
    all_to_all x1, blocking collectives, whole_step(): lax.all_to_all(normalized, ROWS, split_axis=0, concat_axis=0, tiled=True)  12.1 us
    ppermute x2, waiting for transfers between devices, whole_step(): passed = lax.ppermute(sent, 'chol', pairs)  11.2 us
    ppermute x9, starting transfers between devices, shift(): lax.ppermute(value, axis, [(i, (i + step) % size) for i in range(size)])  8.02 us
    pallas_call x1, Pallas kernels, read_early(): pl.pallas_call(read_kernel, in_specs=[pl.BlockSpec(memory_space=pl.ANY)]...  5.66 us
    ppermute x2, starting transfers between devices, whole_step(): received = lax.ppermute(rounded, 'chol', pairs)  4.29 us
    all_to_all x1, starting transfers between devices, to_owners(): return lax.all_to_all(value, ROWS, split_axis=0, concat_axis=0, tiled=True)  3.76 us
  transfers between devices with their start and end apart: 14, of which 9 were waited for; matrix products, arithmetic and copies ran while one was open for 0% of the time, Pallas kernels for 18%

profile of v6, /device:TPU:0, one launch (start us, length us, event | category | flops | bytes accessed | tf_op | source)
XLA Modules:
  0.0 102.1 jit_solution(831143764929528784)
XLA Ops:
  0.0 2.0 %shard_map.64 = (bf16[8,2,48,96]{3,2,1,0:T(8,128)(2,1)S(1)}, bf16[8,2,48,96]{3,2,1,0:T(8,128)(2,1)}) custom-call(f32[8,2,4608]{2,1,0:T(2,128)} %walkers_hbm.1, f32[8,2,96,96]{3,2,1,0:T(8,128)} %inverse_hbm.1), custom_call_target="tpu_custom_call" | custom-call | tf_op jit(solution)/shard_map/pallas_call | solution.py:480
  2.0 0.2 reshape.31.own_ref
  2.2 3.0 %collective-permute-start.1 = (bf16[16,4608]{1,0:T(8,128)(2,1)S(1)}, bf16[16,4608]{1,0:T(8,128)(2,1)S(1)}, u32[]{:S(2)}, u32[]{:S(2)}) collective-permute-start(bf16[16,4608]{1,0:T(8,128)(2,1)S(1)} %reshape.31.own_ref), channel_id=1, source_target_pairs={{0,2},{2,0},{1,3},{3,1},{4,6},{6,4},{5,7},{7,5},{8,10},{10,8},{9,1... | collective-permute-start | bytes 442376 | tf_op jit(solution)/shard_map/ppermute | solution.py:402
  5.3 5.7 %read.1 = (bf16[1024,4608]{1,0:T(8,128)(2,1)S(1)}, bf16[512,2,8,384]{3,2,1,0:T(8,128)(2,1)S(1)}) custom-call(bf16[1024,4608]{1,0:T(8,128)(2,1)} %half_hbm.1, bf16[1024,6,8,384]{3,2,1,0:T(8,128)(2,1)} %bitcast.25), custom_call_target="tpu_custom_call" | custom-call | tf_op jit(solution)/shard_map/read/pallas_call | solution.py:222
  10.9 0.0 copy-start.2
  11.0 0.0 copy-start.1
  11.0 0.1 pad_add_fusion.place_ref.refs_0_
  11.0 0.0 collective-permute-done.1.received_ref
  11.0 3.1 %shard_map.65 = (f32[32,512]{1,0:T(8,128)S(1)}, f32[32,512]{1,0:T(8,128)S(1)}) custom-call(s32[3]{0:T(128)S(1)} %pad_add_fusion.place_ref.refs_0_, bf16[16,4608]{1,0:T(8,128)(2,1)S(1)} %reshape.31.own_ref, bf16[16,4608]{1,0:T(8,128)(2,1)S(1)} %collective-permute-done.1.received_ref, bf16[1024,4608]{1,0:T(8,128)(2,1)S(1)} %get-tuple-element.33.vectors_ref), custom_call_target="tpu_custom_call" | custom-call | tf_op jit(solution)/shard_map/pallas_call | solution.py:516
  14.2 0.1 collective-permute-start.2
  14.3 1.2 %collective-permute-done.2.right_ref = f32[32,512]{1,0:T(8,128)S(1)} collective-permute-done((f32[32,512]{1,0:T(8,128)S(1)}, f32[32,512]{1,0:T(8,128)S(1)}, u32[]{:S(2)}, u32[]{:S(2)}) %collective-permute-start.2) | collective-permute-done | bytes 65568 | tf_op jit(solution)/shard_map/ppermute | solution.py:402
  15.5 1.6 %collective-permute-start.3 = (bf16[32,512]{1,0:T(8,128)(2,1)S(1)}, bf16[32,512]{1,0:T(8,128)(2,1)S(1)}, u32[]{:S(2)}, u32[]{:S(2)}) collective-permute-start(bf16[32,512]{1,0:T(8,128)(2,1)S(1)} %get-tuple-element.37), channel_id=1, source_target_pairs={{0,4},{4,0},{8,12},{12,8},{1,5},{5,1},{9,13},{13,9},{2,6},{6,2},{1... | collective-permute-start | bytes 98312 | tf_op jit(solution)/shard_map/ppermute | solution.py:527
  17.1 2.3 %collective-permute-done.3.right_ref = bf16[32,512]{1,0:T(8,128)(2,1)S(1)} collective-permute-done((bf16[32,512]{1,0:T(8,128)(2,1)S(1)}, bf16[32,512]{1,0:T(8,128)(2,1)S(1)}, u32[]{:S(2)}, u32[]{:S(2)}) %collective-permute-start.3) | collective-permute-done | bytes 32800 | tf_op jit(solution)/shard_map/ppermute | solution.py:527
  19.5 2.6 %collective-permute-start.4 = (bf16[32,512]{1,0:T(8,128)(2,1)S(1)}, bf16[32,512]{1,0:T(8,128)(2,1)S(1)}, u32[]{:S(2)}, u32[]{:S(2)}) collective-permute-start(bf16[32,512]{1,0:T(8,128)(2,1)S(1)} %get-tuple-element.39), channel_id=1, source_target_pairs={{0,8},{4,12},{8,0},{12,4},{1,9},{5,13},{9,1},{13,5},{2,10},{6,14},... | collective-permute-start | bytes 98312 | tf_op jit(solution)/shard_map/ppermute | solution.py:527
  22.2 0.5 collective-permute-start
  22.7 3.0 %collective-permute-done.others_ref = s32[8]{0:T(128)S(1)} collective-permute-done((s32[8]{0:T(128)S(1)}, s32[8]{0:T(128)S(1)}, u32[]{:S(2)}, u32[]{:S(2)}) %collective-permute-start) | collective-permute-done | bytes 64 | tf_op jit(solution)/shard_map/ppermute | solution.py:402
  25.7 0.0 collective-permute-done.4.right_ref
  25.7 0.7 shard_map.68.refs_1_
  26.4 0.1 collective-permute-start.5
  26.5 2.9 %shard_map.69.refs_4_ = bf16[512,2,8,384]{3,2,1,0:T(8,128)(2,1)S(1)} custom-call(f32[32,512]{1,0:T(8,128)S(1)} %get-tuple-element.38.left_ref.order_ref, bf16[1024,6,8,384]{3,2,1,0:T(8,128)(2,1)} %bitcast.26), custom_call_target="tpu_custom_call" | custom-call | tf_op jit(solution)/shard_map/pallas_call | solution.py:534
  29.4 0.0 collective-permute-done.5.refs_2_
  29.4 7.2 %field.3 = (f32[16,16,384]{2,1,0:T(8,128)S(1)}, bf16[16,16,384]{2,1,0:T(8,128)(2,1)S(1)}, bf16[256,8192]{1,0:T(8,128)(2,1)S(1)}, bf16[512,2,8,384]{3,2,1,0:T(8,1...) custom-call(s32[3]{0:T(128)S(1)} %pad_add_fusion.place_ref.refs_0_, ...), custom_call_target="tpu_custom_call" | custom-call | flops 3221225472 | bytes 12582912 | tf_op jit(solution)/shard_map/field/pallas_call | solution.py:284
  36.6 0.6 collective-permute-start.6
  37.2 4.1 %field.4 = (f32[16,16,384]{2,1,0:T(8,128)S(1)}, bf16[16,16,384]{2,1,0:T(8,128)(2,1)S(1)}, bf16[512,2,8,384]{3,2,1,0:T(8,128)(2,1)S(1)}) custom-call(bf16[256,8192]{1,0:T(8,128)(2,1)S(1)} %get-tuple-element.42.refs_0_, bf16[512,2,8,384]{3,2,1,0:T(8,128)(2,1)S(1)} %get-tuple-element.43.refs_1_, bf16[512,2,8,384]{3,2,1,0:T(8,128)(2,1)S(1)} %get-tuple-element.44.refs_2_, ...), custom_call_target="tpu_custom_call" | custom-call | flops 3221225472 | bytes 12582912 | tf_op jit(solution)/shard_map/field/pallas_call | solution.py:284
  41.2 0.0 copy-start
  41.2 3.4 %field.5 = (f32[16,16,384]{2,1,0:T(8,128)S(1)}, bf16[16,16,384]{2,1,0:T(8,128)(2,1)S(1)}) custom-call(bf16[256,8192]{1,0:T(8,128)(2,1)S(1)} %get-tuple-element.42.refs_0_, bf16[512,2,8,384]{3,2,1,0:T(8,128)(2,1)S(1)} %get-tuple-element.46.refs_1_, bf16[512,2,8,384]{3,2,1,0:T(8,128)(2,1)S(1)} %get-tuple-element.47.refs_2_, bf16[1024,6,8,384]{3,2,1,0:T(8,128)(2,1)} %bitcast.29), custom_call_target="tpu_custom_call" | custom-call | flops 3221225472 | bytes 12582912 | tf_op jit(solution)/shard_map/field/pallas_call | solution.py:284
  44.7 1.5 %collective-permute-start.8 = (bf16[8,2,16,384]{3,2,1,0:T(8,128)(2,1)S(1)}, bf16[8,2,16,384]{3,2,1,0:T(8,128)(2,1)S(1)}, u32[]{:S(2)}, u32[]{:S(2)}) collective-permute-start(bf16[8,2,16,384]{3,2,1,0:T(8,128)(2,1)S(1)} %bitcast.24), channel_id=1, source_target_pairs={{0,2},{2,0},{1,3},{3,1},{4,6},{6,4},{5,7},{7,5},{8,10},{10,8},{9,1... | collective-permute-start | bytes 589832 | tf_op jit(solution)/shard_map/ppermute | solution.py:402
  46.2 0.5 collective-permute-start.7
  46.8 0.0 collective-permute-done.6.refs_3_
  46.8 5.7 %collective-permute-done.8.refs_5_ = bf16[8,2,16,384]{3,2,1,0:T(8,128)(2,1)S(1)} collective-permute-done((bf16[8,2,16,384]{3,2,1,0:T(8,128)(2,1)S(1)}, bf16[8,2,16,384]{3,2,1,0:T(8,128)(2,1)S(1)}, u32[]{:S(2)}, u32[]{:S(2)}) %collective-permute-start.8) | collective-permute-done | bytes 196640 | tf_op jit(solution)/shard_map/ppermute | solution.py:402
  52.5 3.5 %collective-permute-done.7.refs_4_ = bf16[8,2,16,384]{3,2,1,0:T(8,128)(2,1)S(1)} collective-permute-done((bf16[8,2,16,384]{3,2,1,0:T(8,128)(2,1)S(1)}, bf16[8,2,16,384]{3,2,1,0:T(8,128)(2,1)S(1)}, u32[]{:S(2)}, u32[]{:S(2)}) %collective-permute-start.7) | collective-permute-done | bytes 196640 | tf_op jit(solution)/shard_map/ppermute | solution.py:402
  56.0 1.0 combine.1
  57.0 3.8 %all-to-all-start = ((bf16[8,2,48,384]{3,2,1,0:T(8,128)(2,1)}), bf16[8,2,48,384]{3,2,1,0:T(8,128)(2,1)S(1)}, u32[]{:S(2)}, u32[]{:S(2)}) async-start(bf16[8,2,48,384]{3,2,1,0:T(8,128)(2,1)} %combine.1), calls=%async_computation | async-start | bytes 1179648 | tf_op jit(solution)/shard_map/all_to_all | solution.py:465
  60.7 1.6 %collective-permute-start.9 = (bf16[8,2,48,96]{3,2,1,0:T(8,128)(2,1)S(1)}, bf16[8,2,48,96]{3,2,1,0:T(8,128)(2,1)S(1)}, u32[]{:S(2)}, u32[]{:S(2)}) collective-permute-start(bf16[8,2,48,96]{3,2,1,0:T(8,128)(2,1)S(1)} %copy-done), channel_id=1, source_target_pairs={{0,2},{2,0},{1,3},{3,1},{4,6},{6,4},{5,7},{7,5},{8,10},{10,8},{9,1... | collective-permute-start | bytes 442376 | tf_op jit(solution)/shard_map/ppermute | solution.py:402
  62.3 5.8 %collective-permute-done.9.received_ref = bf16[8,2,48,96]{3,2,1,0:T(8,128)(2,1)S(1)} collective-permute-done((bf16[8,2,48,96]{3,2,1,0:T(8,128)(2,1)S(1)}, bf16[8,2,48,96]{3,2,1,0:T(8,128)(2,1)S(1)}, u32[]{:S(2)}, u32[]{:S(2)}) %collective-permute-start.9) | collective-permute-done | bytes 147488 | tf_op jit(solution)/shard_map/ppermute | solution.py:402
  68.0 0.7 shard_map.70
  68.7 0.1 collective-permute-start.10
  68.8 1.3 %collective-permute-done.10.received_ref = bf16[4,1,2,48,96]{4,3,2,1,0:T(8,128)(2,1)S(1)} collective-permute-done((bf16[4,1,2,48,96]{4,3,2,1,0:T(8,128)(2,1)S(1)}, bf16[4,1,2,48,96]{4,3,2,1,0:T(8,128)(2,1)S(1)}, u32[]{:S(2)}, u32[]{:S(2)}) %collective-permute-start.10) | collective-permute-done | bytes 73760 | tf_op jit(solution)/shard_map/ppermute | solution.py:402
  70.1 0.6 shard_map.71
  70.7 1.7 %collective-permute-start.11 = (bf16[2,2,2,48,96]{4,3,2,1,0:T(8,128)(2,1)S(1)}, bf16[2,2,2,48,96]{4,3,2,1,0:T(8,128)(2,1)S(1)}, u32[]{:S(2)}, u32[]{:S(2)}) collective-permute-start(bf16[2,2,2,48,96]{4,3,2,1,0:T(8,128)(2,1)S(1)} %get-tuple-element.56), channel_id=1, source_target_pairs={{0,4},{4,0},{8,12},{12,8},{1,5},{5,1},{9,13},{13,9},{2,6},{6,2},{1... | collective-permute-start | bytes 221192 | tf_op jit(solution)/shard_map/ppermute | solution.py:532
  72.4 5.3 %collective-permute-done.11.received_ref = bf16[2,2,2,48,96]{4,3,2,1,0:T(8,128)(2,1)S(1)} collective-permute-done((bf16[2,2,2,48,96]{4,3,2,1,0:T(8,128)(2,1)S(1)}, bf16[2,2,2,48,96]{4,3,2,1,0:T(8,128)(2,1)S(1)}, u32[]{:S(2)}, u32[]{:S(2)}) %collective-permute-start.11) | collective-permute-done | bytes 73760 | tf_op jit(solution)/shard_map/ppermute | solution.py:532
  77.7 0.6 shard_map.72
  78.3 1.2 %collective-permute-start.12 = (bf16[1,4,2,48,96]{4,3,2,1,0:T(8,128)(2,1)S(1)}, bf16[1,4,2,48,96]{4,3,2,1,0:T(8,128)(2,1)S(1)}, u32[]{:S(2)}, u32[]{:S(2)}) collective-permute-start(bf16[1,4,2,48,96]{4,3,2,1,0:T(8,128)(2,1)S(1)} %get-tuple-element.58), channel_id=1, source_target_pairs={{0,8},{4,12},{8,0},{12,4},{1,9},{5,13},{9,1},{13,5},{2,10},{6,14},... | collective-permute-start | bytes 221192 | tf_op jit(solution)/shard_map/ppermute | solution.py:532
  79.5 5.8 %collective-permute-done.12 = bf16[1,4,2,48,96]{4,3,2,1,0:T(8,128)(2,1)S(1)} collective-permute-done((bf16[1,4,2,48,96]{4,3,2,1,0:T(8,128)(2,1)S(1)}, bf16[1,4,2,48,96]{4,3,2,1,0:T(8,128)(2,1)S(1)}, u32[]{:S(2)}, u32[]{:S(2)}) %collective-permute-start.12) | collective-permute-done | bytes 73760 | tf_op jit(solution)/shard_map/ppermute | solution.py:532
  85.3 0.0 all-to-all-done.field_ref
  85.3 3.6 %shard_map.73 = bf16[8,2,48,96]{3,2,1,0:T(8,128)(2,1)S(1)} custom-call(s32[1]{0:T(128)} %bitcast.rank_ref, bf16[8,2,48,384]{3,2,1,0:T(8,128)(2,1)S(1)} %all-to-all-done.field_ref, bf16[4,2,48,96]{3,2,1,0:T(8,128)(2,1)S(1)} %bitcast.20, bf16[4,2,48,96]{3,2,1,0:T(8,128)(2,1)S(1)} %bitcast.21), custom_call_target="tpu_custom_call" | custom-call | tf_op jit(solution)/shard_map/pallas_call | solution.py:391
  88.9 12.1 %all_to_all.10 = bf16[8,2,48,96]{3,2,1,0:T(8,128)(2,1)S(1)} all-to-all(bf16[8,2,48,96]{3,2,1,0:T(8,128)(2,1)S(1)} %shard_map.73), channel_id=1, replica_groups=mesh['groups'=2,'chol'=4,'walk'=2,'orb'=2] {'chol','orb'}, dimensions={0} | all-to-all | bytes 294912 | tf_op jit(solution)/shard_map/all_to_all | solution.py:600
  101.0 1.1 %reshape.39 = f32[8,2,4608]{2,1,0:T(2,128)} reshape(bf16[8,2,48,96]{3,2,1,0:T(8,128)(2,1)S(1)} %all_to_all.10) | data formatting | bytes 442368 | tf_op jit(solution)/shard_map/convert_element_type | solution.py:604
  (5 shorter events, 0.0 us)
Async XLA Ops:
  2.2 8.8 %collective-permute-start.1 = (bf16[16,4608]{1,0:T(8,128)(2,1)S(1)}, bf16[16,4608]{1,0:T(8,128)(2,1)S(1)}, u32[]{:S(2)}, u32[]{:S(2)}) collective-permute-start(bf16[16,4608]{1,0:T(8,128)(2,1)S(1)} %reshape.31.own_ref), channel_id=1, source_target_pairs={{0,2},{2,0},{1,3},{3,1},{4,6},{6,4},{5,7},{7,5},{8,10},{10,8},{9,1... | collective-permute-start | bytes 442376 | tf_op jit(solution)/shard_map/ppermute | solution.py:402
  10.9 11.2 %copy-start.2 = (s32[8]{0:T(128)S(1)}, s32[8]{0:T(128)}, u32[]{:S(2)}) copy-start(s32[8]{0:T(128)} %source_ref.3) | copy-start | bytes 100
  11.0 14.8 %copy-start.1 = (f32[16,1024]{1,0:T(8,128)S(1)}, f32[16,1024]{1,0:T(8,128)}, u32[]{:S(2)}) copy-start(f32[16,1024]{1,0:T(8,128)} %samples_ref.1) | copy-start | bytes 196612
  14.2 1.3 %collective-permute-start.2 = (f32[32,512]{1,0:T(8,128)S(1)}, f32[32,512]{1,0:T(8,128)S(1)}, u32[]{:S(2)}, u32[]{:S(2)}) collective-permute-start(f32[32,512]{1,0:T(8,128)S(1)} %get-tuple-element.35), channel_id=1, source_target_pairs={{0,1},{1,0},{2,3},{3,2},{4,5},{5,4},{6,7},{7,6},{8,9},{9,8},{10,11... | collective-permute-start | bytes 196616 | tf_op jit(solution)/shard_map/ppermute | solution.py:402
  15.5 4.0 %collective-permute-start.3 = (bf16[32,512]{1,0:T(8,128)(2,1)S(1)}, bf16[32,512]{1,0:T(8,128)(2,1)S(1)}, u32[]{:S(2)}, u32[]{:S(2)}) collective-permute-start(bf16[32,512]{1,0:T(8,128)(2,1)S(1)} %get-tuple-element.37), channel_id=1, source_target_pairs={{0,4},{4,0},{8,12},{12,8},{1,5},{5,1},{9,13},{13,9},{2,6},{6,2},{1... | collective-permute-start | bytes 98312 | tf_op jit(solution)/shard_map/ppermute | solution.py:527
  19.5 6.2 %collective-permute-start.4 = (bf16[32,512]{1,0:T(8,128)(2,1)S(1)}, bf16[32,512]{1,0:T(8,128)(2,1)S(1)}, u32[]{:S(2)}, u32[]{:S(2)}) collective-permute-start(bf16[32,512]{1,0:T(8,128)(2,1)S(1)} %get-tuple-element.39), channel_id=1, source_target_pairs={{0,8},{4,12},{8,0},{12,4},{1,9},{5,13},{9,1},{13,5},{2,10},{6,14},... | collective-permute-start | bytes 98312 | tf_op jit(solution)/shard_map/ppermute | solution.py:527
  22.2 3.6 %collective-permute-start = (s32[8]{0:T(128)S(1)}, s32[8]{0:T(128)S(1)}, u32[]{:S(2)}, u32[]{:S(2)}) collective-permute-start(s32[8]{0:T(128)S(1)} %copy-done.2), channel_id=1, source_target_pairs={{0,2},{2,0},{1,3},{3,1},{4,6},{6,4},{5,7},{7,5},{8,10},{10,8},{9,1... | collective-permute-start | bytes 104 | tf_op jit(solution)/shard_map/ppermute | solution.py:402
  26.4 3.0 %collective-permute-start.5 = (bf16[32,512]{1,0:T(8,128)(2,1)S(1)}, bf16[32,512]{1,0:T(8,128)(2,1)S(1)}, u32[]{:S(2)}, u32[]{:S(2)}) collective-permute-start(bf16[32,512]{1,0:T(8,128)(2,1)S(1)} %shard_map.68.refs_1_), channel_id=1, source_target_pairs={{0,1},{1,0},{2,3},{3,2},{4,5},{5,4},{6,7},{7,6},{8,9},{9,8},{10,11... | collective-permute-start | bytes 98312 | tf_op jit(solution)/shard_map/ppermute | solution.py:402
  36.6 10.2 %collective-permute-start.6 = (bf16[8,2,16,384]{3,2,1,0:T(8,128)(2,1)S(1)}, bf16[8,2,16,384]{3,2,1,0:T(8,128)(2,1)S(1)}, u32[]{:S(2)}, u32[]{:S(2)}) collective-permute-start(bf16[8,2,16,384]{3,2,1,0:T(8,128)(2,1)S(1)} %bitcast.22), channel_id=1, source_target_pairs={{0,2},{2,0},{1,3},{3,1},{4,6},{6,4},{5,7},{7,5},{8,10},{10,8},{9,1... | collective-permute-start | bytes 589832 | tf_op jit(solution)/shard_map/ppermute | solution.py:402
  41.2 19.5 %copy-start = (bf16[8,2,48,96]{3,2,1,0:T(8,128)(2,1)S(1)}, bf16[8,2,48,96]{3,2,1,0:T(8,128)(2,1)}, u32[]{:S(2)}) copy-start(bf16[8,2,48,96]{3,2,1,0:T(8,128)(2,1)} %get-tuple-element.52.own_ref) | copy-start | bytes 442372
  44.7 7.8 %collective-permute-start.8 = (bf16[8,2,16,384]{3,2,1,0:T(8,128)(2,1)S(1)}, bf16[8,2,16,384]{3,2,1,0:T(8,128)(2,1)S(1)}, u32[]{:S(2)}, u32[]{:S(2)}) collective-permute-start(bf16[8,2,16,384]{3,2,1,0:T(8,128)(2,1)S(1)} %bitcast.24), channel_id=1, source_target_pairs={{0,2},{2,0},{1,3},{3,1},{4,6},{6,4},{5,7},{7,5},{8,10},{10,8},{9,1... | collective-permute-start | bytes 589832 | tf_op jit(solution)/shard_map/ppermute | solution.py:402
  46.2 9.7 %collective-permute-start.7 = (bf16[8,2,16,384]{3,2,1,0:T(8,128)(2,1)S(1)}, bf16[8,2,16,384]{3,2,1,0:T(8,128)(2,1)S(1)}, u32[]{:S(2)}, u32[]{:S(2)}) collective-permute-start(bf16[8,2,16,384]{3,2,1,0:T(8,128)(2,1)S(1)} %bitcast.23), channel_id=1, source_target_pairs={{0,2},{2,0},{1,3},{3,1},{4,6},{6,4},{5,7},{7,5},{8,10},{10,8},{9,1... | collective-permute-start | bytes 589832 | tf_op jit(solution)/shard_map/ppermute | solution.py:402
  57.0 28.4 %all-to-all-start = ((bf16[8,2,48,384]{3,2,1,0:T(8,128)(2,1)}), bf16[8,2,48,384]{3,2,1,0:T(8,128)(2,1)S(1)}, u32[]{:S(2)}, u32[]{:S(2)}) async-start(bf16[8,2,48,384]{3,2,1,0:T(8,128)(2,1)} %combine.1), calls=%async_computation | async-start | bytes 1179648 | tf_op jit(solution)/shard_map/all_to_all | solution.py:465
  60.7 7.3 %collective-permute-start.9 = (bf16[8,2,48,96]{3,2,1,0:T(8,128)(2,1)S(1)}, bf16[8,2,48,96]{3,2,1,0:T(8,128)(2,1)S(1)}, u32[]{:S(2)}, u32[]{:S(2)}) collective-permute-start(bf16[8,2,48,96]{3,2,1,0:T(8,128)(2,1)S(1)} %copy-done), channel_id=1, source_target_pairs={{0,2},{2,0},{1,3},{3,1},{4,6},{6,4},{5,7},{7,5},{8,10},{10,8},{9,1... | collective-permute-start | bytes 442376 | tf_op jit(solution)/shard_map/ppermute | solution.py:402
  68.7 1.4 %collective-permute-start.10 = (bf16[4,1,2,48,96]{4,3,2,1,0:T(8,128)(2,1)S(1)}, bf16[4,1,2,48,96]{4,3,2,1,0:T(8,128)(2,1)S(1)}, u32[]{:S(2)}, u32[]{:S(2)}) collective-permute-start(bf16[4,1,2,48,96]{4,3,2,1,0:T(8,128)(2,1)S(1)} %get-tuple-element.54), channel_id=1, source_target_pairs={{0,1},{1,0},{2,3},{3,2},{4,5},{5,4},{6,7},{7,6},{8,9},{9,8},{10,11... | collective-permute-start | bytes 221192 | tf_op jit(solution)/shard_map/ppermute | solution.py:402
  70.7 7.0 %collective-permute-start.11 = (bf16[2,2,2,48,96]{4,3,2,1,0:T(8,128)(2,1)S(1)}, bf16[2,2,2,48,96]{4,3,2,1,0:T(8,128)(2,1)S(1)}, u32[]{:S(2)}, u32[]{:S(2)}) collective-permute-start(bf16[2,2,2,48,96]{4,3,2,1,0:T(8,128)(2,1)S(1)} %get-tuple-element.56), channel_id=1, source_target_pairs={{0,4},{4,0},{8,12},{12,8},{1,5},{5,1},{9,13},{13,9},{2,6},{6,2},{1... | collective-permute-start | bytes 221192 | tf_op jit(solution)/shard_map/ppermute | solution.py:532
  78.3 7.0 %collective-permute-start.12 = (bf16[1,4,2,48,96]{4,3,2,1,0:T(8,128)(2,1)S(1)}, bf16[1,4,2,48,96]{4,3,2,1,0:T(8,128)(2,1)S(1)}, u32[]{:S(2)}, u32[]{:S(2)}) collective-permute-start(bf16[1,4,2,48,96]{4,3,2,1,0:T(8,128)(2,1)S(1)} %get-tuple-element.58), channel_id=1, source_target_pairs={{0,8},{4,12},{8,0},{12,4},{1,9},{5,13},{9,1},{13,5},{2,10},{6,14},... | collective-permute-start | bytes 221192 | tf_op jit(solution)/shard_map/ppermute | solution.py:532

commit v7 on v6

--- a/solution.py
+++ b/solution.py
@@ -58,6 +58,29 @@
         jnp.where(lane < 2 * part, pltpu.roll(second, 2 * part, 1), pltpu.roll(third, 2 * part, 1)),
         pltpu.roll(third, 3 * part, 1),
     )
+
+
+def wide_lines(first, second, third, fourth):
+    lane = lax.broadcasted_iota(jnp.int32, first.shape, 1)
+    part = LANES // 4
+    second, third = pltpu.roll(second, 3 * part, 1), pltpu.roll(third, 2 * part, 1)
+    return (
+        jnp.where(lane < 3 * part, first, second),
+        jnp.where(lane < 2 * part, second, third),
+        jnp.where(lane < part, third, pltpu.roll(fourth, part, 1)),
+    )
+
+
+def flatten_kernel(grid_ref, out_ref, rows_ref):
+    count, _, rows, electrons = grid_ref.shape
+    for w in range(count):
+        for c in range(2):
+            rows_ref[c, w * rows : (w + 1) * rows, :electrons] = grid_ref[w, c].astype(FULL)
+    for c in range(2):
+        for k in range(rows // 4):
+            narrow = [rows_ref[c, pl.ds(4 * k + s, count, stride=rows)] for s in range(4)]
+            for t, line in enumerate(wide_lines(*narrow)):
+                out_ref[:, c, (3 * k + t) * LANES : (3 * k + t + 1) * LANES] = line
 
 
 def lines_kernel(
@@ -598,6 +621,13 @@
         width = electrons // sharers
         normalized = lax.dynamic_slice_in_dim(normalized, share * width, width, 3)
     returned = lax.all_to_all(normalized, ROWS, split_axis=0, concat_axis=0, tiled=True)
+    if fast and 4 * electrons == 3 * LANES and row_block % TILE == 0:
+        return local_kernel(
+            flatten_kernel,
+            [ARRAY],
+            jax.ShapeDtypeStruct(walkers.shape, FULL),
+            [VMEM((2, local * row_block, LANES), FULL)],
+        )(returned)
     if sharers > 1:
         returned = returned.reshape(local, sharers, 2, row_block, width)
         returned = returned.transpose(0, 2, 3, 1, 4)

time: 102 us -> 102 us (level)
  local copies, waits for them, and re-layouts: 1.31 us -> 0.22 us
    convert_element_type x1 -> x0, local copies, waits for them, and re-layouts: 1.09 us -> none  [whole_step(): return returned.reshape(local, 2, row_block * electrons).astype(FULL)]
where the time goes in v7:
time: 102 us
  Pallas kernels  36.5 us (36%)
  waiting for transfers between devices  34 us (33%)
  starting transfers between devices  19 us (19%)
  blocking collectives  12.1 us (12%)
    ppermute x9, waiting for transfers between devices, shift(): lax.ppermute(value, axis, [(i, (i + step) % size) for i in range(size)])  20.5 us
    pallas_call x3, Pallas kernels, field_rows(): pl.pallas_call(functools.partial(field_kernel, part, wanted, mine), in_sp...  14.7 us
    all_to_all x1, blocking collectives, whole_step(): lax.all_to_all(normalized, ROWS, split_axis=0, concat_axis=0, tiled=True)  12.1 us
    ppermute x2, waiting for transfers between devices, whole_step(): passed = lax.ppermute(sent, 'chol', pairs)  11.2 us
    ppermute x9, starting transfers between devices, shift(): lax.ppermute(value, axis, [(i, (i + step) % size) for i in range(size)])  8.02 us
    pallas_call x1, Pallas kernels, read_early(): pl.pallas_call(read_kernel, in_specs=[pl.BlockSpec(memory_space=pl.ANY)]...  5.66 us
    ppermute x2, starting transfers between devices, whole_step(): received = lax.ppermute(rounded, 'chol', pairs)  4.29 us
    all_to_all x1, starting transfers between devices, to_owners(): return lax.all_to_all(value, ROWS, split_axis=0, concat_axis=0, tiled=True)  3.76 us
  transfers between devices with their start and end apart: 14, of which 9 were waited for; matrix products, arithmetic and copies ran while one was open for 0% of the time, Pallas kernels for 18%

profile of v7, /device:TPU:0, one launch (start us, length us, event | category | flops | bytes accessed | tf_op | source)
XLA Modules:
  0.0 102.0 jit_solution(5193457210910469551)
XLA Ops:
  0.0 2.0 %shard_map.64 = (bf16[8,2,48,96]{3,2,1,0:T(8,128)(2,1)S(1)}, bf16[8,2,48,96]{3,2,1,0:T(8,128)(2,1)}) custom-call(f32[8,2,4608]{2,1,0:T(2,128)} %walkers_hbm.1, f32[8,2,96,96]{3,2,1,0:T(8,128)} %inverse_hbm.1), custom_call_target="tpu_custom_call" | custom-call | tf_op jit(solution)/shard_map/pallas_call | solution.py:503
  2.0 0.2 reshape.28.own_ref
  2.2 3.0 %collective-permute-start.1 = (bf16[16,4608]{1,0:T(8,128)(2,1)S(1)}, bf16[16,4608]{1,0:T(8,128)(2,1)S(1)}, u32[]{:S(2)}, u32[]{:S(2)}) collective-permute-start(bf16[16,4608]{1,0:T(8,128)(2,1)S(1)} %reshape.28.own_ref), channel_id=1, source_target_pairs={{0,2},{2,0},{1,3},{3,1},{4,6},{6,4},{5,7},{7,5},{8,10},{10,8},{9,1... | collective-permute-start | bytes 442376 | tf_op jit(solution)/shard_map/ppermute | solution.py:425
  5.3 5.7 %read.1 = (bf16[1024,4608]{1,0:T(8,128)(2,1)S(1)}, bf16[512,2,8,384]{3,2,1,0:T(8,128)(2,1)S(1)}) custom-call(bf16[1024,4608]{1,0:T(8,128)(2,1)} %half_hbm.1, bf16[1024,6,8,384]{3,2,1,0:T(8,128)(2,1)} %bitcast.23), custom_call_target="tpu_custom_call" | custom-call | tf_op jit(solution)/shard_map/read/pallas_call | solution.py:245
  10.9 0.0 copy-start.2
  11.0 0.0 copy-start.1
  11.0 0.1 pad_add_fusion.place_ref.refs_0_
  11.0 0.0 collective-permute-done.1.received_ref
  11.0 3.1 %shard_map.65 = (f32[32,512]{1,0:T(8,128)S(1)}, f32[32,512]{1,0:T(8,128)S(1)}) custom-call(s32[3]{0:T(128)S(1)} %pad_add_fusion.place_ref.refs_0_, bf16[16,4608]{1,0:T(8,128)(2,1)S(1)} %reshape.28.own_ref, bf16[16,4608]{1,0:T(8,128)(2,1)S(1)} %collective-permute-done.1.received_ref, bf16[1024,4608]{1,0:T(8,128)(2,1)S(1)} %get-tuple-element.33.vectors_ref), custom_call_target="tpu_custom_call" | custom-call | tf_op jit(solution)/shard_map/pallas_call | solution.py:539
  14.2 0.1 collective-permute-start.2
  14.3 1.2 %collective-permute-done.2.right_ref = f32[32,512]{1,0:T(8,128)S(1)} collective-permute-done((f32[32,512]{1,0:T(8,128)S(1)}, f32[32,512]{1,0:T(8,128)S(1)}, u32[]{:S(2)}, u32[]{:S(2)}) %collective-permute-start.2) | collective-permute-done | bytes 65568 | tf_op jit(solution)/shard_map/ppermute | solution.py:425
  15.5 1.6 %collective-permute-start.3 = (bf16[32,512]{1,0:T(8,128)(2,1)S(1)}, bf16[32,512]{1,0:T(8,128)(2,1)S(1)}, u32[]{:S(2)}, u32[]{:S(2)}) collective-permute-start(bf16[32,512]{1,0:T(8,128)(2,1)S(1)} %get-tuple-element.37), channel_id=1, source_target_pairs={{0,4},{4,0},{8,12},{12,8},{1,5},{5,1},{9,13},{13,9},{2,6},{6,2},{1... | collective-permute-start | bytes 98312 | tf_op jit(solution)/shard_map/ppermute | solution.py:550
  17.1 2.3 %collective-permute-done.3.right_ref = bf16[32,512]{1,0:T(8,128)(2,1)S(1)} collective-permute-done((bf16[32,512]{1,0:T(8,128)(2,1)S(1)}, bf16[32,512]{1,0:T(8,128)(2,1)S(1)}, u32[]{:S(2)}, u32[]{:S(2)}) %collective-permute-start.3) | collective-permute-done | bytes 32800 | tf_op jit(solution)/shard_map/ppermute | solution.py:550
  19.5 2.6 %collective-permute-start.4 = (bf16[32,512]{1,0:T(8,128)(2,1)S(1)}, bf16[32,512]{1,0:T(8,128)(2,1)S(1)}, u32[]{:S(2)}, u32[]{:S(2)}) collective-permute-start(bf16[32,512]{1,0:T(8,128)(2,1)S(1)} %get-tuple-element.39), channel_id=1, source_target_pairs={{0,8},{4,12},{8,0},{12,4},{1,9},{5,13},{9,1},{13,5},{2,10},{6,14},... | collective-permute-start | bytes 98312 | tf_op jit(solution)/shard_map/ppermute | solution.py:550
  22.2 0.5 collective-permute-start
  22.7 3.0 %collective-permute-done.others_ref = s32[8]{0:T(128)S(1)} collective-permute-done((s32[8]{0:T(128)S(1)}, s32[8]{0:T(128)S(1)}, u32[]{:S(2)}, u32[]{:S(2)}) %collective-permute-start) | collective-permute-done | bytes 64 | tf_op jit(solution)/shard_map/ppermute | solution.py:425
  25.7 0.0 collective-permute-done.4.right_ref
  25.7 0.7 shard_map.68.refs_1_
  26.4 0.1 collective-permute-start.5
  26.5 2.9 %shard_map.69.refs_4_ = bf16[512,2,8,384]{3,2,1,0:T(8,128)(2,1)S(1)} custom-call(f32[32,512]{1,0:T(8,128)S(1)} %get-tuple-element.38.left_ref.order_ref, bf16[1024,6,8,384]{3,2,1,0:T(8,128)(2,1)} %bitcast.24), custom_call_target="tpu_custom_call" | custom-call | tf_op jit(solution)/shard_map/pallas_call | solution.py:557
  29.4 0.0 collective-permute-done.5.refs_2_
  29.4 7.2 %field.3 = (f32[16,16,384]{2,1,0:T(8,128)S(1)}, bf16[16,16,384]{2,1,0:T(8,128)(2,1)S(1)}, bf16[256,8192]{1,0:T(8,128)(2,1)S(1)}, bf16[512,2,8,384]{3,2,1,0:T(8,1...) custom-call(s32[3]{0:T(128)S(1)} %pad_add_fusion.place_ref.refs_0_, ...), custom_call_target="tpu_custom_call" | custom-call | flops 3221225472 | bytes 12582912 | tf_op jit(solution)/shard_map/field/pallas_call | solution.py:307
  36.6 0.6 collective-permute-start.6
  37.2 4.1 %field.4 = (f32[16,16,384]{2,1,0:T(8,128)S(1)}, bf16[16,16,384]{2,1,0:T(8,128)(2,1)S(1)}, bf16[512,2,8,384]{3,2,1,0:T(8,128)(2,1)S(1)}) custom-call(bf16[256,8192]{1,0:T(8,128)(2,1)S(1)} %get-tuple-element.42.refs_0_, bf16[512,2,8,384]{3,2,1,0:T(8,128)(2,1)S(1)} %get-tuple-element.43.refs_1_, bf16[512,2,8,384]{3,2,1,0:T(8,128)(2,1)S(1)} %get-tuple-element.44.refs_2_, ...), custom_call_target="tpu_custom_call" | custom-call | flops 3221225472 | bytes 12582912 | tf_op jit(solution)/shard_map/field/pallas_call | solution.py:307
  41.2 0.0 copy-start
  41.2 3.4 %field.5 = (f32[16,16,384]{2,1,0:T(8,128)S(1)}, bf16[16,16,384]{2,1,0:T(8,128)(2,1)S(1)}) custom-call(bf16[256,8192]{1,0:T(8,128)(2,1)S(1)} %get-tuple-element.42.refs_0_, bf16[512,2,8,384]{3,2,1,0:T(8,128)(2,1)S(1)} %get-tuple-element.46.refs_1_, bf16[512,2,8,384]{3,2,1,0:T(8,128)(2,1)S(1)} %get-tuple-element.47.refs_2_, bf16[1024,6,8,384]{3,2,1,0:T(8,128)(2,1)} %bitcast.27), custom_call_target="tpu_custom_call" | custom-call | flops 3221225472 | bytes 12582912 | tf_op jit(solution)/shard_map/field/pallas_call | solution.py:307
  44.7 1.5 %collective-permute-start.8 = (bf16[8,2,16,384]{3,2,1,0:T(8,128)(2,1)S(1)}, bf16[8,2,16,384]{3,2,1,0:T(8,128)(2,1)S(1)}, u32[]{:S(2)}, u32[]{:S(2)}) collective-permute-start(bf16[8,2,16,384]{3,2,1,0:T(8,128)(2,1)S(1)} %bitcast.22), channel_id=1, source_target_pairs={{0,2},{2,0},{1,3},{3,1},{4,6},{6,4},{5,7},{7,5},{8,10},{10,8},{9,1... | collective-permute-start | bytes 589832 | tf_op jit(solution)/shard_map/ppermute | solution.py:425
  46.2 0.5 collective-permute-start.7
  46.8 0.0 collective-permute-done.6.refs_3_
  46.8 5.7 %collective-permute-done.8.refs_5_ = bf16[8,2,16,384]{3,2,1,0:T(8,128)(2,1)S(1)} collective-permute-done((bf16[8,2,16,384]{3,2,1,0:T(8,128)(2,1)S(1)}, bf16[8,2,16,384]{3,2,1,0:T(8,128)(2,1)S(1)}, u32[]{:S(2)}, u32[]{:S(2)}) %collective-permute-start.8) | collective-permute-done | bytes 196640 | tf_op jit(solution)/shard_map/ppermute | solution.py:425
  52.5 3.5 %collective-permute-done.7.refs_4_ = bf16[8,2,16,384]{3,2,1,0:T(8,128)(2,1)S(1)} collective-permute-done((bf16[8,2,16,384]{3,2,1,0:T(8,128)(2,1)S(1)}, bf16[8,2,16,384]{3,2,1,0:T(8,128)(2,1)S(1)}, u32[]{:S(2)}, u32[]{:S(2)}) %collective-permute-start.7) | collective-permute-done | bytes 196640 | tf_op jit(solution)/shard_map/ppermute | solution.py:425
  56.0 1.0 combine.1
  57.0 3.8 %all-to-all-start = ((bf16[8,2,48,384]{3,2,1,0:T(8,128)(2,1)}), bf16[8,2,48,384]{3,2,1,0:T(8,128)(2,1)S(1)}, u32[]{:S(2)}, u32[]{:S(2)}) async-start(bf16[8,2,48,384]{3,2,1,0:T(8,128)(2,1)} %combine.1), calls=%async_computation | async-start | bytes 1179648 | tf_op jit(solution)/shard_map/all_to_all | solution.py:488
  60.7 1.6 %collective-permute-start.9 = (bf16[8,2,48,96]{3,2,1,0:T(8,128)(2,1)S(1)}, bf16[8,2,48,96]{3,2,1,0:T(8,128)(2,1)S(1)}, u32[]{:S(2)}, u32[]{:S(2)}) collective-permute-start(bf16[8,2,48,96]{3,2,1,0:T(8,128)(2,1)S(1)} %copy-done), channel_id=1, source_target_pairs={{0,2},{2,0},{1,3},{3,1},{4,6},{6,4},{5,7},{7,5},{8,10},{10,8},{9,1... | collective-permute-start | bytes 442376 | tf_op jit(solution)/shard_map/ppermute | solution.py:425
  62.3 5.8 %collective-permute-done.9.received_ref = bf16[8,2,48,96]{3,2,1,0:T(8,128)(2,1)S(1)} collective-permute-done((bf16[8,2,48,96]{3,2,1,0:T(8,128)(2,1)S(1)}, bf16[8,2,48,96]{3,2,1,0:T(8,128)(2,1)S(1)}, u32[]{:S(2)}, u32[]{:S(2)}) %collective-permute-start.9) | collective-permute-done | bytes 147488 | tf_op jit(solution)/shard_map/ppermute | solution.py:425
  68.0 0.7 shard_map.70
  68.7 0.1 collective-permute-start.10
  68.8 1.3 %collective-permute-done.10.received_ref = bf16[4,1,2,48,96]{4,3,2,1,0:T(8,128)(2,1)S(1)} collective-permute-done((bf16[4,1,2,48,96]{4,3,2,1,0:T(8,128)(2,1)S(1)}, bf16[4,1,2,48,96]{4,3,2,1,0:T(8,128)(2,1)S(1)}, u32[]{:S(2)}, u32[]{:S(2)}) %collective-permute-start.10) | collective-permute-done | bytes 73760 | tf_op jit(solution)/shard_map/ppermute | solution.py:425
  70.1 0.6 shard_map.71
  70.7 1.7 %collective-permute-start.11 = (bf16[2,2,2,48,96]{4,3,2,1,0:T(8,128)(2,1)S(1)}, bf16[2,2,2,48,96]{4,3,2,1,0:T(8,128)(2,1)S(1)}, u32[]{:S(2)}, u32[]{:S(2)}) collective-permute-start(bf16[2,2,2,48,96]{4,3,2,1,0:T(8,128)(2,1)S(1)} %get-tuple-element.56), channel_id=1, source_target_pairs={{0,4},{4,0},{8,12},{12,8},{1,5},{5,1},{9,13},{13,9},{2,6},{6,2},{1... | collective-permute-start | bytes 221192 | tf_op jit(solution)/shard_map/ppermute | solution.py:555
  72.4 5.3 %collective-permute-done.11.received_ref = bf16[2,2,2,48,96]{4,3,2,1,0:T(8,128)(2,1)S(1)} collective-permute-done((bf16[2,2,2,48,96]{4,3,2,1,0:T(8,128)(2,1)S(1)}, bf16[2,2,2,48,96]{4,3,2,1,0:T(8,128)(2,1)S(1)}, u32[]{:S(2)}, u32[]{:S(2)}) %collective-permute-start.11) | collective-permute-done | bytes 73760 | tf_op jit(solution)/shard_map/ppermute | solution.py:555
  77.7 0.6 shard_map.72
  78.3 1.2 %collective-permute-start.12 = (bf16[1,4,2,48,96]{4,3,2,1,0:T(8,128)(2,1)S(1)}, bf16[1,4,2,48,96]{4,3,2,1,0:T(8,128)(2,1)S(1)}, u32[]{:S(2)}, u32[]{:S(2)}) collective-permute-start(bf16[1,4,2,48,96]{4,3,2,1,0:T(8,128)(2,1)S(1)} %get-tuple-element.58), channel_id=1, source_target_pairs={{0,8},{4,12},{8,0},{12,4},{1,9},{5,13},{9,1},{13,5},{2,10},{6,14},... | collective-permute-start | bytes 221192 | tf_op jit(solution)/shard_map/ppermute | solution.py:555
  79.5 5.8 %collective-permute-done.12 = bf16[1,4,2,48,96]{4,3,2,1,0:T(8,128)(2,1)S(1)} collective-permute-done((bf16[1,4,2,48,96]{4,3,2,1,0:T(8,128)(2,1)S(1)}, bf16[1,4,2,48,96]{4,3,2,1,0:T(8,128)(2,1)S(1)}, u32[]{:S(2)}, u32[]{:S(2)}) %collective-permute-start.12) | collective-permute-done | bytes 73760 | tf_op jit(solution)/shard_map/ppermute | solution.py:555
  85.3 0.0 all-to-all-done.field_ref
  85.3 3.6 %shard_map.73 = bf16[8,2,48,96]{3,2,1,0:T(8,128)(2,1)S(1)} custom-call(s32[1]{0:T(128)} %bitcast.rank_ref, bf16[8,2,48,384]{3,2,1,0:T(8,128)(2,1)S(1)} %all-to-all-done.field_ref, bf16[4,2,48,96]{3,2,1,0:T(8,128)(2,1)S(1)} %bitcast.18, bf16[4,2,48,96]{3,2,1,0:T(8,128)(2,1)S(1)} %bitcast.19), custom_call_target="tpu_custom_call" | custom-call | tf_op jit(solution)/shard_map/pallas_call | solution.py:414
  88.9 12.1 %all_to_all.10.grid_ref = bf16[8,2,48,96]{3,2,1,0:T(8,128)(2,1)S(1)} all-to-all(bf16[8,2,48,96]{3,2,1,0:T(8,128)(2,1)S(1)} %shard_map.73), channel_id=1, replica_groups=mesh['groups'=2,'chol'=4,'walk'=2,'orb'=2] {'chol','orb'}, dimensions={0} | all-to-all | bytes 294912 | tf_op jit(solution)/shard_map/all_to_all | solution.py:623
  101.0 1.0 shard_map.74
  (5 shorter events, 0.0 us)
Async XLA Ops:
  2.2 8.8 %collective-permute-start.1 = (bf16[16,4608]{1,0:T(8,128)(2,1)S(1)}, bf16[16,4608]{1,0:T(8,128)(2,1)S(1)}, u32[]{:S(2)}, u32[]{:S(2)}) collective-permute-start(bf16[16,4608]{1,0:T(8,128)(2,1)S(1)} %reshape.28.own_ref), channel_id=1, source_target_pairs={{0,2},{2,0},{1,3},{3,1},{4,6},{6,4},{5,7},{7,5},{8,10},{10,8},{9,1... | collective-permute-start | bytes 442376 | tf_op jit(solution)/shard_map/ppermute | solution.py:425
  10.9 11.2 %copy-start.2 = (s32[8]{0:T(128)S(1)}, s32[8]{0:T(128)}, u32[]{:S(2)}) copy-start(s32[8]{0:T(128)} %source_ref.3) | copy-start | bytes 100
  11.0 14.8 %copy-start.1 = (f32[16,1024]{1,0:T(8,128)S(1)}, f32[16,1024]{1,0:T(8,128)}, u32[]{:S(2)}) copy-start(f32[16,1024]{1,0:T(8,128)} %samples_ref.1) | copy-start | bytes 196612
  14.2 1.3 %collective-permute-start.2 = (f32[32,512]{1,0:T(8,128)S(1)}, f32[32,512]{1,0:T(8,128)S(1)}, u32[]{:S(2)}, u32[]{:S(2)}) collective-permute-start(f32[32,512]{1,0:T(8,128)S(1)} %get-tuple-element.35), channel_id=1, source_target_pairs={{0,1},{1,0},{2,3},{3,2},{4,5},{5,4},{6,7},{7,6},{8,9},{9,8},{10,11... | collective-permute-start | bytes 196616 | tf_op jit(solution)/shard_map/ppermute | solution.py:425
  15.5 4.0 %collective-permute-start.3 = (bf16[32,512]{1,0:T(8,128)(2,1)S(1)}, bf16[32,512]{1,0:T(8,128)(2,1)S(1)}, u32[]{:S(2)}, u32[]{:S(2)}) collective-permute-start(bf16[32,512]{1,0:T(8,128)(2,1)S(1)} %get-tuple-element.37), channel_id=1, source_target_pairs={{0,4},{4,0},{8,12},{12,8},{1,5},{5,1},{9,13},{13,9},{2,6},{6,2},{1... | collective-permute-start | bytes 98312 | tf_op jit(solution)/shard_map/ppermute | solution.py:550
  19.5 6.2 %collective-permute-start.4 = (bf16[32,512]{1,0:T(8,128)(2,1)S(1)}, bf16[32,512]{1,0:T(8,128)(2,1)S(1)}, u32[]{:S(2)}, u32[]{:S(2)}) collective-permute-start(bf16[32,512]{1,0:T(8,128)(2,1)S(1)} %get-tuple-element.39), channel_id=1, source_target_pairs={{0,8},{4,12},{8,0},{12,4},{1,9},{5,13},{9,1},{13,5},{2,10},{6,14},... | collective-permute-start | bytes 98312 | tf_op jit(solution)/shard_map/ppermute | solution.py:550
  22.2 3.6 %collective-permute-start = (s32[8]{0:T(128)S(1)}, s32[8]{0:T(128)S(1)}, u32[]{:S(2)}, u32[]{:S(2)}) collective-permute-start(s32[8]{0:T(128)S(1)} %copy-done.2), channel_id=1, source_target_pairs={{0,2},{2,0},{1,3},{3,1},{4,6},{6,4},{5,7},{7,5},{8,10},{10,8},{9,1... | collective-permute-start | bytes 104 | tf_op jit(solution)/shard_map/ppermute | solution.py:425
  26.4 3.0 %collective-permute-start.5 = (bf16[32,512]{1,0:T(8,128)(2,1)S(1)}, bf16[32,512]{1,0:T(8,128)(2,1)S(1)}, u32[]{:S(2)}, u32[]{:S(2)}) collective-permute-start(bf16[32,512]{1,0:T(8,128)(2,1)S(1)} %shard_map.68.refs_1_), channel_id=1, source_target_pairs={{0,1},{1,0},{2,3},{3,2},{4,5},{5,4},{6,7},{7,6},{8,9},{9,8},{10,11... | collective-permute-start | bytes 98312 | tf_op jit(solution)/shard_map/ppermute | solution.py:425
  36.6 10.2 %collective-permute-start.6 = (bf16[8,2,16,384]{3,2,1,0:T(8,128)(2,1)S(1)}, bf16[8,2,16,384]{3,2,1,0:T(8,128)(2,1)S(1)}, u32[]{:S(2)}, u32[]{:S(2)}) collective-permute-start(bf16[8,2,16,384]{3,2,1,0:T(8,128)(2,1)S(1)} %bitcast.20), channel_id=1, source_target_pairs={{0,2},{2,0},{1,3},{3,1},{4,6},{6,4},{5,7},{7,5},{8,10},{10,8},{9,1... | collective-permute-start | bytes 589832 | tf_op jit(solution)/shard_map/ppermute | solution.py:425
  41.2 19.5 %copy-start = (bf16[8,2,48,96]{3,2,1,0:T(8,128)(2,1)S(1)}, bf16[8,2,48,96]{3,2,1,0:T(8,128)(2,1)}, u32[]{:S(2)}) copy-start(bf16[8,2,48,96]{3,2,1,0:T(8,128)(2,1)} %get-tuple-element.52.own_ref) | copy-start | bytes 442372
  44.7 7.8 %collective-permute-start.8 = (bf16[8,2,16,384]{3,2,1,0:T(8,128)(2,1)S(1)}, bf16[8,2,16,384]{3,2,1,0:T(8,128)(2,1)S(1)}, u32[]{:S(2)}, u32[]{:S(2)}) collective-permute-start(bf16[8,2,16,384]{3,2,1,0:T(8,128)(2,1)S(1)} %bitcast.22), channel_id=1, source_target_pairs={{0,2},{2,0},{1,3},{3,1},{4,6},{6,4},{5,7},{7,5},{8,10},{10,8},{9,1... | collective-permute-start | bytes 589832 | tf_op jit(solution)/shard_map/ppermute | solution.py:425
  46.2 9.7 %collective-permute-start.7 = (bf16[8,2,16,384]{3,2,1,0:T(8,128)(2,1)S(1)}, bf16[8,2,16,384]{3,2,1,0:T(8,128)(2,1)S(1)}, u32[]{:S(2)}, u32[]{:S(2)}) collective-permute-start(bf16[8,2,16,384]{3,2,1,0:T(8,128)(2,1)S(1)} %bitcast.21), channel_id=1, source_target_pairs={{0,2},{2,0},{1,3},{3,1},{4,6},{6,4},{5,7},{7,5},{8,10},{10,8},{9,1... | collective-permute-start | bytes 589832 | tf_op jit(solution)/shard_map/ppermute | solution.py:425
  57.0 28.4 %all-to-all-start = ((bf16[8,2,48,384]{3,2,1,0:T(8,128)(2,1)}), bf16[8,2,48,384]{3,2,1,0:T(8,128)(2,1)S(1)}, u32[]{:S(2)}, u32[]{:S(2)}) async-start(bf16[8,2,48,384]{3,2,1,0:T(8,128)(2,1)} %combine.1), calls=%async_computation | async-start | bytes 1179648 | tf_op jit(solution)/shard_map/all_to_all | solution.py:488
  60.7 7.3 %collective-permute-start.9 = (bf16[8,2,48,96]{3,2,1,0:T(8,128)(2,1)S(1)}, bf16[8,2,48,96]{3,2,1,0:T(8,128)(2,1)S(1)}, u32[]{:S(2)}, u32[]{:S(2)}) collective-permute-start(bf16[8,2,48,96]{3,2,1,0:T(8,128)(2,1)S(1)} %copy-done), channel_id=1, source_target_pairs={{0,2},{2,0},{1,3},{3,1},{4,6},{6,4},{5,7},{7,5},{8,10},{10,8},{9,1... | collective-permute-start | bytes 442376 | tf_op jit(solution)/shard_map/ppermute | solution.py:425
  68.7 1.4 %collective-permute-start.10 = (bf16[4,1,2,48,96]{4,3,2,1,0:T(8,128)(2,1)S(1)}, bf16[4,1,2,48,96]{4,3,2,1,0:T(8,128)(2,1)S(1)}, u32[]{:S(2)}, u32[]{:S(2)}) collective-permute-start(bf16[4,1,2,48,96]{4,3,2,1,0:T(8,128)(2,1)S(1)} %get-tuple-element.54), channel_id=1, source_target_pairs={{0,1},{1,0},{2,3},{3,2},{4,5},{5,4},{6,7},{7,6},{8,9},{9,8},{10,11... | collective-permute-start | bytes 221192 | tf_op jit(solution)/shard_map/ppermute | solution.py:425
  70.7 7.0 %collective-permute-start.11 = (bf16[2,2,2,48,96]{4,3,2,1,0:T(8,128)(2,1)S(1)}, bf16[2,2,2,48,96]{4,3,2,1,0:T(8,128)(2,1)S(1)}, u32[]{:S(2)}, u32[]{:S(2)}) collective-permute-start(bf16[2,2,2,48,96]{4,3,2,1,0:T(8,128)(2,1)S(1)} %get-tuple-element.56), channel_id=1, source_target_pairs={{0,4},{4,0},{8,12},{12,8},{1,5},{5,1},{9,13},{13,9},{2,6},{6,2},{1... | collective-permute-start | bytes 221192 | tf_op jit(solution)/shard_map/ppermute | solution.py:555
  78.3 7.0 %collective-permute-start.12 = (bf16[1,4,2,48,96]{4,3,2,1,0:T(8,128)(2,1)S(1)}, bf16[1,4,2,48,96]{4,3,2,1,0:T(8,128)(2,1)S(1)}, u32[]{:S(2)}, u32[]{:S(2)}) collective-permute-start(bf16[1,4,2,48,96]{4,3,2,1,0:T(8,128)(2,1)S(1)} %get-tuple-element.58), channel_id=1, source_target_pairs={{0,8},{4,12},{8,0},{12,4},{1,9},{5,13},{9,1},{13,5},{2,10},{6,14},... | collective-permute-start | bytes 221192 | tf_op jit(solution)/shard_map/ppermute | solution.py:555

commit v8 on v7

--- a/solution.py
+++ b/solution.py
@@ -281,7 +281,7 @@
         total = product if total is None else total + product
     for t in range(tiles):
         slab = total[:, t * orbitals : (t + 1) * orbitals].reshape(count, TILE, orbitals)
-        own_ref[:, t * TILE : (t + 1) * TILE] = slab[:mine]
+        own_ref[:, t * TILE : (t + 1) * TILE] = slab[:mine].astype(HALF)
         sent_ref[:, t * TILE : (t + 1) * TILE] = slab[mine:].astype(HALF)
     for copy in copies:
         copy.wait()
@@ -292,7 +292,7 @@
     vectors = 2 * height
     rows = tiles * TILE
     out_shape = [
-        jax.ShapeDtypeStruct((mine, rows, orbitals), FULL),
+        jax.ShapeDtypeStruct((mine, rows, orbitals), HALF),
         jax.ShapeDtypeStruct((count - mine, rows, orbitals), HALF),
     ]
     if part == 0:
@@ -327,7 +327,7 @@
     others = len(received_refs) // chunks
     rows = own_refs[0].shape[2]
     for c in range(chunks):
-        total = own_refs[c][...]
+        total = own_refs[c][...].astype(FULL)
         for received_ref in received_refs[c * others : (c + 1) * others]:
             total = total + received_ref[...].astype(FULL)
         out_ref[:, :, c * rows : (c + 1) * rows] = total.astype(HALF)

time: 102 us -> 102 us (level)
  transfers between devices with their start and end apart: 14 -> 14, of which waited for: 9 -> 9; matrix products, arithmetic and copies ran while one was open for 0% -> 0% of each run, Pallas kernels for 18% -> 17%
where the time goes in v8:
time: 102 us; the launch traced here: 101 us
  Pallas kernels  35.9 us (35%)
  waiting for transfers between devices  34 us (33%)
  starting transfers between devices  19 us (19%)
  blocking collectives  12.1 us (12%)
    ppermute x9, waiting for transfers between devices, shift(): lax.ppermute(value, axis, [(i, (i + step) % size) for i in range(size)])  20.5 us
    pallas_call x3, Pallas kernels, field_rows(): pl.pallas_call(functools.partial(field_kernel, part, wanted, mine), in_sp...  14.1 us
    all_to_all x1, blocking collectives, whole_step(): lax.all_to_all(normalized, ROWS, split_axis=0, concat_axis=0, tiled=True)  12.1 us
    ppermute x2, waiting for transfers between devices, whole_step(): passed = lax.ppermute(sent, 'chol', pairs)  11.2 us
    ppermute x9, starting transfers between devices, shift(): lax.ppermute(value, axis, [(i, (i + step) % size) for i in range(size)])  8.02 us
    pallas_call x1, Pallas kernels, read_early(): pl.pallas_call(read_kernel, in_specs=[pl.BlockSpec(memory_space=pl.ANY)]...  5.66 us
    ppermute x2, starting transfers between devices, whole_step(): received = lax.ppermute(rounded, 'chol', pairs)  4.29 us
    all_to_all x1, starting transfers between devices, to_owners(): return lax.all_to_all(value, ROWS, split_axis=0, concat_axis=0, tiled=True)  3.76 us
  transfers between devices with their start and end apart: 14, of which 9 were waited for; matrix products, arithmetic and copies ran while one was open for 0% of the time, Pallas kernels for 17%

profile of v8, /device:TPU:0, one launch (start us, length us, event | category | flops | bytes accessed | tf_op | source)
XLA Modules:
  0.0 101.5 jit_solution(5701972071928312168)
XLA Ops:
  0.0 2.0 %shard_map.64 = (bf16[8,2,48,96]{3,2,1,0:T(8,128)(2,1)S(1)}, bf16[8,2,48,96]{3,2,1,0:T(8,128)(2,1)}) custom-call(f32[8,2,4608]{2,1,0:T(2,128)} %walkers_hbm.1, f32[8,2,96,96]{3,2,1,0:T(8,128)} %inverse_hbm.1), custom_call_target="tpu_custom_call" | custom-call | tf_op jit(solution)/shard_map/pallas_call | solution.py:503
  2.0 0.2 reshape.28.own_ref
  2.2 3.0 %collective-permute-start.1 = (bf16[16,4608]{1,0:T(8,128)(2,1)S(1)}, bf16[16,4608]{1,0:T(8,128)(2,1)S(1)}, u32[]{:S(2)}, u32[]{:S(2)}) collective-permute-start(bf16[16,4608]{1,0:T(8,128)(2,1)S(1)} %reshape.28.own_ref), channel_id=1, source_target_pairs={{0,2},{2,0},{1,3},{3,1},{4,6},{6,4},{5,7},{7,5},{8,10},{10,8},{9,1... | collective-permute-start | bytes 442376 | tf_op jit(solution)/shard_map/ppermute | solution.py:425
  5.3 5.7 %read.1 = (bf16[1024,4608]{1,0:T(8,128)(2,1)S(1)}, bf16[512,2,8,384]{3,2,1,0:T(8,128)(2,1)S(1)}) custom-call(bf16[1024,4608]{1,0:T(8,128)(2,1)} %half_hbm.1, bf16[1024,6,8,384]{3,2,1,0:T(8,128)(2,1)} %bitcast.23), custom_call_target="tpu_custom_call" | custom-call | tf_op jit(solution)/shard_map/read/pallas_call | solution.py:245
  10.9 0.0 copy-start.2
  11.0 0.0 copy-start.1
  11.0 0.1 pad_add_fusion.place_ref.refs_0_
  11.0 0.0 collective-permute-done.1.received_ref
  11.0 3.1 %shard_map.65 = (f32[32,512]{1,0:T(8,128)S(1)}, f32[32,512]{1,0:T(8,128)S(1)}) custom-call(s32[3]{0:T(128)S(1)} %pad_add_fusion.place_ref.refs_0_, bf16[16,4608]{1,0:T(8,128)(2,1)S(1)} %reshape.28.own_ref, bf16[16,4608]{1,0:T(8,128)(2,1)S(1)} %collective-permute-done.1.received_ref, bf16[1024,4608]{1,0:T(8,128)(2,1)S(1)} %get-tuple-element.33.vectors_ref), custom_call_target="tpu_custom_call" | custom-call | tf_op jit(solution)/shard_map/pallas_call | solution.py:539
  14.2 0.1 collective-permute-start.2
  14.3 1.2 %collective-permute-done.2.right_ref = f32[32,512]{1,0:T(8,128)S(1)} collective-permute-done((f32[32,512]{1,0:T(8,128)S(1)}, f32[32,512]{1,0:T(8,128)S(1)}, u32[]{:S(2)}, u32[]{:S(2)}) %collective-permute-start.2) | collective-permute-done | bytes 65568 | tf_op jit(solution)/shard_map/ppermute | solution.py:425
  15.5 1.6 %collective-permute-start.3 = (bf16[32,512]{1,0:T(8,128)(2,1)S(1)}, bf16[32,512]{1,0:T(8,128)(2,1)S(1)}, u32[]{:S(2)}, u32[]{:S(2)}) collective-permute-start(bf16[32,512]{1,0:T(8,128)(2,1)S(1)} %get-tuple-element.37), channel_id=1, source_target_pairs={{0,4},{4,0},{8,12},{12,8},{1,5},{5,1},{9,13},{13,9},{2,6},{6,2},{1... | collective-permute-start | bytes 98312 | tf_op jit(solution)/shard_map/ppermute | solution.py:550
  17.1 2.3 %collective-permute-done.3.right_ref = bf16[32,512]{1,0:T(8,128)(2,1)S(1)} collective-permute-done((bf16[32,512]{1,0:T(8,128)(2,1)S(1)}, bf16[32,512]{1,0:T(8,128)(2,1)S(1)}, u32[]{:S(2)}, u32[]{:S(2)}) %collective-permute-start.3) | collective-permute-done | bytes 32800 | tf_op jit(solution)/shard_map/ppermute | solution.py:550
  19.5 2.6 %collective-permute-start.4 = (bf16[32,512]{1,0:T(8,128)(2,1)S(1)}, bf16[32,512]{1,0:T(8,128)(2,1)S(1)}, u32[]{:S(2)}, u32[]{:S(2)}) collective-permute-start(bf16[32,512]{1,0:T(8,128)(2,1)S(1)} %get-tuple-element.39), channel_id=1, source_target_pairs={{0,8},{4,12},{8,0},{12,4},{1,9},{5,13},{9,1},{13,5},{2,10},{6,14},... | collective-permute-start | bytes 98312 | tf_op jit(solution)/shard_map/ppermute | solution.py:550
  22.2 0.5 collective-permute-start
  22.7 3.0 %collective-permute-done.others_ref = s32[8]{0:T(128)S(1)} collective-permute-done((s32[8]{0:T(128)S(1)}, s32[8]{0:T(128)S(1)}, u32[]{:S(2)}, u32[]{:S(2)}) %collective-permute-start) | collective-permute-done | bytes 64 | tf_op jit(solution)/shard_map/ppermute | solution.py:425
  25.7 0.0 collective-permute-done.4.right_ref
  25.7 0.7 shard_map.68.refs_1_
  26.4 0.1 collective-permute-start.5
  26.5 2.9 %shard_map.69.refs_4_ = bf16[512,2,8,384]{3,2,1,0:T(8,128)(2,1)S(1)} custom-call(f32[32,512]{1,0:T(8,128)S(1)} %get-tuple-element.38.left_ref.order_ref, bf16[1024,6,8,384]{3,2,1,0:T(8,128)(2,1)} %bitcast.24), custom_call_target="tpu_custom_call" | custom-call | tf_op jit(solution)/shard_map/pallas_call | solution.py:557
  29.4 0.0 collective-permute-done.5.refs_2_
  29.4 7.2 %field.3 = (bf16[16,16,384]{2,1,0:T(8,128)(2,1)S(1)}, bf16[16,16,384]{2,1,0:T(8,128)(2,1)S(1)}, bf16[256,8192]{1,0:T(8,128)(2,1)S(1)}, bf16[512,2,8,384]{3,2,1,0...) custom-call(s32[3]{0:T(128)S(1)} %pad_add_fusion.place_ref.refs_0_, ...), custom_call_target="tpu_custom_call" | custom-call | flops 3221225472 | bytes 12582912 | tf_op jit(solution)/shard_map/field/pallas_call | solution.py:307
  36.6 0.6 collective-permute-start.6
  37.2 3.5 %field.4 = (bf16[16,16,384]{2,1,0:T(8,128)(2,1)S(1)}, bf16[16,16,384]{2,1,0:T(8,128)(2,1)S(1)}, bf16[512,2,8,384]{3,2,1,0:T(8,128)(2,1)S(1)}) custom-call(bf16[256,8192]{1,0:T(8,128)(2,1)S(1)} %get-tuple-element.42.refs_0_, bf16[512,2,8,384]{3,2,1,0:T(8,128)(2,1)S(1)} %get-tuple-element.43.refs_1_, bf16[512,2,8,384]{3,2,1,0:T(8,128)(2,1)S(1)} %get-tuple-element.44.refs_2_, ...), custom_call_target="tpu_custom_call" | custom-call | flops 3221225472 | bytes 12582912 | tf_op jit(solution)/shard_map/field/pallas_call | solution.py:307
  40.6 0.0 copy-start
  40.7 3.4 %field.5 = (bf16[16,16,384]{2,1,0:T(8,128)(2,1)S(1)}, bf16[16,16,384]{2,1,0:T(8,128)(2,1)S(1)}) custom-call(bf16[256,8192]{1,0:T(8,128)(2,1)S(1)} %get-tuple-element.42.refs_0_, bf16[512,2,8,384]{3,2,1,0:T(8,128)(2,1)S(1)} %get-tuple-element.46.refs_1_, bf16[512,2,8,384]{3,2,1,0:T(8,128)(2,1)S(1)} %get-tuple-element.47.refs_2_, ...), custom_call_target="tpu_custom_call" | custom-call | flops 3221225472 | bytes 12582912 | tf_op jit(solution)/shard_map/field/pallas_call | solution.py:307
  44.1 1.5 %collective-permute-start.8 = (bf16[8,2,16,384]{3,2,1,0:T(8,128)(2,1)S(1)}, bf16[8,2,16,384]{3,2,1,0:T(8,128)(2,1)S(1)}, u32[]{:S(2)}, u32[]{:S(2)}) collective-permute-start(bf16[8,2,16,384]{3,2,1,0:T(8,128)(2,1)S(1)} %bitcast.22), channel_id=1, source_target_pairs={{0,2},{2,0},{1,3},{3,1},{4,6},{6,4},{5,7},{7,5},{8,10},{10,8},{9,1... | collective-permute-start | bytes 589832 | tf_op jit(solution)/shard_map/ppermute | solution.py:425
  45.7 0.5 collective-permute-start.7
  46.2 0.0 collective-permute-done.6.refs_3_
  46.2 5.7 %collective-permute-done.8.refs_5_ = bf16[8,2,16,384]{3,2,1,0:T(8,128)(2,1)S(1)} collective-permute-done((bf16[8,2,16,384]{3,2,1,0:T(8,128)(2,1)S(1)}, bf16[8,2,16,384]{3,2,1,0:T(8,128)(2,1)S(1)}, u32[]{:S(2)}, u32[]{:S(2)}) %collective-permute-start.8) | collective-permute-done | bytes 196640 | tf_op jit(solution)/shard_map/ppermute | solution.py:425
  52.0 3.5 %collective-permute-done.7.refs_4_ = bf16[8,2,16,384]{3,2,1,0:T(8,128)(2,1)S(1)} collective-permute-done((bf16[8,2,16,384]{3,2,1,0:T(8,128)(2,1)S(1)}, bf16[8,2,16,384]{3,2,1,0:T(8,128)(2,1)S(1)}, u32[]{:S(2)}, u32[]{:S(2)}) %collective-permute-start.7) | collective-permute-done | bytes 196640 | tf_op jit(solution)/shard_map/ppermute | solution.py:425
  55.4 1.0 combine.1
  56.4 3.8 %all-to-all-start = ((bf16[8,2,48,384]{3,2,1,0:T(8,128)(2,1)}), bf16[8,2,48,384]{3,2,1,0:T(8,128)(2,1)S(1)}, u32[]{:S(2)}, u32[]{:S(2)}) async-start(bf16[8,2,48,384]{3,2,1,0:T(8,128)(2,1)} %combine.1), calls=%async_computation | async-start | bytes 1179648 | tf_op jit(solution)/shard_map/all_to_all | solution.py:488
  60.2 1.5 %collective-permute-start.9 = (bf16[8,2,48,96]{3,2,1,0:T(8,128)(2,1)S(1)}, bf16[8,2,48,96]{3,2,1,0:T(8,128)(2,1)S(1)}, u32[]{:S(2)}, u32[]{:S(2)}) collective-permute-start(bf16[8,2,48,96]{3,2,1,0:T(8,128)(2,1)S(1)} %copy-done), channel_id=1, source_target_pairs={{0,2},{2,0},{1,3},{3,1},{4,6},{6,4},{5,7},{7,5},{8,10},{10,8},{9,1... | collective-permute-start | bytes 442376 | tf_op jit(solution)/shard_map/ppermute | solution.py:425
  61.7 5.8 %collective-permute-done.9.received_ref = bf16[8,2,48,96]{3,2,1,0:T(8,128)(2,1)S(1)} collective-permute-done((bf16[8,2,48,96]{3,2,1,0:T(8,128)(2,1)S(1)}, bf16[8,2,48,96]{3,2,1,0:T(8,128)(2,1)S(1)}, u32[]{:S(2)}, u32[]{:S(2)}) %collective-permute-start.9) | collective-permute-done | bytes 147488 | tf_op jit(solution)/shard_map/ppermute | solution.py:425
  67.5 0.7 shard_map.70
  68.2 0.1 collective-permute-start.10
  68.2 1.3 %collective-permute-done.10.received_ref = bf16[4,1,2,48,96]{4,3,2,1,0:T(8,128)(2,1)S(1)} collective-permute-done((bf16[4,1,2,48,96]{4,3,2,1,0:T(8,128)(2,1)S(1)}, bf16[4,1,2,48,96]{4,3,2,1,0:T(8,128)(2,1)S(1)}, u32[]{:S(2)}, u32[]{:S(2)}) %collective-permute-start.10) | collective-permute-done | bytes 73760 | tf_op jit(solution)/shard_map/ppermute | solution.py:425
  69.5 0.6 shard_map.71
  70.1 1.7 %collective-permute-start.11 = (bf16[2,2,2,48,96]{4,3,2,1,0:T(8,128)(2,1)S(1)}, bf16[2,2,2,48,96]{4,3,2,1,0:T(8,128)(2,1)S(1)}, u32[]{:S(2)}, u32[]{:S(2)}) collective-permute-start(bf16[2,2,2,48,96]{4,3,2,1,0:T(8,128)(2,1)S(1)} %get-tuple-element.56), channel_id=1, source_target_pairs={{0,4},{4,0},{8,12},{12,8},{1,5},{5,1},{9,13},{13,9},{2,6},{6,2},{1... | collective-permute-start | bytes 221192 | tf_op jit(solution)/shard_map/ppermute | solution.py:555
  71.8 5.3 %collective-permute-done.11.received_ref = bf16[2,2,2,48,96]{4,3,2,1,0:T(8,128)(2,1)S(1)} collective-permute-done((bf16[2,2,2,48,96]{4,3,2,1,0:T(8,128)(2,1)S(1)}, bf16[2,2,2,48,96]{4,3,2,1,0:T(8,128)(2,1)S(1)}, u32[]{:S(2)}, u32[]{:S(2)}) %collective-permute-start.11) | collective-permute-done | bytes 73760 | tf_op jit(solution)/shard_map/ppermute | solution.py:555
  77.1 0.6 shard_map.72
  77.7 1.2 %collective-permute-start.12 = (bf16[1,4,2,48,96]{4,3,2,1,0:T(8,128)(2,1)S(1)}, bf16[1,4,2,48,96]{4,3,2,1,0:T(8,128)(2,1)S(1)}, u32[]{:S(2)}, u32[]{:S(2)}) collective-permute-start(bf16[1,4,2,48,96]{4,3,2,1,0:T(8,128)(2,1)S(1)} %get-tuple-element.58), channel_id=1, source_target_pairs={{0,8},{4,12},{8,0},{12,4},{1,9},{5,13},{9,1},{13,5},{2,10},{6,14},... | collective-permute-start | bytes 221192 | tf_op jit(solution)/shard_map/ppermute | solution.py:555
  78.9 5.8 %collective-permute-done.12 = bf16[1,4,2,48,96]{4,3,2,1,0:T(8,128)(2,1)S(1)} collective-permute-done((bf16[1,4,2,48,96]{4,3,2,1,0:T(8,128)(2,1)S(1)}, bf16[1,4,2,48,96]{4,3,2,1,0:T(8,128)(2,1)S(1)}, u32[]{:S(2)}, u32[]{:S(2)}) %collective-permute-start.12) | collective-permute-done | bytes 73760 | tf_op jit(solution)/shard_map/ppermute | solution.py:555
  84.8 0.0 all-to-all-done.field_ref
  84.8 3.6 %shard_map.73 = bf16[8,2,48,96]{3,2,1,0:T(8,128)(2,1)S(1)} custom-call(s32[1]{0:T(128)} %bitcast.rank_ref, bf16[8,2,48,384]{3,2,1,0:T(8,128)(2,1)S(1)} %all-to-all-done.field_ref, bf16[4,2,48,96]{3,2,1,0:T(8,128)(2,1)S(1)} %bitcast.18, bf16[4,2,48,96]{3,2,1,0:T(8,128)(2,1)S(1)} %bitcast.19), custom_call_target="tpu_custom_call" | custom-call | tf_op jit(solution)/shard_map/pallas_call | solution.py:414
  88.4 12.1 %all_to_all.10.grid_ref = bf16[8,2,48,96]{3,2,1,0:T(8,128)(2,1)S(1)} all-to-all(bf16[8,2,48,96]{3,2,1,0:T(8,128)(2,1)S(1)} %shard_map.73), channel_id=1, replica_groups=mesh['groups'=2,'chol'=4,'walk'=2,'orb'=2] {'chol','orb'}, dimensions={0} | all-to-all | bytes 294912 | tf_op jit(solution)/shard_map/all_to_all | solution.py:623
  100.5 1.0 shard_map.74
  (5 shorter events, 0.0 us)
Async XLA Ops:
  2.2 8.8 %collective-permute-start.1 = (bf16[16,4608]{1,0:T(8,128)(2,1)S(1)}, bf16[16,4608]{1,0:T(8,128)(2,1)S(1)}, u32[]{:S(2)}, u32[]{:S(2)}) collective-permute-start(bf16[16,4608]{1,0:T(8,128)(2,1)S(1)} %reshape.28.own_ref), channel_id=1, source_target_pairs={{0,2},{2,0},{1,3},{3,1},{4,6},{6,4},{5,7},{7,5},{8,10},{10,8},{9,1... | collective-permute-start | bytes 442376 | tf_op jit(solution)/shard_map/ppermute | solution.py:425
  10.9 11.2 %copy-start.2 = (s32[8]{0:T(128)S(1)}, s32[8]{0:T(128)}, u32[]{:S(2)}) copy-start(s32[8]{0:T(128)} %source_ref.3) | copy-start | bytes 100
  11.0 14.8 %copy-start.1 = (f32[16,1024]{1,0:T(8,128)S(1)}, f32[16,1024]{1,0:T(8,128)}, u32[]{:S(2)}) copy-start(f32[16,1024]{1,0:T(8,128)} %samples_ref.1) | copy-start | bytes 196612
  14.2 1.3 %collective-permute-start.2 = (f32[32,512]{1,0:T(8,128)S(1)}, f32[32,512]{1,0:T(8,128)S(1)}, u32[]{:S(2)}, u32[]{:S(2)}) collective-permute-start(f32[32,512]{1,0:T(8,128)S(1)} %get-tuple-element.35), channel_id=1, source_target_pairs={{0,1},{1,0},{2,3},{3,2},{4,5},{5,4},{6,7},{7,6},{8,9},{9,8},{10,11... | collective-permute-start | bytes 196616 | tf_op jit(solution)/shard_map/ppermute | solution.py:425
  15.5 4.0 %collective-permute-start.3 = (bf16[32,512]{1,0:T(8,128)(2,1)S(1)}, bf16[32,512]{1,0:T(8,128)(2,1)S(1)}, u32[]{:S(2)}, u32[]{:S(2)}) collective-permute-start(bf16[32,512]{1,0:T(8,128)(2,1)S(1)} %get-tuple-element.37), channel_id=1, source_target_pairs={{0,4},{4,0},{8,12},{12,8},{1,5},{5,1},{9,13},{13,9},{2,6},{6,2},{1... | collective-permute-start | bytes 98312 | tf_op jit(solution)/shard_map/ppermute | solution.py:550
  19.5 6.2 %collective-permute-start.4 = (bf16[32,512]{1,0:T(8,128)(2,1)S(1)}, bf16[32,512]{1,0:T(8,128)(2,1)S(1)}, u32[]{:S(2)}, u32[]{:S(2)}) collective-permute-start(bf16[32,512]{1,0:T(8,128)(2,1)S(1)} %get-tuple-element.39), channel_id=1, source_target_pairs={{0,8},{4,12},{8,0},{12,4},{1,9},{5,13},{9,1},{13,5},{2,10},{6,14},... | collective-permute-start | bytes 98312 | tf_op jit(solution)/shard_map/ppermute | solution.py:550
  22.2 3.6 %collective-permute-start = (s32[8]{0:T(128)S(1)}, s32[8]{0:T(128)S(1)}, u32[]{:S(2)}, u32[]{:S(2)}) collective-permute-start(s32[8]{0:T(128)S(1)} %copy-done.2), channel_id=1, source_target_pairs={{0,2},{2,0},{1,3},{3,1},{4,6},{6,4},{5,7},{7,5},{8,10},{10,8},{9,1... | collective-permute-start | bytes 104 | tf_op jit(solution)/shard_map/ppermute | solution.py:425
  26.4 3.0 %collective-permute-start.5 = (bf16[32,512]{1,0:T(8,128)(2,1)S(1)}, bf16[32,512]{1,0:T(8,128)(2,1)S(1)}, u32[]{:S(2)}, u32[]{:S(2)}) collective-permute-start(bf16[32,512]{1,0:T(8,128)(2,1)S(1)} %shard_map.68.refs_1_), channel_id=1, source_target_pairs={{0,1},{1,0},{2,3},{3,2},{4,5},{5,4},{6,7},{7,6},{8,9},{9,8},{10,11... | collective-permute-start | bytes 98312 | tf_op jit(solution)/shard_map/ppermute | solution.py:425
  36.6 9.6 %collective-permute-start.6 = (bf16[8,2,16,384]{3,2,1,0:T(8,128)(2,1)S(1)}, bf16[8,2,16,384]{3,2,1,0:T(8,128)(2,1)S(1)}, u32[]{:S(2)}, u32[]{:S(2)}) collective-permute-start(bf16[8,2,16,384]{3,2,1,0:T(8,128)(2,1)S(1)} %bitcast.20), channel_id=1, source_target_pairs={{0,2},{2,0},{1,3},{3,1},{4,6},{6,4},{5,7},{7,5},{8,10},{10,8},{9,1... | collective-permute-start | bytes 589832 | tf_op jit(solution)/shard_map/ppermute | solution.py:425
  40.6 19.5 %copy-start = (bf16[8,2,48,96]{3,2,1,0:T(8,128)(2,1)S(1)}, bf16[8,2,48,96]{3,2,1,0:T(8,128)(2,1)}, u32[]{:S(2)}) copy-start(bf16[8,2,48,96]{3,2,1,0:T(8,128)(2,1)} %get-tuple-element.52.own_ref) | copy-start | bytes 442372
  44.1 7.8 %collective-permute-start.8 = (bf16[8,2,16,384]{3,2,1,0:T(8,128)(2,1)S(1)}, bf16[8,2,16,384]{3,2,1,0:T(8,128)(2,1)S(1)}, u32[]{:S(2)}, u32[]{:S(2)}) collective-permute-start(bf16[8,2,16,384]{3,2,1,0:T(8,128)(2,1)S(1)} %bitcast.22), channel_id=1, source_target_pairs={{0,2},{2,0},{1,3},{3,1},{4,6},{6,4},{5,7},{7,5},{8,10},{10,8},{9,1... | collective-permute-start | bytes 589832 | tf_op jit(solution)/shard_map/ppermute | solution.py:425
  45.7 9.7 %collective-permute-start.7 = (bf16[8,2,16,384]{3,2,1,0:T(8,128)(2,1)S(1)}, bf16[8,2,16,384]{3,2,1,0:T(8,128)(2,1)S(1)}, u32[]{:S(2)}, u32[]{:S(2)}) collective-permute-start(bf16[8,2,16,384]{3,2,1,0:T(8,128)(2,1)S(1)} %bitcast.21), channel_id=1, source_target_pairs={{0,2},{2,0},{1,3},{3,1},{4,6},{6,4},{5,7},{7,5},{8,10},{10,8},{9,1... | collective-permute-start | bytes 589832 | tf_op jit(solution)/shard_map/ppermute | solution.py:425
  56.4 28.4 %all-to-all-start = ((bf16[8,2,48,384]{3,2,1,0:T(8,128)(2,1)}), bf16[8,2,48,384]{3,2,1,0:T(8,128)(2,1)S(1)}, u32[]{:S(2)}, u32[]{:S(2)}) async-start(bf16[8,2,48,384]{3,2,1,0:T(8,128)(2,1)} %combine.1), calls=%async_computation | async-start | bytes 1179648 | tf_op jit(solution)/shard_map/all_to_all | solution.py:488
  60.2 7.3 %collective-permute-start.9 = (bf16[8,2,48,96]{3,2,1,0:T(8,128)(2,1)S(1)}, bf16[8,2,48,96]{3,2,1,0:T(8,128)(2,1)S(1)}, u32[]{:S(2)}, u32[]{:S(2)}) collective-permute-start(bf16[8,2,48,96]{3,2,1,0:T(8,128)(2,1)S(1)} %copy-done), channel_id=1, source_target_pairs={{0,2},{2,0},{1,3},{3,1},{4,6},{6,4},{5,7},{7,5},{8,10},{10,8},{9,1... | collective-permute-start | bytes 442376 | tf_op jit(solution)/shard_map/ppermute | solution.py:425
  68.2 1.4 %collective-permute-start.10 = (bf16[4,1,2,48,96]{4,3,2,1,0:T(8,128)(2,1)S(1)}, bf16[4,1,2,48,96]{4,3,2,1,0:T(8,128)(2,1)S(1)}, u32[]{:S(2)}, u32[]{:S(2)}) collective-permute-start(bf16[4,1,2,48,96]{4,3,2,1,0:T(8,128)(2,1)S(1)} %get-tuple-element.54), channel_id=1, source_target_pairs={{0,1},{1,0},{2,3},{3,2},{4,5},{5,4},{6,7},{7,6},{8,9},{9,8},{10,11... | collective-permute-start | bytes 221192 | tf_op jit(solution)/shard_map/ppermute | solution.py:425
  70.1 7.0 %collective-permute-start.11 = (bf16[2,2,2,48,96]{4,3,2,1,0:T(8,128)(2,1)S(1)}, bf16[2,2,2,48,96]{4,3,2,1,0:T(8,128)(2,1)S(1)}, u32[]{:S(2)}, u32[]{:S(2)}) collective-permute-start(bf16[2,2,2,48,96]{4,3,2,1,0:T(8,128)(2,1)S(1)} %get-tuple-element.56), channel_id=1, source_target_pairs={{0,4},{4,0},{8,12},{12,8},{1,5},{5,1},{9,13},{13,9},{2,6},{6,2},{1... | collective-permute-start | bytes 221192 | tf_op jit(solution)/shard_map/ppermute | solution.py:555
  77.7 7.0 %collective-permute-start.12 = (bf16[1,4,2,48,96]{4,3,2,1,0:T(8,128)(2,1)S(1)}, bf16[1,4,2,48,96]{4,3,2,1,0:T(8,128)(2,1)S(1)}, u32[]{:S(2)}, u32[]{:S(2)}) collective-permute-start(bf16[1,4,2,48,96]{4,3,2,1,0:T(8,128)(2,1)S(1)} %get-tuple-element.58), channel_id=1, source_target_pairs={{0,8},{4,12},{8,0},{12,4},{1,9},{5,13},{9,1},{13,5},{2,10},{6,14},... | collective-permute-start | bytes 221192 | tf_op jit(solution)/shard_map/ppermute | solution.py:555

commit v9 on v8

--- a/solution.py
+++ b/solution.py
@@ -185,8 +185,10 @@
 def start_reading(pairs, semaphores):
     copies = []
     for source_ref, target_ref in pairs:
-        for block in range(target_ref.shape[0] // LANES):
-            group = pl.ds(block * LANES, LANES)
+        height = target_ref.shape[0]
+        size = 2 * LANES if height % (2 * LANES) == 0 else LANES
+        for block in range(height // size):
+            group = pl.ds(block * size, size)
             semaphore = semaphores.at[len(copies)]
             copy = pltpu.make_async_copy(source_ref.at[group], target_ref.at[group], semaphore)
             copy.start()

time: 102 us -> 102 us (level)
  no operation moved by 1% of the time
where the time goes in v9:
time: 102 us; the launch traced here: 101 us
  Pallas kernels  35.9 us (35%)
  waiting for transfers between devices  34 us (33%)
  starting transfers between devices  19 us (19%)
  blocking collectives  12.1 us (12%)
    ppermute x9, waiting for transfers between devices, shift(): lax.ppermute(value, axis, [(i, (i + step) % size) for i in range(size)])  20.5 us
    pallas_call x3, Pallas kernels, field_rows(): pl.pallas_call(functools.partial(field_kernel, part, wanted, mine), in_sp...  14.1 us
    all_to_all x1, blocking collectives, whole_step(): lax.all_to_all(normalized, ROWS, split_axis=0, concat_axis=0, tiled=True)  12.1 us
    ppermute x2, waiting for transfers between devices, whole_step(): passed = lax.ppermute(sent, 'chol', pairs)  11.2 us
    ppermute x9, starting transfers between devices, shift(): lax.ppermute(value, axis, [(i, (i + step) % size) for i in range(size)])  8 us
    pallas_call x1, Pallas kernels, read_early(): pl.pallas_call(read_kernel, in_specs=[pl.BlockSpec(memory_space=pl.ANY)]...  5.67 us
    ppermute x2, starting transfers between devices, whole_step(): received = lax.ppermute(rounded, 'chol', pairs)  4.31 us
    all_to_all x1, starting transfers between devices, to_owners(): return lax.all_to_all(value, ROWS, split_axis=0, concat_axis=0, tiled=True)  3.76 us
  transfers between devices with their start and end apart: 14, of which 9 were waited for; matrix products, arithmetic and copies ran while one was open for 0% of the time, Pallas kernels for 17%

profile of v9, /device:TPU:0, one launch (start us, length us, event | category | flops | bytes accessed | tf_op | source)
XLA Modules:
  0.0 101.5 jit_solution(3066710044506134149)
XLA Ops:
  0.0 2.0 %shard_map.64 = (bf16[8,2,48,96]{3,2,1,0:T(8,128)(2,1)S(1)}, bf16[8,2,48,96]{3,2,1,0:T(8,128)(2,1)}) custom-call(f32[8,2,4608]{2,1,0:T(2,128)} %walkers_hbm.1, f32[8,2,96,96]{3,2,1,0:T(8,128)} %inverse_hbm.1), custom_call_target="tpu_custom_call" | custom-call | tf_op jit(solution)/shard_map/pallas_call | solution.py:505
  2.0 0.2 reshape.28.own_ref
  2.2 3.0 %collective-permute-start.1 = (bf16[16,4608]{1,0:T(8,128)(2,1)S(1)}, bf16[16,4608]{1,0:T(8,128)(2,1)S(1)}, u32[]{:S(2)}, u32[]{:S(2)}) collective-permute-start(bf16[16,4608]{1,0:T(8,128)(2,1)S(1)} %reshape.28.own_ref), channel_id=1, source_target_pairs={{0,2},{2,0},{1,3},{3,1},{4,6},{6,4},{5,7},{7,5},{8,10},{10,8},{9,1... | collective-permute-start | bytes 442376 | tf_op jit(solution)/shard_map/ppermute | solution.py:427
  5.3 5.7 %read.1 = (bf16[1024,4608]{1,0:T(8,128)(2,1)S(1)}, bf16[512,2,8,384]{3,2,1,0:T(8,128)(2,1)S(1)}) custom-call(bf16[1024,4608]{1,0:T(8,128)(2,1)} %half_hbm.1, bf16[1024,6,8,384]{3,2,1,0:T(8,128)(2,1)} %bitcast.23), custom_call_target="tpu_custom_call" | custom-call | tf_op jit(solution)/shard_map/read/pallas_call | solution.py:247
  11.0 0.0 copy-start.2
  11.0 0.0 copy-start.1
  11.0 0.1 pad_add_fusion.place_ref.refs_0_
  11.1 0.0 collective-permute-done.1.received_ref
  11.1 3.1 %shard_map.65 = (f32[32,512]{1,0:T(8,128)S(1)}, f32[32,512]{1,0:T(8,128)S(1)}) custom-call(s32[3]{0:T(128)S(1)} %pad_add_fusion.place_ref.refs_0_, bf16[16,4608]{1,0:T(8,128)(2,1)S(1)} %reshape.28.own_ref, bf16[16,4608]{1,0:T(8,128)(2,1)S(1)} %collective-permute-done.1.received_ref, bf16[1024,4608]{1,0:T(8,128)(2,1)S(1)} %get-tuple-element.33.vectors_ref), custom_call_target="tpu_custom_call" | custom-call | tf_op jit(solution)/shard_map/pallas_call | solution.py:541
  14.2 0.1 collective-permute-start.2
  14.3 1.2 %collective-permute-done.2.right_ref = f32[32,512]{1,0:T(8,128)S(1)} collective-permute-done((f32[32,512]{1,0:T(8,128)S(1)}, f32[32,512]{1,0:T(8,128)S(1)}, u32[]{:S(2)}, u32[]{:S(2)}) %collective-permute-start.2) | collective-permute-done | bytes 65568 | tf_op jit(solution)/shard_map/ppermute | solution.py:427
  15.5 1.6 %collective-permute-start.3 = (bf16[32,512]{1,0:T(8,128)(2,1)S(1)}, bf16[32,512]{1,0:T(8,128)(2,1)S(1)}, u32[]{:S(2)}, u32[]{:S(2)}) collective-permute-start(bf16[32,512]{1,0:T(8,128)(2,1)S(1)} %get-tuple-element.37), channel_id=1, source_target_pairs={{0,4},{4,0},{8,12},{12,8},{1,5},{5,1},{9,13},{13,9},{2,6},{6,2},{1... | collective-permute-start | bytes 98312 | tf_op jit(solution)/shard_map/ppermute | solution.py:552
  17.2 2.3 %collective-permute-done.3.right_ref = bf16[32,512]{1,0:T(8,128)(2,1)S(1)} collective-permute-done((bf16[32,512]{1,0:T(8,128)(2,1)S(1)}, bf16[32,512]{1,0:T(8,128)(2,1)S(1)}, u32[]{:S(2)}, u32[]{:S(2)}) %collective-permute-start.3) | collective-permute-done | bytes 32800 | tf_op jit(solution)/shard_map/ppermute | solution.py:552
  19.5 2.7 %collective-permute-start.4 = (bf16[32,512]{1,0:T(8,128)(2,1)S(1)}, bf16[32,512]{1,0:T(8,128)(2,1)S(1)}, u32[]{:S(2)}, u32[]{:S(2)}) collective-permute-start(bf16[32,512]{1,0:T(8,128)(2,1)S(1)} %get-tuple-element.39), channel_id=1, source_target_pairs={{0,8},{4,12},{8,0},{12,4},{1,9},{5,13},{9,1},{13,5},{2,10},{6,14},... | collective-permute-start | bytes 98312 | tf_op jit(solution)/shard_map/ppermute | solution.py:552
  22.2 0.5 collective-permute-start
  22.7 3.0 %collective-permute-done.others_ref = s32[8]{0:T(128)S(1)} collective-permute-done((s32[8]{0:T(128)S(1)}, s32[8]{0:T(128)S(1)}, u32[]{:S(2)}, u32[]{:S(2)}) %collective-permute-start) | collective-permute-done | bytes 64 | tf_op jit(solution)/shard_map/ppermute | solution.py:427
  25.7 0.0 collective-permute-done.4.right_ref
  25.8 0.7 shard_map.68.refs_1_
  26.4 0.1 collective-permute-start.5
  26.5 2.9 %shard_map.69.refs_4_ = bf16[512,2,8,384]{3,2,1,0:T(8,128)(2,1)S(1)} custom-call(f32[32,512]{1,0:T(8,128)S(1)} %get-tuple-element.38.left_ref.order_ref, bf16[1024,6,8,384]{3,2,1,0:T(8,128)(2,1)} %bitcast.24), custom_call_target="tpu_custom_call" | custom-call | tf_op jit(solution)/shard_map/pallas_call | solution.py:559
  29.4 0.0 collective-permute-done.5.refs_2_
  29.4 7.2 %field.3 = (bf16[16,16,384]{2,1,0:T(8,128)(2,1)S(1)}, bf16[16,16,384]{2,1,0:T(8,128)(2,1)S(1)}, bf16[256,8192]{1,0:T(8,128)(2,1)S(1)}, bf16[512,2,8,384]{3,2,1,0...) custom-call(s32[3]{0:T(128)S(1)} %pad_add_fusion.place_ref.refs_0_, ...), custom_call_target="tpu_custom_call" | custom-call | flops 3221225472 | bytes 12582912 | tf_op jit(solution)/shard_map/field/pallas_call | solution.py:309
  36.6 0.6 collective-permute-start.6
  37.2 3.5 %field.4 = (bf16[16,16,384]{2,1,0:T(8,128)(2,1)S(1)}, bf16[16,16,384]{2,1,0:T(8,128)(2,1)S(1)}, bf16[512,2,8,384]{3,2,1,0:T(8,128)(2,1)S(1)}) custom-call(bf16[256,8192]{1,0:T(8,128)(2,1)S(1)} %get-tuple-element.42.refs_0_, bf16[512,2,8,384]{3,2,1,0:T(8,128)(2,1)S(1)} %get-tuple-element.43.refs_1_, bf16[512,2,8,384]{3,2,1,0:T(8,128)(2,1)S(1)} %get-tuple-element.44.refs_2_, ...), custom_call_target="tpu_custom_call" | custom-call | flops 3221225472 | bytes 12582912 | tf_op jit(solution)/shard_map/field/pallas_call | solution.py:309
  40.7 0.0 copy-start
  40.7 3.4 %field.5 = (bf16[16,16,384]{2,1,0:T(8,128)(2,1)S(1)}, bf16[16,16,384]{2,1,0:T(8,128)(2,1)S(1)}) custom-call(bf16[256,8192]{1,0:T(8,128)(2,1)S(1)} %get-tuple-element.42.refs_0_, bf16[512,2,8,384]{3,2,1,0:T(8,128)(2,1)S(1)} %get-tuple-element.46.refs_1_, bf16[512,2,8,384]{3,2,1,0:T(8,128)(2,1)S(1)} %get-tuple-element.47.refs_2_, ...), custom_call_target="tpu_custom_call" | custom-call | flops 3221225472 | bytes 12582912 | tf_op jit(solution)/shard_map/field/pallas_call | solution.py:309
  44.1 1.6 %collective-permute-start.8 = (bf16[8,2,16,384]{3,2,1,0:T(8,128)(2,1)S(1)}, bf16[8,2,16,384]{3,2,1,0:T(8,128)(2,1)S(1)}, u32[]{:S(2)}, u32[]{:S(2)}) collective-permute-start(bf16[8,2,16,384]{3,2,1,0:T(8,128)(2,1)S(1)} %bitcast.22), channel_id=1, source_target_pairs={{0,2},{2,0},{1,3},{3,1},{4,6},{6,4},{5,7},{7,5},{8,10},{10,8},{9,1... | collective-permute-start | bytes 589832 | tf_op jit(solution)/shard_map/ppermute | solution.py:427
  45.7 0.5 collective-permute-start.7
  46.2 0.0 collective-permute-done.6.refs_3_
  46.2 5.7 %collective-permute-done.8.refs_5_ = bf16[8,2,16,384]{3,2,1,0:T(8,128)(2,1)S(1)} collective-permute-done((bf16[8,2,16,384]{3,2,1,0:T(8,128)(2,1)S(1)}, bf16[8,2,16,384]{3,2,1,0:T(8,128)(2,1)S(1)}, u32[]{:S(2)}, u32[]{:S(2)}) %collective-permute-start.8) | collective-permute-done | bytes 196640 | tf_op jit(solution)/shard_map/ppermute | solution.py:427
  52.0 3.5 %collective-permute-done.7.refs_4_ = bf16[8,2,16,384]{3,2,1,0:T(8,128)(2,1)S(1)} collective-permute-done((bf16[8,2,16,384]{3,2,1,0:T(8,128)(2,1)S(1)}, bf16[8,2,16,384]{3,2,1,0:T(8,128)(2,1)S(1)}, u32[]{:S(2)}, u32[]{:S(2)}) %collective-permute-start.7) | collective-permute-done | bytes 196640 | tf_op jit(solution)/shard_map/ppermute | solution.py:427
  55.4 1.0 combine.1
  56.4 3.8 %all-to-all-start = ((bf16[8,2,48,384]{3,2,1,0:T(8,128)(2,1)}), bf16[8,2,48,384]{3,2,1,0:T(8,128)(2,1)S(1)}, u32[]{:S(2)}, u32[]{:S(2)}) async-start(bf16[8,2,48,384]{3,2,1,0:T(8,128)(2,1)} %combine.1), calls=%async_computation | async-start | bytes 1179648 | tf_op jit(solution)/shard_map/all_to_all | solution.py:490
  60.2 1.6 %collective-permute-start.9 = (bf16[8,2,48,96]{3,2,1,0:T(8,128)(2,1)S(1)}, bf16[8,2,48,96]{3,2,1,0:T(8,128)(2,1)S(1)}, u32[]{:S(2)}, u32[]{:S(2)}) collective-permute-start(bf16[8,2,48,96]{3,2,1,0:T(8,128)(2,1)S(1)} %copy-done), channel_id=1, source_target_pairs={{0,2},{2,0},{1,3},{3,1},{4,6},{6,4},{5,7},{7,5},{8,10},{10,8},{9,1... | collective-permute-start | bytes 442376 | tf_op jit(solution)/shard_map/ppermute | solution.py:427
  61.8 5.7 %collective-permute-done.9.received_ref = bf16[8,2,48,96]{3,2,1,0:T(8,128)(2,1)S(1)} collective-permute-done((bf16[8,2,48,96]{3,2,1,0:T(8,128)(2,1)S(1)}, bf16[8,2,48,96]{3,2,1,0:T(8,128)(2,1)S(1)}, u32[]{:S(2)}, u32[]{:S(2)}) %collective-permute-start.9) | collective-permute-done | bytes 147488 | tf_op jit(solution)/shard_map/ppermute | solution.py:427
  67.5 0.7 shard_map.70
  68.2 0.1 collective-permute-start.10
  68.2 1.3 %collective-permute-done.10.received_ref = bf16[4,1,2,48,96]{4,3,2,1,0:T(8,128)(2,1)S(1)} collective-permute-done((bf16[4,1,2,48,96]{4,3,2,1,0:T(8,128)(2,1)S(1)}, bf16[4,1,2,48,96]{4,3,2,1,0:T(8,128)(2,1)S(1)}, u32[]{:S(2)}, u32[]{:S(2)}) %collective-permute-start.10) | collective-permute-done | bytes 73760 | tf_op jit(solution)/shard_map/ppermute | solution.py:427
  69.5 0.6 shard_map.71
  70.1 1.7 %collective-permute-start.11 = (bf16[2,2,2,48,96]{4,3,2,1,0:T(8,128)(2,1)S(1)}, bf16[2,2,2,48,96]{4,3,2,1,0:T(8,128)(2,1)S(1)}, u32[]{:S(2)}, u32[]{:S(2)}) collective-permute-start(bf16[2,2,2,48,96]{4,3,2,1,0:T(8,128)(2,1)S(1)} %get-tuple-element.56), channel_id=1, source_target_pairs={{0,4},{4,0},{8,12},{12,8},{1,5},{5,1},{9,13},{13,9},{2,6},{6,2},{1... | collective-permute-start | bytes 221192 | tf_op jit(solution)/shard_map/ppermute | solution.py:557
  71.8 5.3 %collective-permute-done.11.received_ref = bf16[2,2,2,48,96]{4,3,2,1,0:T(8,128)(2,1)S(1)} collective-permute-done((bf16[2,2,2,48,96]{4,3,2,1,0:T(8,128)(2,1)S(1)}, bf16[2,2,2,48,96]{4,3,2,1,0:T(8,128)(2,1)S(1)}, u32[]{:S(2)}, u32[]{:S(2)}) %collective-permute-start.11) | collective-permute-done | bytes 73760 | tf_op jit(solution)/shard_map/ppermute | solution.py:557
  77.2 0.6 shard_map.72
  77.8 1.2 %collective-permute-start.12 = (bf16[1,4,2,48,96]{4,3,2,1,0:T(8,128)(2,1)S(1)}, bf16[1,4,2,48,96]{4,3,2,1,0:T(8,128)(2,1)S(1)}, u32[]{:S(2)}, u32[]{:S(2)}) collective-permute-start(bf16[1,4,2,48,96]{4,3,2,1,0:T(8,128)(2,1)S(1)} %get-tuple-element.58), channel_id=1, source_target_pairs={{0,8},{4,12},{8,0},{12,4},{1,9},{5,13},{9,1},{13,5},{2,10},{6,14},... | collective-permute-start | bytes 221192 | tf_op jit(solution)/shard_map/ppermute | solution.py:557
  79.0 5.8 %collective-permute-done.12 = bf16[1,4,2,48,96]{4,3,2,1,0:T(8,128)(2,1)S(1)} collective-permute-done((bf16[1,4,2,48,96]{4,3,2,1,0:T(8,128)(2,1)S(1)}, bf16[1,4,2,48,96]{4,3,2,1,0:T(8,128)(2,1)S(1)}, u32[]{:S(2)}, u32[]{:S(2)}) %collective-permute-start.12) | collective-permute-done | bytes 73760 | tf_op jit(solution)/shard_map/ppermute | solution.py:557
  84.8 0.0 all-to-all-done.field_ref
  84.8 3.6 %shard_map.73 = bf16[8,2,48,96]{3,2,1,0:T(8,128)(2,1)S(1)} custom-call(s32[1]{0:T(128)} %bitcast.rank_ref, bf16[8,2,48,384]{3,2,1,0:T(8,128)(2,1)S(1)} %all-to-all-done.field_ref, bf16[4,2,48,96]{3,2,1,0:T(8,128)(2,1)S(1)} %bitcast.18, bf16[4,2,48,96]{3,2,1,0:T(8,128)(2,1)S(1)} %bitcast.19), custom_call_target="tpu_custom_call" | custom-call | tf_op jit(solution)/shard_map/pallas_call | solution.py:416
  88.4 12.1 %all_to_all.10.grid_ref = bf16[8,2,48,96]{3,2,1,0:T(8,128)(2,1)S(1)} all-to-all(bf16[8,2,48,96]{3,2,1,0:T(8,128)(2,1)S(1)} %shard_map.73), channel_id=1, replica_groups=mesh['groups'=2,'chol'=4,'walk'=2,'orb'=2] {'chol','orb'}, dimensions={0} | all-to-all | bytes 294912 | tf_op jit(solution)/shard_map/all_to_all | solution.py:625
  100.5 1.0 shard_map.74
  (5 shorter events, 0.0 us)
Async XLA Ops:
  2.2 8.8 %collective-permute-start.1 = (bf16[16,4608]{1,0:T(8,128)(2,1)S(1)}, bf16[16,4608]{1,0:T(8,128)(2,1)S(1)}, u32[]{:S(2)}, u32[]{:S(2)}) collective-permute-start(bf16[16,4608]{1,0:T(8,128)(2,1)S(1)} %reshape.28.own_ref), channel_id=1, source_target_pairs={{0,2},{2,0},{1,3},{3,1},{4,6},{6,4},{5,7},{7,5},{8,10},{10,8},{9,1... | collective-permute-start | bytes 442376 | tf_op jit(solution)/shard_map/ppermute | solution.py:427
  11.0 11.2 %copy-start.2 = (s32[8]{0:T(128)S(1)}, s32[8]{0:T(128)}, u32[]{:S(2)}) copy-start(s32[8]{0:T(128)} %source_ref.3) | copy-start | bytes 100
  11.0 14.8 %copy-start.1 = (f32[16,1024]{1,0:T(8,128)S(1)}, f32[16,1024]{1,0:T(8,128)}, u32[]{:S(2)}) copy-start(f32[16,1024]{1,0:T(8,128)} %samples_ref.1) | copy-start | bytes 196612
  14.2 1.3 %collective-permute-start.2 = (f32[32,512]{1,0:T(8,128)S(1)}, f32[32,512]{1,0:T(8,128)S(1)}, u32[]{:S(2)}, u32[]{:S(2)}) collective-permute-start(f32[32,512]{1,0:T(8,128)S(1)} %get-tuple-element.35), channel_id=1, source_target_pairs={{0,1},{1,0},{2,3},{3,2},{4,5},{5,4},{6,7},{7,6},{8,9},{9,8},{10,11... | collective-permute-start | bytes 196616 | tf_op jit(solution)/shard_map/ppermute | solution.py:427
  15.5 4.0 %collective-permute-start.3 = (bf16[32,512]{1,0:T(8,128)(2,1)S(1)}, bf16[32,512]{1,0:T(8,128)(2,1)S(1)}, u32[]{:S(2)}, u32[]{:S(2)}) collective-permute-start(bf16[32,512]{1,0:T(8,128)(2,1)S(1)} %get-tuple-element.37), channel_id=1, source_target_pairs={{0,4},{4,0},{8,12},{12,8},{1,5},{5,1},{9,13},{13,9},{2,6},{6,2},{1... | collective-permute-start | bytes 98312 | tf_op jit(solution)/shard_map/ppermute | solution.py:552
  19.5 6.2 %collective-permute-start.4 = (bf16[32,512]{1,0:T(8,128)(2,1)S(1)}, bf16[32,512]{1,0:T(8,128)(2,1)S(1)}, u32[]{:S(2)}, u32[]{:S(2)}) collective-permute-start(bf16[32,512]{1,0:T(8,128)(2,1)S(1)} %get-tuple-element.39), channel_id=1, source_target_pairs={{0,8},{4,12},{8,0},{12,4},{1,9},{5,13},{9,1},{13,5},{2,10},{6,14},... | collective-permute-start | bytes 98312 | tf_op jit(solution)/shard_map/ppermute | solution.py:552
  22.2 3.6 %collective-permute-start = (s32[8]{0:T(128)S(1)}, s32[8]{0:T(128)S(1)}, u32[]{:S(2)}, u32[]{:S(2)}) collective-permute-start(s32[8]{0:T(128)S(1)} %copy-done.2), channel_id=1, source_target_pairs={{0,2},{2,0},{1,3},{3,1},{4,6},{6,4},{5,7},{7,5},{8,10},{10,8},{9,1... | collective-permute-start | bytes 104 | tf_op jit(solution)/shard_map/ppermute | solution.py:427
  26.4 3.0 %collective-permute-start.5 = (bf16[32,512]{1,0:T(8,128)(2,1)S(1)}, bf16[32,512]{1,0:T(8,128)(2,1)S(1)}, u32[]{:S(2)}, u32[]{:S(2)}) collective-permute-start(bf16[32,512]{1,0:T(8,128)(2,1)S(1)} %shard_map.68.refs_1_), channel_id=1, source_target_pairs={{0,1},{1,0},{2,3},{3,2},{4,5},{5,4},{6,7},{7,6},{8,9},{9,8},{10,11... | collective-permute-start | bytes 98312 | tf_op jit(solution)/shard_map/ppermute | solution.py:427
  36.6 9.6 %collective-permute-start.6 = (bf16[8,2,16,384]{3,2,1,0:T(8,128)(2,1)S(1)}, bf16[8,2,16,384]{3,2,1,0:T(8,128)(2,1)S(1)}, u32[]{:S(2)}, u32[]{:S(2)}) collective-permute-start(bf16[8,2,16,384]{3,2,1,0:T(8,128)(2,1)S(1)} %bitcast.20), channel_id=1, source_target_pairs={{0,2},{2,0},{1,3},{3,1},{4,6},{6,4},{5,7},{7,5},{8,10},{10,8},{9,1... | collective-permute-start | bytes 589832 | tf_op jit(solution)/shard_map/ppermute | solution.py:427
  40.7 19.5 %copy-start = (bf16[8,2,48,96]{3,2,1,0:T(8,128)(2,1)S(1)}, bf16[8,2,48,96]{3,2,1,0:T(8,128)(2,1)}, u32[]{:S(2)}) copy-start(bf16[8,2,48,96]{3,2,1,0:T(8,128)(2,1)} %get-tuple-element.52.own_ref) | copy-start | bytes 442372
  44.1 7.8 %collective-permute-start.8 = (bf16[8,2,16,384]{3,2,1,0:T(8,128)(2,1)S(1)}, bf16[8,2,16,384]{3,2,1,0:T(8,128)(2,1)S(1)}, u32[]{:S(2)}, u32[]{:S(2)}) collective-permute-start(bf16[8,2,16,384]{3,2,1,0:T(8,128)(2,1)S(1)} %bitcast.22), channel_id=1, source_target_pairs={{0,2},{2,0},{1,3},{3,1},{4,6},{6,4},{5,7},{7,5},{8,10},{10,8},{9,1... | collective-permute-start | bytes 589832 | tf_op jit(solution)/shard_map/ppermute | solution.py:427
  45.7 9.7 %collective-permute-start.7 = (bf16[8,2,16,384]{3,2,1,0:T(8,128)(2,1)S(1)}, bf16[8,2,16,384]{3,2,1,0:T(8,128)(2,1)S(1)}, u32[]{:S(2)}, u32[]{:S(2)}) collective-permute-start(bf16[8,2,16,384]{3,2,1,0:T(8,128)(2,1)S(1)} %bitcast.21), channel_id=1, source_target_pairs={{0,2},{2,0},{1,3},{3,1},{4,6},{6,4},{5,7},{7,5},{8,10},{10,8},{9,1... | collective-permute-start | bytes 589832 | tf_op jit(solution)/shard_map/ppermute | solution.py:427
  56.4 28.4 %all-to-all-start = ((bf16[8,2,48,384]{3,2,1,0:T(8,128)(2,1)}), bf16[8,2,48,384]{3,2,1,0:T(8,128)(2,1)S(1)}, u32[]{:S(2)}, u32[]{:S(2)}) async-start(bf16[8,2,48,384]{3,2,1,0:T(8,128)(2,1)} %combine.1), calls=%async_computation | async-start | bytes 1179648 | tf_op jit(solution)/shard_map/all_to_all | solution.py:490
  60.2 7.3 %collective-permute-start.9 = (bf16[8,2,48,96]{3,2,1,0:T(8,128)(2,1)S(1)}, bf16[8,2,48,96]{3,2,1,0:T(8,128)(2,1)S(1)}, u32[]{:S(2)}, u32[]{:S(2)}) collective-permute-start(bf16[8,2,48,96]{3,2,1,0:T(8,128)(2,1)S(1)} %copy-done), channel_id=1, source_target_pairs={{0,2},{2,0},{1,3},{3,1},{4,6},{6,4},{5,7},{7,5},{8,10},{10,8},{9,1... | collective-permute-start | bytes 442376 | tf_op jit(solution)/shard_map/ppermute | solution.py:427
  68.2 1.4 %collective-permute-start.10 = (bf16[4,1,2,48,96]{4,3,2,1,0:T(8,128)(2,1)S(1)}, bf16[4,1,2,48,96]{4,3,2,1,0:T(8,128)(2,1)S(1)}, u32[]{:S(2)}, u32[]{:S(2)}) collective-permute-start(bf16[4,1,2,48,96]{4,3,2,1,0:T(8,128)(2,1)S(1)} %get-tuple-element.54), channel_id=1, source_target_pairs={{0,1},{1,0},{2,3},{3,2},{4,5},{5,4},{6,7},{7,6},{8,9},{9,8},{10,11... | collective-permute-start | bytes 221192 | tf_op jit(solution)/shard_map/ppermute | solution.py:427
  70.1 7.0 %collective-permute-start.11 = (bf16[2,2,2,48,96]{4,3,2,1,0:T(8,128)(2,1)S(1)}, bf16[2,2,2,48,96]{4,3,2,1,0:T(8,128)(2,1)S(1)}, u32[]{:S(2)}, u32[]{:S(2)}) collective-permute-start(bf16[2,2,2,48,96]{4,3,2,1,0:T(8,128)(2,1)S(1)} %get-tuple-element.56), channel_id=1, source_target_pairs={{0,4},{4,0},{8,12},{12,8},{1,5},{5,1},{9,13},{13,9},{2,6},{6,2},{1... | collective-permute-start | bytes 221192 | tf_op jit(solution)/shard_map/ppermute | solution.py:557
  77.8 7.0 %collective-permute-start.12 = (bf16[1,4,2,48,96]{4,3,2,1,0:T(8,128)(2,1)S(1)}, bf16[1,4,2,48,96]{4,3,2,1,0:T(8,128)(2,1)S(1)}, u32[]{:S(2)}, u32[]{:S(2)}) collective-permute-start(bf16[1,4,2,48,96]{4,3,2,1,0:T(8,128)(2,1)S(1)} %get-tuple-element.58), channel_id=1, source_target_pairs={{0,8},{4,12},{8,0},{12,4},{1,9},{5,13},{9,1},{13,5},{2,10},{6,14},... | collective-permute-start | bytes 221192 | tf_op jit(solution)/shard_map/ppermute | solution.py:557
